TPU v7x, 256 devices: a whole 4x4x8 slice. The times are simulated.
256 devices in a mesh: dp: 32 (over y_hi, z, core), shard: 8 (over x, y_lo).
Axes of the slice: x: 4, y: 4 (y_hi: 2, y_lo: 2; y = y_hi * 2 + y_lo), z: 8, core: 2. Of those that a mesh axis runs over, the one named last changes fastest.
Arguments:
- resid_in: bfloat16 [4096, 8192], P('dp', 'shard'), may hold values from -6 to 6
- hidden: bfloat16 [4096, 28672], P('shard', 'dp'), may hold values from -6 to 6
- w_down: bfloat16 [28672, 8192], P('dp', 'shard'), may hold values from -0.03125 to 0.03125
- frozen: bfloat16 [4096, 8192], P(('dp', 'shard')), may hold values from -6 to 6
- steer: bfloat16 [8192], P('shard'), may hold values from -6 to 6
- forget_flags: int32 [16], replicated, may hold values from 0 to 1, as said below
Outputs:
- updated: bfloat16 [4096, 8192], P('dp', 'shard')
- grad_down: float32 [28672, 8192], P('dp', 'shard')
Inputs may be any that keep to these rules, and one draw needn't show every extreme that they name: `forget_flags`: exactly half of the 16 sequences are forget sequences.
All inputs are finite; a program needn't handle non-finite values.
Results may differ from a plain program's by a relative error of at most 0.0019.
Values may be sent and summed in bfloat16 or wider, within the bound.
A program may use at most 128 MiB of HBM per device.

v0:
```python
import math

import jax
import jax.numpy as jnp
from jax import lax
from jax.sharding import PartitionSpec as P

SEQ_LEN = 256


retain_weight = 2.0


def per_device(resid_in, hidden, w_down, frozen, steer, forget_flags):
    whole_hidden = lax.all_gather(hidden, "shard", axis=0, tiled=True)
    tok_rows = resid_in.shape[0]
    mlp_out = lax.psum_scatter(
        jnp.dot(whole_hidden, w_down, preferred_element_type=jnp.float32),
        "dp",
        scatter_dimension=0,
        tiled=True,
    )
    residual = resid_in.astype(jnp.float32) + mlp_out
    updated = residual.astype(jnp.bfloat16)
    target_rows = lax.all_to_all(frozen, "shard", split_axis=1, concat_axis=0, tiled=True)
    start_row = lax.axis_index("dp") * tok_rows
    seq_ids = (start_row + jnp.arange(tok_rows, dtype=jnp.int32)) // SEQ_LEN
    seq_match = seq_ids[:, None] == jnp.arange(forget_flags.shape[0], dtype=jnp.int32)[None, :]
    is_forget = jnp.sum(jnp.where(seq_match, forget_flags[None, :], 0), axis=1) > 0
    total_tokens = tok_rows * lax.axis_size("dp")
    target = jnp.where(
        is_forget[:, None], steer.astype(jnp.float32)[None, :], target_rows.astype(jnp.float32)
    )
    loss_weight = jnp.where(is_forget, 1.0, retain_weight).astype(jnp.float32)
    slopes = (loss_weight[:, None] * (residual - target) * (1.0 / math.sqrt(total_tokens))).astype(
        jnp.bfloat16
    )
    all_slopes = lax.all_gather(slopes, "dp", axis=0, tiled=True)
    grad_down = lax.dot_general(
        whole_hidden, all_slopes, (((0,), (0,)), ((), ())), preferred_element_type=jnp.float32
    )
    return (updated, grad_down)


def solution(mesh):
    in_specs = (
        P("dp", "shard"),
        P("shard", "dp"),
        P("dp", "shard"),
        P(("dp", "shard"), None),
        P("shard"),
        P(),
    )
    out_specs = (P("dp", "shard"), P("dp", "shard"))
    return jax.shard_map(
        per_device, mesh=mesh, in_specs=in_specs, out_specs=out_specs, check_vma=False
    )
```

profile of v0, /device:TPU:29, one launch (start us, length us, event | category | flops | bytes accessed | tf_op | source)
XLA Modules:
  0.0 528.9 jit_solution(17514021398669694060)
XLA Ops:
  7.2 0.0 copy-start
  7.2 0.0 all-gather.3.cloned.1.call-start
  7.2 0.7 all-gather.3.cloned.1.call-update
  7.9 0.0 reduce-scatter.2.cloned.1.call-start
  8.0 155.2 %all-gather.3.cloned.1.call-done = bf16[4096,896]{1,0:T(8,128)(2,1)} async-done(((bf16[512,896]{1,0:T(8,128)(2,1)}), bf16[4096,896]{1,0:T(8,128)(2,1)}) %all-gather.3.cloned.1.call-update) | async-done | bytes 7340048 | tf_op jit(solution)/shard_map/all_gather | solution.py:15
  163.1 0.0 copy-done
  163.1 14.3 %fusion.5 = f32[4096,1024]{1,0:T(8,128)} fusion(bf16[4096,896]{1,0:T(8,128)(2,1)} %all-gather.3.cloned.1.call-done, bf16[896,1024]{1,0:T(8,128)(2,1)S(1)} %copy-done), kind=kOutput, calls=%fused_computation.17 | convolution fusion | flops 7516192768 | bytes 25952256 | tf_op jit(solution)/shard_map/dot_general | solution.py:18
  177.5 0.0 copy-start.1
  177.5 0.0 copy-start.4
  177.5 0.0 copy-start.3
  177.5 0.0 copy-start.2
  177.5 0.0 reduce-scatter.2.cloned.1.call-update
  177.5 0.9 copy-done.1
  178.4 0.7 copy.14
  179.1 6.1 %all-to-all-start = ((bf16[16,8,1024]{2,0,1:T(8,128)(2,1)}), bf16[16,8,1024]{2,0,1:T(8,128)(2,1)S(1)}, u32[]{:S(2)}, u32[]{:S(2)}) async-start(bf16[16,8,1024]{2,0,1:T(8,128)(2,1)} %bitcast.21), calls=%async_computation.1 | async-start | bytes 524288 | tf_op jit(solution)/shard_map/all_to_all | solution.py:25
  185.2 0.0 all-gather.5.cloned.1.call-start
  185.2 0.0 copy-done.4
  185.2 0.1 select_reduce_fusion
  185.3 0.0 copy-done.3
  185.3 3.0 all-to-all-done
  188.3 206.4 %reduce-scatter.2.cloned.1.call-done = f32[128,1024]{1,0:T(8,128)} async-done(((f32[4096,1024]{1,0:T(8,128)}), f32[128,1024]{1,0:T(8,128)}) %reduce-scatter.2.cloned.1.call-update) | async-done | bytes 524304 | tf_op jit(solution)/shard_map/reduce_scatter | solution.py:17
  394.8 0.0 copy-done.2
  394.8 2.0 fusion.3
  396.8 0.0 all-gather.5.cloned.1.call-update
  396.8 106.0 %all-gather.5.cloned.1.call-done = bf16[4096,1024]{1,0:T(8,128)(2,1)} async-done(((bf16[128,1024]{1,0:T(8,128)(2,1)}), bf16[4096,1024]{1,0:T(8,128)(2,1)}) %all-gather.5.cloned.1.call-update) | async-done | bytes 8388624 | tf_op jit(solution)/shard_map/all_gather | solution.py:38
  502.8 14.6 %convolution_bitcast_fusion = f32[896,1024]{0,1:T(8,128)} fusion(bf16[4096,1024]{1,0:T(8,128)(2,1)} %all-gather.5.cloned.1.call-done, bf16[4096,896]{1,0:T(8,128)(2,1)} %all-gather.3.cloned.1.call-done), kind=kOutput, calls=%fused_computation | convolution fusion | flops 7516192768 | bytes 19398656 | tf_op jit(solution)/shard_map/dot_general | solution.py:39
  517.4 5.0 copy.11
  (4 shorter events, 0.0 us)
Async XLA Ops:
  7.2 155.9 %copy-start = (bf16[896,1024]{1,0:T(8,128)(2,1)S(1)}, bf16[896,1024]{1,0:T(8,128)(2,1)}, u32[]{:S(2)}) copy-start(bf16[896,1024]{1,0:T(8,128)(2,1)} %param.8) | copy-start | bytes 5505028
  7.2 155.9 %all-gather.3.cloned.1.call-start = ((), (), s32[]{:S(2)}) async-start(), calls=%async_computation.2 | async-start | bytes 8257536 | tf_op jit(solution)/shard_map/all_gather | solution.py:15
  7.9 386.9 %reduce-scatter.2.cloned.1.call-start = ((), (), s32[]{:S(2)}) async-start(), calls=%async_computation.3 | async-start | bytes 17301504 | tf_op jit(solution)/shard_map/reduce_scatter | solution.py:17
  177.5 0.9 copy-start.1
  177.5 7.8 %copy-start.4 = (s32[16]{0:T(128)S(1)}, s32[16]{0:T(128)}, u32[]{:S(2)}) copy-start(s32[16]{0:T(128)} %param.11) | copy-start | bytes 196
  177.5 7.9 %copy-start.3 = (bf16[1024]{0:T(1024)(128)(2,1)S(1)}, bf16[1024]{0:T(1024)(128)(2,1)}, u32[]{:S(2)}) copy-start(bf16[1024]{0:T(1024)(128)(2,1)} %param.10) | copy-start | bytes 6148
  177.5 217.3 %copy-start.2 = (bf16[128,1024]{1,0:T(8,128)(2,1)S(1)}, bf16[128,1024]{1,0:T(8,128)(2,1)}, u32[]{:S(2)}) copy-start(bf16[128,1024]{1,0:T(8,128)(2,1)} %param.6) | copy-start | bytes 786436
  179.1 9.2 %all-to-all-start = ((bf16[16,8,1024]{2,0,1:T(8,128)(2,1)}), bf16[16,8,1024]{2,0,1:T(8,128)(2,1)S(1)}, u32[]{:S(2)}, u32[]{:S(2)}) async-start(bf16[16,8,1024]{2,0,1:T(8,128)(2,1)} %bitcast.21), calls=%async_computation.1 | async-start | bytes 524288 | tf_op jit(solution)/shard_map/all_to_all | solution.py:25
  185.2 317.6 %all-gather.5.cloned.1.call-start = ((), (), s32[]{:S(2)}) async-start(), calls=%async_computation.4 | async-start | bytes 8650752 | tf_op jit(solution)/shard_map/all_gather | solution.py:38
Sparse Core Ops, SparseCore 0:
  9.8 153.2 all-gather.2
  177.6 217.1 reduce-scatter.1
  398.5 104.2 all-gather.4
where the time goes:
time: 532 us; the launch traced here: 529 us
  waiting for transfers between devices  471 us (89%)
  matrix products  29 us (5%)
  between operations  13.8 us (3%)
  local copies, waits for them, and re-layouts  6.64 us (1%)
  starting transfers between devices  6.15 us (1%)
    reduce_scatter x1, waiting for transfers between devices, per_device(): lax.psum_scatter(jnp.dot(whole_hidden, w_down, preferred_element_type=jnp...  206 us
    all_gather x1, waiting for transfers between devices, per_device(): whole_hidden = lax.all_gather(hidden, 'shard', axis=0, tiled=True)  155 us
    all_gather x1, waiting for transfers between devices, per_device(): all_slopes = lax.all_gather(slopes, 'dp', axis=0, tiled=True)  106 us
    dot_general x1, matrix products, per_device(): lax.dot_general(whole_hidden, all_slopes, (((0,), (0,)), ((), ())), prefe...  14.6 us
    dot_general x1, matrix products, per_device(): jnp.dot(whole_hidden, w_down, preferred_element_type=jnp.float32)  14.3 us
  transfers between devices with their start and end apart: 4, of which 4 were waited for; matrix products, arithmetic and copies ran while one was open for 0% of the time, Pallas kernels for 0%

commit v1 on v0

v1 whole, which is shorter than its diff:
```python
import math

import jax
import jax.numpy as jnp
from jax import lax
from jax.sharding import Mesh, PartitionSpec as P

SEQ_LEN = 256


retain_weight = 2.0


def per_device(resid_in, hidden, w_down, frozen, steer, forget_flags):
    n_c = lax.axis_size("c")
    tok_rows, d_cols = resid_in.shape
    ff_rows = w_down.shape[0]
    whole_hidden = lax.all_gather(hidden, "shard", axis=0, tiled=True)
    total_tokens = whole_hidden.shape[0]
    wh = whole_hidden.reshape(n_c, 2, tok_rows, ff_rows)
    swapped = lax.all_to_all(wh, "core", split_axis=1, concat_axis=1, tiled=True)
    mine = jnp.transpose(swapped, (0, 2, 1, 3)).reshape(n_c * tok_rows, 2 * ff_rows)
    pair_w = lax.all_gather(w_down, "core", axis=0, tiled=True)
    partial = jnp.dot(mine, pair_w, preferred_element_type=jnp.float32)
    mlp_out = lax.psum_scatter(partial, "c", scatter_dimension=0, tiled=True)
    residual = resid_in.astype(jnp.float32) + mlp_out
    updated = residual.astype(jnp.bfloat16)
    target_rows = lax.all_to_all(frozen, "shard", split_axis=1, concat_axis=0, tiled=True)
    row_block = lax.axis_index("c") * 2 + lax.axis_index("core")
    start_row = row_block * tok_rows
    seq_ids = (start_row + jnp.arange(tok_rows, dtype=jnp.int32)) // SEQ_LEN
    seq_match = seq_ids[:, None] == jnp.arange(forget_flags.shape[0], dtype=jnp.int32)[None, :]
    is_forget = jnp.sum(jnp.where(seq_match, forget_flags[None, :], 0), axis=1) > 0
    target = jnp.where(
        is_forget[:, None], steer.astype(jnp.float32)[None, :], target_rows.astype(jnp.float32)
    )
    loss_weight = jnp.where(is_forget, 1.0, retain_weight).astype(jnp.float32)
    slopes = (loss_weight[:, None] * (residual - target) * (1.0 / math.sqrt(total_tokens))).astype(
        jnp.bfloat16
    )
    half_slopes = lax.all_gather(slopes, "c", axis=0, tiled=False)
    all_slopes = lax.all_gather(half_slopes, "core", axis=0, tiled=False)
    grad_down = jnp.einsum(
        "mptf,pmtd->fd", wh, all_slopes, preferred_element_type=jnp.float32
    )
    return (updated, grad_down)


def solution(mesh):
    n_dp, n_shard = mesh.devices.shape
    pair_mesh = Mesh(mesh.devices.reshape(n_dp // 2, 2, n_shard), ("c", "core", "shard"))
    dp = ("c", "core")
    in_specs = (
        P(dp, "shard"),
        P("shard", dp),
        P(dp, "shard"),
        P(("c", "core", "shard"), None),
        P("shard"),
        P(),
    )
    out_specs = (P(dp, "shard"), P(dp, "shard"))
    return jax.shard_map(
        per_device, mesh=pair_mesh, in_specs=in_specs, out_specs=out_specs, check_vma=False
    )
```

time: 532 us -> 583 us (1.096)
  waiting for transfers between devices: 471 us -> 496 us
  local copies, waits for them, and re-layouts: 6.64 us -> 23.1 us
  blocking collectives: 0 us -> 11.3 us
    all_gather x1 -> x3, waiting for transfers between devices: 106 us -> 129 us  [the longest x1 100 us: per_device(): half_slopes = lax.all_gather(slopes, 'c', axis=0, tiled=False)]
    transpose x0 -> x1, local copies, waits for them, and re-layouts: none -> 12.5 us  [per_device(): jnp.transpose(swapped, (0, 2, 1, 3)).reshape(n_c * tok_rows, 2 * ff_rows)]
    all_to_all x0 -> x1, blocking collectives: none -> 11.3 us  [per_device(): lax.all_to_all(wh, 'core', split_axis=1, concat_axis=1, tiled=True)]
  transfers between devices with their start and end apart: 4 -> 6, of which waited for: 4 -> 5; matrix products, arithmetic and copies ran while one was open for 0% -> 3% of each run, Pallas kernels for 0% -> 0%
where the time goes in v1:
time: 583 us; the launch traced here: 581 us
  waiting for transfers between devices  496 us (85%)
  matrix products  27.9 us (5%)
  local copies, waits for them, and re-layouts  23.1 us (4%)
  between operations  13.8 us (2%)
  blocking collectives  11.3 us (2%)
  starting transfers between devices  6.19 us (1%)
    reduce_scatter x1, waiting for transfers between devices, per_device(): mlp_out = lax.psum_scatter(partial, 'c', scatter_dimension=0, tiled=True)  207 us
    all_gather x1, waiting for transfers between devices, per_device(): whole_hidden = lax.all_gather(hidden, 'shard', axis=0, tiled=True)  154 us
    all_gather x1, waiting for transfers between devices, per_device(): half_slopes = lax.all_gather(slopes, 'c', axis=0, tiled=False)  100 us
    all_gather x1, waiting for transfers between devices, per_device(): all_slopes = lax.all_gather(half_slopes, 'core', axis=0, tiled=False)  28.6 us
    dot_general x1, matrix products, per_device(): jnp.einsum('mptf,pmtd->fd', wh, all_slopes, preferred_element_type=jnp.fl...  14.6 us
    dot_general x1, matrix products, per_device(): partial = jnp.dot(mine, pair_w, preferred_element_type=jnp.float32)  13.2 us
    transpose x1, local copies, waits for them, and re-layouts, per_device(): jnp.transpose(swapped, (0, 2, 1, 3)).reshape(n_c * tok_rows, 2 * ff_rows)  12.5 us
  transfers between devices with their start and end apart: 6, of which 5 were waited for; matrix products, arithmetic and copies ran while one was open for 3% of the time, Pallas kernels for 0%

profile of v1, /device:TPU:29, one launch (start us, length us, event | category | flops | bytes accessed | tf_op | source)
XLA Modules:
  0.0 580.8 jit_solution(232954384777330829)
XLA Ops:
  7.2 0.0 all-gather.7.cloned.1.call-start
  7.2 0.7 all-gather.7.cloned.1.call-update
  7.9 0.0 all-gather.9.cloned.1.call-start
  7.9 0.7 all-gather.9.cloned.1.call-update
  8.6 0.0 reduce-scatter.2.cloned.1.call-start
  8.7 154.4 %all-gather.7.cloned.1.call-done = bf16[4096,896]{1,0:T(8,128)(2,1)} async-done(((bf16[512,896]{1,0:T(8,128)(2,1)}), bf16[4096,896]{1,0:T(8,128)(2,1)}) %all-gather.7.cloned.1.call-update) | async-done | bytes 7340048 | tf_op jit(solution)/shard_map/all_gather | solution.py:18
  163.1 4.0 copy.19
  167.1 11.3 %all_to_all.18 = bf16[16,2,128,896]{3,2,0,1:T(8,128)(2,1)} all-to-all(bf16[16,2,128,896]{3,2,0,1:T(8,128)(2,1)S(1)} %copy.19), channel_id=1, replica_groups=mesh['c'=16,'core'=2,'shard'=8] {'core'}, dimensions={1} | all-to-all | bytes 14680064 | tf_op jit(solution)/shard_map/all_to_all | solution.py:21
  178.4 12.5 %copy.20 = bf16[16,128,2,896]{1,0,3,2:T(8,128)(2,1)} copy(bf16[16,128,2,896]{3,1,0,2:T(8,128)(2,1)} %bitcast.35) | data formatting | bytes 14680064 | tf_op jit(solution)/shard_map/transpose | solution.py:22
  190.9 0.0 all-gather.9.cloned.1.call-done
  190.9 13.2 %fusion.2 = f32[2048,1024]{1,0:T(8,128)} fusion(bf16[1792,1024]{1,0:T(8,128)(2,1)} %all-gather.9.cloned.1.call-done, bf16[224,8,16,128]{3,2,1,0:T(8,128)(2,1)} %bitcast.38), kind=kOutput, calls=%fused_computation.2 | convolution fusion | flops 7516192768 | bytes 19398656 | tf_op jit(solution)/shard_map/dot_general | solution.py:24
  204.1 0.0 copy-start
  204.1 0.0 copy-start.3
  204.1 0.0 copy-start.2
  204.1 0.0 copy-start.1
  204.1 0.0 reduce-scatter.2.cloned.1.call-update
  204.1 0.9 copy-done
  205.0 0.7 copy.38
  205.8 6.0 %all-to-all-start.1 = ((bf16[16,8,1024]{2,0,1:T(8,128)(2,1)}), bf16[16,8,1024]{2,0,1:T(8,128)(2,1)S(1)}, u32[]{:S(2)}, u32[]{:S(2)}) async-start(bf16[16,8,1024]{2,0,1:T(8,128)(2,1)} %bitcast.34), calls=%async_computation.2 | async-start | bytes 524288 | tf_op jit(solution)/shard_map/all_to_all | solution.py:28
  211.8 0.0 all-gather.11.cloned.1.call-start
  211.8 0.0 copy-done.3
  211.8 0.1 select_reduce_fusion
  211.9 0.0 copy-done.2
  211.9 4.2 all-to-all-done.1
  216.2 207.4 %reduce-scatter.2.cloned.1.call-done = f32[128,1024]{1,0:T(8,128)} async-done(((f32[2048,1024]{1,0:T(8,128)}), f32[128,1024]{1,0:T(8,128)}) %reduce-scatter.2.cloned.1.call-update) | async-done | bytes 524304 | tf_op jit(solution)/shard_map/reduce_scatter | solution.py:25
  423.6 0.0 copy-done.1
  423.6 2.0 fusion.11
  425.6 0.0 all-gather.11.cloned.1.call-update
  425.6 0.0 all-gather.13.cloned.1.call-start
  425.6 100.3 %all-gather.11.cloned.1.call-done = bf16[2048,1024]{1,0:T(8,128)(2,1)} async-done(((bf16[128,1024]{1,0:T(8,128)(2,1)}), bf16[2048,1024]{1,0:T(8,128)(2,1)}) %all-gather.11.cloned.1.call-update) | async-done | bytes 4194320 | tf_op jit(solution)/shard_map/all_gather | solution.py:41
  526.0 0.0 all-gather.13.cloned.1.call-update
  526.0 28.6 %all-gather.13.cloned.1.call-done = bf16[32,128,1024]{2,1,0:T(8,128)(2,1)} async-done(((bf16[16,128,1024]{2,1,0:T(8,128)(2,1)}), bf16[32,128,1024]{2,1,0:T(8,128)(2,1)}) %all-gather.13.cloned.1.call-update) | async-done | bytes 8388624 | tf_op jit(solution)/shard_map/all_gather | solution.py:42
  554.6 14.6 %fusion.5 = f32[896,1024]{0,1:T(8,128)} fusion(bf16[16,2,128,896]{3,2,1,0:T(8,128)(2,1)} %bitcast.37, bf16[2,16,128,1024]{3,2,1,0:T(8,128)(2,1)} %bitcast.41), kind=kOutput, calls=%fused_computation.5 | convolution fusion | flops 7516192768 | bytes 19398656 | tf_op jit(solution)/shard_map/mptf,pmtd->fd/dot_general | solution.py:43
  569.3 5.0 copy.23
  (4 shorter events, 0.0 us)
Async XLA Ops:
  7.2 155.9 %all-gather.7.cloned.1.call-start = ((), (), s32[]{:S(2)}) async-start(), calls=%async_computation.3 | async-start | bytes 8257536 | tf_op jit(solution)/shard_map/all_gather | solution.py:18
  7.9 183.0 %all-gather.9.cloned.1.call-start = ((), (), s32[]{:S(2)}) async-start(), calls=%async_computation.4 | async-start | bytes 5505024 | tf_op jit(solution)/shard_map/all_gather | solution.py:23
  8.6 414.9 %reduce-scatter.2.cloned.1.call-start = ((), (), s32[]{:S(2)}) async-start(), calls=%async_computation.5 | async-start | bytes 8912896 | tf_op jit(solution)/shard_map/reduce_scatter | solution.py:25
  204.1 0.9 copy-start
  204.1 7.7 %copy-start.3 = (s32[16]{0:T(128)S(1)}, s32[16]{0:T(128)}, u32[]{:S(2)}) copy-start(s32[16]{0:T(128)} %param.11) | copy-start | bytes 196
  204.1 7.8 %copy-start.2 = (bf16[1024]{0:T(1024)(128)(2,1)S(1)}, bf16[1024]{0:T(1024)(128)(2,1)}, u32[]{:S(2)}) copy-start(bf16[1024]{0:T(1024)(128)(2,1)} %param.10) | copy-start | bytes 6148
  204.1 219.4 %copy-start.1 = (bf16[128,1024]{1,0:T(8,128)(2,1)S(1)}, bf16[128,1024]{1,0:T(8,128)(2,1)}, u32[]{:S(2)}) copy-start(bf16[128,1024]{1,0:T(8,128)(2,1)} %param.6) | copy-start | bytes 786436
  205.8 10.4 %all-to-all-start.1 = ((bf16[16,8,1024]{2,0,1:T(8,128)(2,1)}), bf16[16,8,1024]{2,0,1:T(8,128)(2,1)S(1)}, u32[]{:S(2)}, u32[]{:S(2)}) async-start(bf16[16,8,1024]{2,0,1:T(8,128)(2,1)} %bitcast.34), calls=%async_computation.2 | async-start | bytes 524288 | tf_op jit(solution)/shard_map/all_to_all | solution.py:28
  211.8 314.2 %all-gather.11.cloned.1.call-start = ((), (), s32[]{:S(2)}) async-start(), calls=%async_computation.6 | async-start | bytes 4456448 | tf_op jit(solution)/shard_map/all_gather | solution.py:41
  425.6 129.1 %all-gather.13.cloned.1.call-start = ((), (), s32[]{:S(2)}) async-start(), calls=%async_computation.7 | async-start | bytes 12582912 | tf_op jit(solution)/shard_map/all_gather | solution.py:42
Sparse Core Ops, SparseCore 0:
  9.8 153.2 all-gather.6
  164.9 21.3 all-gather.8
  204.3 219.2 reduce-scatter.1
  426.6 99.3 all-gather.10
  527.6 26.9 all-gather.12

commit v2 on v0

--- a/solution.py
+++ b/solution.py
@@ -11,15 +11,19 @@
 retain_weight = 2.0
 
 
+def gather_by_all_to_all(x, axis_name):
+    n = lax.axis_size(axis_name)
+    tiled = jnp.tile(x, (n,) + (1,) * (x.ndim - 1))
+    return lax.all_to_all(tiled, axis_name, split_axis=0, concat_axis=0, tiled=True)
+
+
 def per_device(resid_in, hidden, w_down, frozen, steer, forget_flags):
-    whole_hidden = lax.all_gather(hidden, "shard", axis=0, tiled=True)
-    tok_rows = resid_in.shape[0]
-    mlp_out = lax.psum_scatter(
-        jnp.dot(whole_hidden, w_down, preferred_element_type=jnp.float32),
-        "dp",
-        scatter_dimension=0,
-        tiled=True,
-    )
+    n_dp = lax.axis_size("dp")
+    tok_rows, d_cols = resid_in.shape
+    whole_hidden = gather_by_all_to_all(hidden, "shard")
+    partial = jnp.dot(whole_hidden, w_down, preferred_element_type=jnp.float32)
+    pieces = lax.all_to_all(partial, "dp", split_axis=0, concat_axis=0, tiled=True)
+    mlp_out = jnp.sum(pieces.reshape(n_dp, tok_rows, d_cols), axis=0)
     residual = resid_in.astype(jnp.float32) + mlp_out
     updated = residual.astype(jnp.bfloat16)
     target_rows = lax.all_to_all(frozen, "shard", split_axis=1, concat_axis=0, tiled=True)
@@ -27,7 +31,7 @@
     seq_ids = (start_row + jnp.arange(tok_rows, dtype=jnp.int32)) // SEQ_LEN
     seq_match = seq_ids[:, None] == jnp.arange(forget_flags.shape[0], dtype=jnp.int32)[None, :]
     is_forget = jnp.sum(jnp.where(seq_match, forget_flags[None, :], 0), axis=1) > 0
-    total_tokens = tok_rows * lax.axis_size("dp")
+    total_tokens = tok_rows * n_dp
     target = jnp.where(
         is_forget[:, None], steer.astype(jnp.float32)[None, :], target_rows.astype(jnp.float32)
     )
@@ -35,7 +39,7 @@
     slopes = (loss_weight[:, None] * (residual - target) * (1.0 / math.sqrt(total_tokens))).astype(
         jnp.bfloat16
     )
-    all_slopes = lax.all_gather(slopes, "dp", axis=0, tiled=True)
+    all_slopes = gather_by_all_to_all(slopes, "dp")
     grad_down = lax.dot_general(
         whole_hidden, all_slopes, (((0,), (0,)), ((), ())), preferred_element_type=jnp.float32
     )

time: 532 us -> 715 us (1.34)
  blocking collectives: 0 us -> 289 us
  waiting for transfers between devices: 471 us -> 360 us
  starting transfers between devices: 6.15 us -> 19.3 us
  between operations: 13.8 us -> 0.75 us
    all_to_all x0 -> x1, waiting for transfers between devices: none -> 360 us  [per_device(): lax.all_to_all(partial, 'dp', split_axis=0, concat_axis=0, tiled=True)]
    all_to_all x0 -> x2, blocking collectives: none -> 289 us  [gather_by_all_to_all(): lax.all_to_all(tiled, axis_name, split_axis=0, concat_axis=0, tiled=True)]
    all_gather x2 -> x0, waiting for transfers between devices: 261 us -> none  [the longest x1 155 us: per_device(): whole_hidden = lax.all_gather(hidden, 'shard', axis=0, tiled=True)]
    reduce_scatter x1 -> x0, waiting for transfers between devices: 206 us -> none  [per_device(): lax.psum_scatter(jnp.dot(whole_hidden, w_down, preferred_element_type=jnp...]
    all_to_all x0 -> x1, starting transfers between devices: none -> 13.3 us  [per_device(): lax.all_to_all(partial, 'dp', split_axis=0, concat_axis=0, tiled=True)]
    reduce_sum x0 -> x1, other arithmetic: none -> 7.49 us  [per_device(): mlp_out = jnp.sum(pieces.reshape(n_dp, tok_rows, d_cols), axis=0)]
  transfers between devices with their start and end apart: 4 -> 2, of which waited for: 4 -> 1; matrix products, arithmetic and copies ran while one was open for 0% -> 1% of each run, Pallas kernels for 0% -> 0%
where the time goes in v2:
time: 715 us; the launch traced here: 711 us
  waiting for transfers between devices  360 us (50%)
  blocking collectives  289 us (40%)
  matrix products  22.4 us (3%)
  starting transfers between devices  19.3 us (3%)
  local copies, waits for them, and re-layouts  12 us (2%)
  other arithmetic  8.49 us (1%)
    all_to_all x1, waiting for transfers between devices, per_device(): lax.all_to_all(partial, 'dp', split_axis=0, concat_axis=0, tiled=True)  360 us
    all_to_all x2, blocking collectives, gather_by_all_to_all(): lax.all_to_all(tiled, axis_name, split_axis=0, concat_axis=0, tiled=True)  289 us
  transfers between devices with their start and end apart: 2, of which 1 were waited for; matrix products, arithmetic and copies ran while one was open for 1% of the time, Pallas kernels for 0%

profile of v2, /device:TPU:29, one launch (start us, length us, event | category | flops | bytes accessed | tf_op | source)
XLA Modules:
  0.0 711.4 jit_solution(12974173704672447546)
XLA Ops:
  0.6 0.0 copy-start
  0.6 2.3 tile.4
  2.9 85.0 %all_to_all.37 = bf16[8,512,896]{2,1,0:T(8,128)(2,1)S(1)} all-to-all(bf16[8,512,896]{2,1,0:T(8,128)(2,1)S(1)} %tile.4), channel_id=1, replica_groups=mesh['dp'=32,'shard'=8] {'shard'}, dimensions={0} | all-to-all | bytes 14680064 | tf_op jit(solution)/shard_map/all_to_all | solution.py:17
  87.9 0.0 copy-start.2
  87.9 2.9 copy-done.2
  90.8 0.0 copy-done
  90.9 11.3 %fusion = f32[32,128,1024]{2,1,0:T(8,128)} fusion(bf16[32,128,896]{2,1,0:T(8,128)(2,1)S(1)} %bitcast.28, bf16[896,1024]{1,0:T(8,128)(2,1)S(1)} %copy-done), kind=kOutput, calls=%fused_computation.1 | convolution fusion | flops 7516192768 | bytes 25952256 | tf_op jit(solution)/shard_map/dot_general | solution.py:24
  102.2 0.0 copy-start.3
  102.2 0.0 copy-start.6
  102.2 0.0 copy-start.5
  102.2 13.3 %all-to-all-start.1 = ((f32[32,128,1024]{2,1,0:T(8,128)}), f32[32,128,1024]{2,1,0:T(8,128)}, u32[]{:S(2)}, u32[]{:S(2)}) async-start(f32[32,128,1024]{2,1,0:T(8,128)} %fusion), calls=%async_computation.1 | async-start | bytes 33554432 | tf_op jit(solution)/shard_map/all_to_all | solution.py:25
  115.5 0.0 copy-done.3
  115.5 0.7 copy.14
  116.2 0.0 copy-done.6
  116.3 0.1 select_reduce_fusion
  116.3 359.9 %all-to-all-done.1 = f32[32,128,1024]{2,1,0:T(8,128)} async-done(((f32[32,128,1024]{2,1,0:T(8,128)}), f32[32,128,1024]{2,1,0:T(8,128)}, u32[]{:S(2)}, u32[]{:S(2)}) %all-to-all-start.1) | async-done | bytes 16777248 | tf_op jit(solution)/shard_map/all_to_all | solution.py:25
  476.3 6.0 all-to-all-start.2
  482.3 0.0 copy-done.5
  482.3 0.0 copy-start.4
  482.3 7.5 %reduce_sum.18 = f32[128,1024]{1,0:T(8,128)S(1)} reduce(f32[32,128,1024]{2,1,0:T(8,128)} %all-to-all-done.1, f32[]{:T(128)} %constant.10.clone.1), dimensions={0}, to_apply=%region_0.0 | reduce | flops 4063232 | bytes 17301508 | tf_op jit(solution)/shard_map/reduce_sum | solution.py:26
  489.8 0.0 all-to-all-done.2
  489.8 0.0 copy-done.4
  489.8 0.9 fusion.5
  490.7 0.0 slice-start
  490.7 1.1 tile.5
  491.8 0.0 slice-start.1
  491.8 203.5 %all_to_all.38 = bf16[32,128,1024]{2,1,0:T(8,128)(2,1)S(1)} all-to-all(bf16[32,128,1024]{2,1,0:T(8,128)(2,1)S(1)} %tile.5), channel_id=1, replica_groups=mesh['dp'=32,'shard'=8] {'dp'}, dimensions={0} | all-to-all | bytes 16777216 | tf_op jit(solution)/shard_map/all_to_all | solution.py:17
  695.3 0.0 slice-done
  695.3 0.0 slice-done.1
  695.3 0.0 copy-start.1
  695.3 11.1 %convolution_bitcast_fusion = f32[896,1024]{0,1:T(8,128)} fusion(bf16[4096,1024]{1,0:T(8,128)(2,1)S(1)} %bitcast.27, bf16[4096,896]{1,0:T(8,128)(2,1)S(1)} %bitcast.31), kind=kOutput, calls=%fused_computation | convolution fusion | flops 7516192768 | bytes 19398656 | tf_op jit(solution)/shard_map/dot_general | solution.py:43
  706.4 5.0 copy.11
  711.4 0.0 copy-done.1
  (5 shorter events, 0.0 us)
Async XLA Ops:
  0.6 90.2 %copy-start = (bf16[896,1024]{1,0:T(8,128)(2,1)S(1)}, bf16[896,1024]{1,0:T(8,128)(2,1)}, u32[]{:S(2)}) copy-start(bf16[896,1024]{1,0:T(8,128)(2,1)} %param.8) | copy-start | bytes 5505028
  87.9 2.9 copy-start.2
  102.2 13.3 %copy-start.3 = (bf16[16,8192]{1,0:T(8,128)(2,1)S(1)}, bf16[16,8192]{1,0:T(8,128)(2,1)}, u32[]{:S(2)}) copy-start(bf16[16,8192]{1,0:T(8,128)(2,1)} %param.9) | copy-start | bytes 786436
  102.2 14.0 %copy-start.6 = (s32[16]{0:T(128)S(1)}, s32[16]{0:T(128)}, u32[]{:S(2)}) copy-start(s32[16]{0:T(128)} %param.11) | copy-start | bytes 196
  102.2 380.0 %copy-start.5 = (bf16[1024]{0:T(1024)(128)(2,1)S(1)}, bf16[1024]{0:T(1024)(128)(2,1)}, u32[]{:S(2)}) copy-start(bf16[1024]{0:T(1024)(128)(2,1)} %param.10) | copy-start | bytes 6148
  102.2 374.0 %all-to-all-start.1 = ((f32[32,128,1024]{2,1,0:T(8,128)}), f32[32,128,1024]{2,1,0:T(8,128)}, u32[]{:S(2)}, u32[]{:S(2)}) async-start(f32[32,128,1024]{2,1,0:T(8,128)} %fusion), calls=%async_computation.1 | async-start | bytes 33554432 | tf_op jit(solution)/shard_map/all_to_all | solution.py:25
  476.3 13.5 %all-to-all-start.2 = ((bf16[16,8,1024]{2,0,1:T(8,128)(2,1)}), bf16[16,8,1024]{2,0,1:T(8,128)(2,1)S(1)}, u32[]{:S(2)}, u32[]{:S(2)}) async-start(bf16[16,8,1024]{2,0,1:T(8,128)(2,1)} %bitcast.26), calls=%async_computation.2 | async-start | bytes 524288 | tf_op jit(solution)/shard_map/all_to_all | solution.py:29
  482.3 7.5 %copy-start.4 = (bf16[128,1024]{1,0:T(8,128)(2,1)S(1)}, bf16[128,1024]{1,0:T(8,128)(2,1)}, u32[]{:S(2)}) copy-start(bf16[128,1024]{1,0:T(8,128)(2,1)} %param.6) | copy-start | bytes 786436
  490.7 204.6 %slice-start = ((s8[7340032]{0:T(1024)(128)(4,1)}), s8[4194304]{0:T(1024)(128)(4,1)S(1)}, s32[]{:S(2)}) async-start(s8[7340032]{0:T(1024)(128)(4,1)} %bitcast.29), calls=%async_computation.4 | async-start | bytes 8388608
  491.8 203.6 %slice-start.1 = ((s8[7340032]{0:T(1024)(128)(4,1)}), s8[3145728]{0:T(1024)(128)(4,1)S(1)}, s32[]{:S(2)}) async-start(s8[7340032]{0:T(1024)(128)(4,1)} %bitcast.29), calls=%async_computation.5 | async-start | bytes 6291456
  695.3 16.1 %copy-start.1 = (bf16[896,1024]{1,0:T(8,128)(2,1)S(1)}, bf16[896,1024]{1,0:T(8,128)(2,1)}, u32[]{:S(2)}) copy-start(bf16[896,1024]{1,0:T(8,128)(2,1)} %param.8) | copy-start | bytes 5505028

commit v3 on v0

--- a/solution.py
+++ b/solution.py
@@ -1,18 +1,76 @@
+import functools
 import math
 
 import jax
 import jax.numpy as jnp
 from jax import lax
+from jax.experimental import pallas as pl
+from jax.experimental.pallas import tpu as pltpu
 from jax.sharding import PartitionSpec as P
 
 SEQ_LEN = 256
+MESH = pl.DeviceIdType.MESH
 
 
 retain_weight = 2.0
 
 
+def shard_gather_kernel(n, x_ref, out_ref, send_sem, recv_sem):
+    me = lax.axis_index("shard")
+    row = lax.axis_index("dp")
+
+    barrier = pltpu.get_barrier_semaphore()
+    for off in range(1, n):
+        peer = lax.rem(me + off, n)
+        pl.semaphore_signal(barrier, inc=1, device_id=(row, peer), device_id_type=MESH)
+    pl.semaphore_wait(barrier, n - 1)
+
+    local = pltpu.make_async_copy(x_ref, out_ref.at[me], recv_sem.at[me])
+    local.start()
+    copies = []
+    for off in range(1, n):
+        peer = lax.rem(me + off, n)
+        copy = pltpu.make_async_remote_copy(
+            src_ref=x_ref,
+            dst_ref=out_ref.at[me],
+            send_sem=send_sem.at[off - 1],
+            recv_sem=recv_sem.at[me],
+            device_id=(row, peer),
+            device_id_type=MESH,
+        )
+        copy.start()
+        copies.append(copy)
+    for copy in copies:
+        copy.wait_send()
+    local.wait()
+    for off in range(1, n):
+        src = lax.rem(me + n - off, n)
+        arrival = pltpu.make_async_remote_copy(
+            src_ref=x_ref,
+            dst_ref=out_ref.at[src],
+            send_sem=send_sem.at[off - 1],
+            recv_sem=recv_sem.at[src],
+            device_id=(row, src),
+            device_id_type=MESH,
+        )
+        arrival.wait_recv()
+
+
+def shard_gather(x):
+    n = lax.axis_size("shard")
+    out = pl.pallas_call(
+        functools.partial(shard_gather_kernel, n),
+        out_shape=jax.ShapeDtypeStruct((n,) + x.shape, x.dtype),
+        in_specs=[pl.BlockSpec(memory_space=pl.ANY)],
+        out_specs=pl.BlockSpec(memory_space=pl.ANY),
+        scratch_shapes=[pltpu.SemaphoreType.DMA((n - 1,)), pltpu.SemaphoreType.DMA((n,))],
+        compiler_params=pltpu.CompilerParams(collective_id=0, has_side_effects=True),
+    )(x)
+    return out.reshape((n * x.shape[0],) + x.shape[1:])
+
+
 def per_device(resid_in, hidden, w_down, frozen, steer, forget_flags):
-    whole_hidden = lax.all_gather(hidden, "shard", axis=0, tiled=True)
+    whole_hidden = shard_gather(hidden)
     tok_rows = resid_in.shape[0]
     mlp_out = lax.psum_scatter(
         jnp.dot(whole_hidden, w_down, preferred_element_type=jnp.float32),

time: 532 us -> 506 us (0.951)
  waiting for transfers between devices: 471 us -> 317 us
  Pallas kernels: 0 us -> 129 us
    all_gather x1 -> x0, waiting for transfers between devices: 155 us -> none  [per_device(): whole_hidden = lax.all_gather(hidden, 'shard', axis=0, tiled=True)]
    pallas_call x0 -> x1, Pallas kernels: none -> 129 us  [shard_gather(): pl.pallas_call(functools.partial(shard_gather_kernel, n), out_shape=jax.S...]
  transfers between devices with their start and end apart: 4 -> 3, of which waited for: 4 -> 3; matrix products, arithmetic and copies ran while one was open for 0% -> 0% of each run, Pallas kernels for 0% -> 0%
where the time goes in v3:
time: 506 us; the launch traced here: 503 us
  waiting for transfers between devices  317 us (63%)
  Pallas kernels  129 us (25%)
  matrix products  29 us (6%)
  between operations  14.1 us (3%)
  local copies, waits for them, and re-layouts  6.64 us (1%)
  starting transfers between devices  5.18 us (1%)
    reduce_scatter x1, waiting for transfers between devices, per_device(): lax.psum_scatter(jnp.dot(whole_hidden, w_down, preferred_element_type=jnp...  208 us
    pallas_call x1, Pallas kernels, shard_gather(): pl.pallas_call(functools.partial(shard_gather_kernel, n), out_shape=jax.S...  129 us
    all_gather x1, waiting for transfers between devices, per_device(): all_slopes = lax.all_gather(slopes, 'dp', axis=0, tiled=True)  106 us
    dot_general x1, matrix products, per_device(): lax.dot_general(whole_hidden, all_slopes, (((0,), (0,)), ((), ())), prefe...  14.6 us
    dot_general x1, matrix products, per_device(): jnp.dot(whole_hidden, w_down, preferred_element_type=jnp.float32)  14.3 us
  transfers between devices with their start and end apart: 3, of which 3 were waited for; matrix products, arithmetic and copies ran while one was open for 0% of the time, Pallas kernels for 0%

profile of v3, /device:TPU:29, one launch (start us, length us, event | category | flops | bytes accessed | tf_op | source)
XLA Modules:
  0.0 502.5 jit_solution(4373170235784485654)
XLA Ops:
  7.2 0.0 copy-start
  7.2 0.0 reduce-scatter.2.cloned.1.call-start
  7.2 128.6 %shard_map.77 = bf16[8,512,896]{2,1,0:T(8,128)(2,1)} custom-call(bf16[512,896]{1,0:T(8,128)(2,1)} %x_ref.1), custom_call_target="tpu_custom_call" | custom-call | tf_op jit(solution)/shard_map/pallas_call | solution.py:61
  135.8 0.0 copy-done
  135.8 14.3 %fusion.5 = f32[4096,1024]{1,0:T(8,128)} fusion(bf16[4096,896]{1,0:T(8,128)(2,1)} %bitcast.23, bf16[896,1024]{1,0:T(8,128)(2,1)S(1)} %copy-done), kind=kOutput, calls=%fused_computation.17 | convolution fusion | flops 7516192768 | bytes 25952256 | tf_op jit(solution)/shard_map/dot_general | solution.py:76
  150.2 0.0 copy-start.1
  150.2 0.0 copy-start.4
  150.2 0.0 copy-start.3
  150.2 0.0 copy-start.2
  150.2 0.0 reduce-scatter.2.cloned.1.call-update
  150.2 0.9 copy-done.1
  151.1 0.7 copy.14
  151.8 5.1 %all-to-all-start = ((bf16[16,8,1024]{2,0,1:T(8,128)(2,1)}), bf16[16,8,1024]{2,0,1:T(8,128)(2,1)S(1)}, u32[]{:S(2)}, u32[]{:S(2)}) async-start(bf16[16,8,1024]{2,0,1:T(8,128)(2,1)} %bitcast.22), calls=%async_computation.1 | async-start | bytes 524288 | tf_op jit(solution)/shard_map/all_to_all | solution.py:83
  157.0 0.0 all-gather.2.cloned.1.call-start
  157.0 0.0 copy-done.4
  157.0 0.1 select_reduce_fusion
  157.1 0.0 copy-done.3
  157.1 2.7 all-to-all-done
  159.8 208.4 %reduce-scatter.2.cloned.1.call-done = f32[128,1024]{1,0:T(8,128)} async-done(((f32[4096,1024]{1,0:T(8,128)}), f32[128,1024]{1,0:T(8,128)}) %reduce-scatter.2.cloned.1.call-update) | async-done | bytes 524304 | tf_op jit(solution)/shard_map/reduce_scatter | solution.py:75
  368.3 0.0 copy-done.2
  368.3 2.0 fusion.3
  370.3 0.0 all-gather.2.cloned.1.call-update
  370.3 105.8 %all-gather.2.cloned.1.call-done = bf16[4096,1024]{1,0:T(8,128)(2,1)} async-done(((bf16[128,1024]{1,0:T(8,128)(2,1)}), bf16[4096,1024]{1,0:T(8,128)(2,1)}) %all-gather.2.cloned.1.call-update) | async-done | bytes 8388624 | tf_op jit(solution)/shard_map/all_gather | solution.py:96
  476.1 14.6 %convolution_bitcast_fusion = f32[896,1024]{0,1:T(8,128)} fusion(bf16[4096,1024]{1,0:T(8,128)(2,1)} %all-gather.2.cloned.1.call-done, bf16[4096,896]{1,0:T(8,128)(2,1)} %bitcast.24), kind=kOutput, calls=%fused_computation | convolution fusion | flops 7516192768 | bytes 19398656 | tf_op jit(solution)/shard_map/dot_general | solution.py:97
  490.7 5.0 copy.11
  (4 shorter events, 0.0 us)
Async XLA Ops:
  7.2 128.7 %copy-start = (bf16[896,1024]{1,0:T(8,128)(2,1)S(1)}, bf16[896,1024]{1,0:T(8,128)(2,1)}, u32[]{:S(2)}) copy-start(bf16[896,1024]{1,0:T(8,128)(2,1)} %param.8) | copy-start | bytes 5505028
  7.2 361.1 %reduce-scatter.2.cloned.1.call-start = ((), (), s32[]{:S(2)}) async-start(), calls=%async_computation.2 | async-start | bytes 17301504 | tf_op jit(solution)/shard_map/reduce_scatter | solution.py:75
  150.2 0.9 copy-start.1
  150.2 6.8 %copy-start.4 = (s32[16]{0:T(128)S(1)}, s32[16]{0:T(128)}, u32[]{:S(2)}) copy-start(s32[16]{0:T(128)} %param.11) | copy-start | bytes 196
  150.2 6.9 %copy-start.3 = (bf16[1024]{0:T(1024)(128)(2,1)S(1)}, bf16[1024]{0:T(1024)(128)(2,1)}, u32[]{:S(2)}) copy-start(bf16[1024]{0:T(1024)(128)(2,1)} %param.10) | copy-start | bytes 6148
  150.2 218.1 %copy-start.2 = (bf16[128,1024]{1,0:T(8,128)(2,1)S(1)}, bf16[128,1024]{1,0:T(8,128)(2,1)}, u32[]{:S(2)}) copy-start(bf16[128,1024]{1,0:T(8,128)(2,1)} %param.6) | copy-start | bytes 786436
  151.8 8.0 %all-to-all-start = ((bf16[16,8,1024]{2,0,1:T(8,128)(2,1)}), bf16[16,8,1024]{2,0,1:T(8,128)(2,1)S(1)}, u32[]{:S(2)}, u32[]{:S(2)}) async-start(bf16[16,8,1024]{2,0,1:T(8,128)(2,1)} %bitcast.22), calls=%async_computation.1 | async-start | bytes 524288 | tf_op jit(solution)/shard_map/all_to_all | solution.py:83
  157.0 319.1 %all-gather.2.cloned.1.call-start = ((), (), s32[]{:S(2)}) async-start(), calls=%async_computation.3 | async-start | bytes 8650752 | tf_op jit(solution)/shard_map/all_gather | solution.py:96
Sparse Core Ops, SparseCore 0:
  150.3 217.8 reduce-scatter.1
  372.0 104.0 all-gather.1

commit v4 on v3

v4 whole, which is shorter than its diff:
```python
import functools
import math

import jax
import jax.numpy as jnp
from jax import lax
from jax.experimental import pallas as pl
from jax.experimental.pallas import tpu as pltpu
from jax.sharding import Mesh, PartitionSpec as P

SEQ_LEN = 256
MESH = pl.DeviceIdType.MESH


retain_weight = 2.0


def shard_gather_kernel(n, x_ref, out_ref, send_sem, recv_sem):
    me = lax.axis_index("shard")
    row = (lax.axis_index("yh"), lax.axis_index("z"), lax.axis_index("core"))

    barrier = pltpu.get_barrier_semaphore()
    for off in range(1, n):
        peer = lax.rem(me + off, n)
        pl.semaphore_signal(barrier, inc=1, device_id=row + (peer,), device_id_type=MESH)
    pl.semaphore_wait(barrier, n - 1)

    local = pltpu.make_async_copy(x_ref, out_ref.at[me], recv_sem.at[me])
    local.start()
    copies = []
    for off in range(1, n):
        peer = lax.rem(me + off, n)
        copy = pltpu.make_async_remote_copy(
            src_ref=x_ref,
            dst_ref=out_ref.at[me],
            send_sem=send_sem.at[off - 1],
            recv_sem=recv_sem.at[me],
            device_id=row + (peer,),
            device_id_type=MESH,
        )
        copy.start()
        copies.append(copy)
    for copy in copies:
        copy.wait_send()
    local.wait()
    for off in range(1, n):
        src = lax.rem(me + n - off, n)
        arrival = pltpu.make_async_remote_copy(
            src_ref=x_ref,
            dst_ref=out_ref.at[src],
            send_sem=send_sem.at[off - 1],
            recv_sem=recv_sem.at[src],
            device_id=row + (src,),
            device_id_type=MESH,
        )
        arrival.wait_recv()


def shard_gather(x):
    n = lax.axis_size("shard")
    out = pl.pallas_call(
        functools.partial(shard_gather_kernel, n),
        out_shape=jax.ShapeDtypeStruct((n,) + x.shape, x.dtype),
        in_specs=[pl.BlockSpec(memory_space=pl.ANY)],
        out_specs=pl.BlockSpec(memory_space=pl.ANY),
        scratch_shapes=[pltpu.SemaphoreType.DMA((n - 1,)), pltpu.SemaphoreType.DMA((n,))],
        compiler_params=pltpu.CompilerParams(collective_id=0, has_side_effects=True),
    )(x)
    return out.reshape((n * x.shape[0],) + x.shape[1:])


DP = ("yh", "z", "core")


def per_device(resid_in, hidden, w_down, frozen, steer, forget_flags):
    n_yh, n_z, n_c = (lax.axis_size(a) for a in DP)
    tok_rows, d_cols = resid_in.shape
    whole_hidden = shard_gather(hidden)
    total_tokens, ff_rows = whole_hidden.shape
    hp = (
        whole_hidden.reshape(n_yh, n_z, n_c, tok_rows, ff_rows)
        .transpose(2, 1, 0, 3, 4)
        .reshape(total_tokens, ff_rows)
    )
    partial = jnp.dot(hp, w_down, preferred_element_type=jnp.float32)
    partial = lax.psum_scatter(partial, "core", scatter_dimension=0, tiled=True)
    partial = lax.psum_scatter(partial, "z", scatter_dimension=0, tiled=True)
    mlp_out = lax.psum_scatter(partial, "yh", scatter_dimension=0, tiled=True)
    residual = resid_in.astype(jnp.float32) + mlp_out
    updated = residual.astype(jnp.bfloat16)
    target_rows = lax.all_to_all(frozen, "shard", split_axis=1, concat_axis=0, tiled=True)
    row_block = (lax.axis_index("yh") * n_z + lax.axis_index("z")) * n_c + lax.axis_index("core")
    start_row = row_block * tok_rows
    seq_ids = (start_row + jnp.arange(tok_rows, dtype=jnp.int32)) // SEQ_LEN
    seq_match = seq_ids[:, None] == jnp.arange(forget_flags.shape[0], dtype=jnp.int32)[None, :]
    is_forget = jnp.sum(jnp.where(seq_match, forget_flags[None, :], 0), axis=1) > 0
    target = jnp.where(
        is_forget[:, None], steer.astype(jnp.float32)[None, :], target_rows.astype(jnp.float32)
    )
    loss_weight = jnp.where(is_forget, 1.0, retain_weight).astype(jnp.float32)
    slopes = (loss_weight[:, None] * (residual - target) * (1.0 / math.sqrt(total_tokens))).astype(
        jnp.bfloat16
    )
    gathered = lax.all_gather(slopes, "yh", axis=0, tiled=True)
    gathered = lax.all_gather(gathered, "z", axis=0, tiled=True)
    all_slopes = lax.all_gather(gathered, "core", axis=0, tiled=True)
    grad_down = lax.dot_general(
        hp, all_slopes, (((0,), (0,)), ((), ())), preferred_element_type=jnp.float32
    )
    return (updated, grad_down)


def solution(mesh):
    n_dp, n_shard = mesh.devices.shape
    n_z = 8
    parts = mesh.devices.reshape(n_dp // (2 * n_z), n_z, 2, n_shard)
    split_mesh = Mesh(parts, DP + ("shard",))
    in_specs = (
        P(DP, "shard"),
        P("shard", DP),
        P(DP, "shard"),
        P(DP + ("shard",), None),
        P("shard"),
        P(),
    )
    out_specs = (P(DP, "shard"), P(DP, "shard"))
    return jax.shard_map(
        per_device, mesh=split_mesh, in_specs=in_specs, out_specs=out_specs, check_vma=False
    )
```

time: 506 us -> 437 us (0.86)
  waiting for transfers between devices: 317 us -> 237 us
  blocking collectives: 0 us -> 9.43 us
  local copies, waits for them, and re-layouts: 6.64 us -> 12.8 us
    reduce_scatter x1 -> x3, waiting for transfers between devices: 208 us -> 151 us  [the longest x1 98.5 us: per_device(): partial = lax.psum_scatter(partial, 'z', scatter_dimension=0, tiled=True)]
    all_gather x1 -> x2, waiting for transfers between devices: 106 us -> 82.7 us  [the longest x1 56.8 us: per_device(): gathered = lax.all_gather(gathered, 'z', axis=0, tiled=True)]
    all_gather x0 -> x1, blocking collectives: none -> 9.43 us  [per_device(): gathered = lax.all_gather(slopes, 'yh', axis=0, tiled=True)]
  transfers between devices with their start and end apart: 3 -> 6, of which waited for: 3 -> 6; matrix products, arithmetic and copies ran while one was open for 0% -> 0% of each run, Pallas kernels for 0% -> 0%
where the time goes in v4:
time: 437 us; the launch traced here: 436 us
  waiting for transfers between devices  237 us (54%)
  Pallas kernels  129 us (30%)
  matrix products  26.3 us (6%)
  between operations  13.9 us (3%)
  local copies, waits for them, and re-layouts  12.8 us (3%)
  blocking collectives  9.43 us (2%)
  starting transfers between devices  5.3 us (1%)
    pallas_call x1, Pallas kernels, shard_gather(): pl.pallas_call(functools.partial(shard_gather_kernel, n), out_shape=jax.S...  129 us
    reduce_scatter x1, waiting for transfers between devices, per_device(): partial = lax.psum_scatter(partial, 'z', scatter_dimension=0, tiled=True)  98.5 us
    all_gather x1, waiting for transfers between devices, per_device(): gathered = lax.all_gather(gathered, 'z', axis=0, tiled=True)  56.8 us
    reduce_scatter x1, waiting for transfers between devices, per_device(): partial = lax.psum_scatter(partial, 'core', scatter_dimension=0, tiled=True)  35.4 us
    all_gather x1, waiting for transfers between devices, per_device(): all_slopes = lax.all_gather(gathered, 'core', axis=0, tiled=True)  25.9 us
    reduce_scatter x1, waiting for transfers between devices, per_device(): mlp_out = lax.psum_scatter(partial, 'yh', scatter_dimension=0, tiled=True)  17.3 us
    dot_general x1, matrix products, per_device(): lax.dot_general(hp, all_slopes, (((0,), (0,)), ((), ())), preferred_eleme...  14.6 us
    dot_general x1, matrix products, per_device(): partial = jnp.dot(hp, w_down, preferred_element_type=jnp.float32)  11.7 us
  transfers between devices with their start and end apart: 6, of which 6 were waited for; matrix products, arithmetic and copies ran while one was open for 0% of the time, Pallas kernels for 0%

profile of v4, /device:TPU:29, one launch (start us, length us, event | category | flops | bytes accessed | tf_op | source)
XLA Modules:
  0.0 435.6 jit_solution(11179000097198311725)
XLA Ops:
  7.2 0.0 copy-start
  7.2 0.0 reduce-scatter.4.cloned.1.call-start
  7.2 128.6 %shard_map.77 = bf16[8,512,896]{2,1,0:T(8,128)(2,1)} custom-call(bf16[512,896]{1,0:T(8,128)(2,1)} %x_ref.1), custom_call_target="tpu_custom_call" | custom-call | tf_op jit(solution)/shard_map/pallas_call | solution.py:61
  135.8 4.0 copy.13
  139.9 0.0 copy-start.1
  139.9 3.0 copy-done.1
  142.9 0.0 copy-done
  142.9 11.7 %fusion.5 = f32[4096,1024]{1,0:T(8,128)} fusion(bf16[4096,896]{1,0:T(8,128)(2,1)S(1)} %bitcast.27, bf16[896,1024]{1,0:T(8,128)(2,1)S(1)} %copy-done), kind=kOutput, calls=%fused_computation.17 | convolution fusion | flops 7516192768 | bytes 25952256 | tf_op jit(solution)/shard_map/dot_general | solution.py:85
  154.5 0.0 reduce-scatter.4.cloned.1.call-update
  154.6 0.0 copy-start.2
  154.6 0.0 copy-start.5
  154.6 0.0 copy-start.4
  154.6 0.0 copy-start.3
  154.6 0.0 reduce-scatter.6.cloned.1.call-start
  154.7 35.4 %reduce-scatter.4.cloned.1.call-done = f32[2048,1024]{1,0:T(8,128)} async-done(((f32[4096,1024]{1,0:T(8,128)}), f32[2048,1024]{1,0:T(8,128)}) %reduce-scatter.4.cloned.1.call-update) | async-done | bytes 8388624 | tf_op jit(solution)/shard_map/reduce_scatter | solution.py:86
  190.1 0.0 reduce-scatter.6.cloned.1.call-update
  190.1 0.0 reduce-scatter.8.cloned.1.call-start
  190.2 98.5 %reduce-scatter.6.cloned.1.call-done = f32[256,1024]{1,0:T(8,128)} async-done(((f32[2048,1024]{1,0:T(8,128)}), f32[256,1024]{1,0:T(8,128)}) %reduce-scatter.6.cloned.1.call-update) | async-done | bytes 1048592 | tf_op jit(solution)/shard_map/reduce_scatter | solution.py:87
  288.7 0.0 reduce-scatter.8.cloned.1.call-update
  288.7 0.0 copy-done.2
  288.7 0.7 copy.18
  289.4 5.1 %all-to-all-start = ((bf16[16,8,1024]{2,0,1:T(8,128)(2,1)}), bf16[16,8,1024]{2,0,1:T(8,128)(2,1)S(1)}, u32[]{:S(2)}, u32[]{:S(2)}) async-start(bf16[16,8,1024]{2,0,1:T(8,128)(2,1)} %bitcast.25), calls=%async_computation.3 | async-start | bytes 524288 | tf_op jit(solution)/shard_map/all_to_all | solution.py:91
  294.6 0.0 all-gather.3.cloned.1.call-start
  294.6 0.0 copy-done.5
  294.6 0.1 select_reduce_fusion
  294.7 0.0 copy-done.4
  294.7 3.3 all-to-all-done
  298.0 17.3 %reduce-scatter.8.cloned.1.call-done = f32[128,1024]{1,0:T(8,128)} async-done(((f32[256,1024]{1,0:T(8,128)}), f32[128,1024]{1,0:T(8,128)}) %reduce-scatter.8.cloned.1.call-update) | async-done | bytes 524304 | tf_op jit(solution)/shard_map/reduce_scatter | solution.py:88
  315.3 0.0 copy-done.3
  315.3 1.9 fusion.3
  317.2 9.4 %all_gather.9 = bf16[256,1024]{1,0:T(8,128)(2,1)} all-gather(bf16[128,1024]{1,0:T(8,128)(2,1)S(1)} %get-tuple-element.8), channel_id=1, replica_groups=mesh['yh'=2,'z'=8,'core'=2,'shard'=8] {'yh'}, dimensions={0}, use_global_device_ids=true | all-gather | bytes 786432 | tf_op jit(solution)/shard_map/all_gather | solution.py:104
  326.7 0.0 all-gather.3.cloned.1.call-update
  326.7 0.0 all-gather.5.cloned.1.call-start
  326.8 56.8 %all-gather.3.cloned.1.call-done = bf16[2048,1024]{1,0:T(8,128)(2,1)} async-done(((bf16[256,1024]{1,0:T(8,128)(2,1)}), bf16[2048,1024]{1,0:T(8,128)(2,1)}) %all-gather.3.cloned.1.call-update) | async-done | bytes 4194320 | tf_op jit(solution)/shard_map/all_gather | solution.py:105
  383.6 0.0 all-gather.5.cloned.1.call-update
  383.6 25.9 %all-gather.5.cloned.1.call-done = bf16[4096,1024]{1,0:T(8,128)(2,1)} async-done(((bf16[2048,1024]{1,0:T(8,128)(2,1)}), bf16[4096,1024]{1,0:T(8,128)(2,1)}) %all-gather.5.cloned.1.call-update) | async-done | bytes 8388624 | tf_op jit(solution)/shard_map/all_gather | solution.py:106
  409.5 14.6 %convolution_bitcast_fusion = f32[896,1024]{0,1:T(8,128)} fusion(bf16[4096,1024]{1,0:T(8,128)(2,1)} %all-gather.5.cloned.1.call-done, bf16[4096,896]{1,0:T(8,128)(2,1)} %bitcast.28), kind=kOutput, calls=%fused_computation | convolution fusion | flops 7516192768 | bytes 19398656 | tf_op jit(solution)/shard_map/dot_general | solution.py:107
  424.1 5.0 %copy.15 = f32[896,1024]{1,0:T(8,128)} copy(f32[896,1024]{0,1:T(8,128)} %convolution_bitcast_fusion) | data formatting | bytes 7340032
  (4 shorter events, 0.0 us)
Async XLA Ops:
  7.2 135.7 %copy-start = (bf16[896,1024]{1,0:T(8,128)(2,1)S(1)}, bf16[896,1024]{1,0:T(8,128)(2,1)}, u32[]{:S(2)}) copy-start(bf16[896,1024]{1,0:T(8,128)(2,1)} %param.8) | copy-start | bytes 5505028
  7.2 182.9 %reduce-scatter.4.cloned.1.call-start = ((), (), s32[]{:S(2)}) async-start(), calls=%async_computation.4 | async-start | bytes 25165824 | tf_op jit(solution)/shard_map/reduce_scatter | solution.py:86
  139.9 3.0 copy-start.1
  154.6 134.1 %copy-start.2 = (bf16[16,8192]{1,0:T(8,128)(2,1)S(1)}, bf16[16,8192]{1,0:T(8,128)(2,1)}, u32[]{:S(2)}) copy-start(bf16[16,8192]{1,0:T(8,128)(2,1)} %param.9) | copy-start | bytes 786436
  154.6 140.0 %copy-start.5 = (s32[16]{0:T(128)S(1)}, s32[16]{0:T(128)}, u32[]{:S(2)}) copy-start(s32[16]{0:T(128)} %param.11) | copy-start | bytes 196
  154.6 140.1 %copy-start.4 = (bf16[1024]{0:T(1024)(128)(2,1)S(1)}, bf16[1024]{0:T(1024)(128)(2,1)}, u32[]{:S(2)}) copy-start(bf16[1024]{0:T(1024)(128)(2,1)} %param.10) | copy-start | bytes 6148
  154.6 160.7 %copy-start.3 = (bf16[128,1024]{1,0:T(8,128)(2,1)S(1)}, bf16[128,1024]{1,0:T(8,128)(2,1)}, u32[]{:S(2)}) copy-start(bf16[128,1024]{1,0:T(8,128)(2,1)} %param.6) | copy-start | bytes 786436
  154.6 134.1 %reduce-scatter.6.cloned.1.call-start = ((), (), s32[]{:S(2)}) async-start(), calls=%async_computation.5 | async-start | bytes 9437184 | tf_op jit(solution)/shard_map/reduce_scatter | solution.py:87
  190.1 125.2 %reduce-scatter.8.cloned.1.call-start = ((), (), s32[]{:S(2)}) async-start(), calls=%async_computation.6 | async-start | bytes 1572864 | tf_op jit(solution)/shard_map/reduce_scatter | solution.py:88
  289.4 8.6 %all-to-all-start = ((bf16[16,8,1024]{2,0,1:T(8,128)(2,1)}), bf16[16,8,1024]{2,0,1:T(8,128)(2,1)S(1)}, u32[]{:S(2)}, u32[]{:S(2)}) async-start(bf16[16,8,1024]{2,0,1:T(8,128)(2,1)} %bitcast.25), calls=%async_computation.3 | async-start | bytes 524288 | tf_op jit(solution)/shard_map/all_to_all | solution.py:91
  294.6 89.0 %all-gather.3.cloned.1.call-start = ((), (), s32[]{:S(2)}) async-start(), calls=%async_computation.7 | async-start | bytes 4718592 | tf_op jit(solution)/shard_map/all_gather | solution.py:105
  326.7 82.8 %all-gather.5.cloned.1.call-start = ((), (), s32[]{:S(2)}) async-start(), calls=%async_computation.8 | async-start | bytes 12582912 | tf_op jit(solution)/shard_map/all_gather | solution.py:106
Sparse Core Ops, SparseCore 0:
  154.7 35.3 reduce-scatter.3
  192.8 95.8 reduce-scatter.5
  291.3 23.9 reduce-scatter.7
  326.8 56.7 all-gather.2
  385.2 24.2 all-gather.4

commit v5 on v4

--- a/solution.py
+++ b/solution.py
@@ -15,14 +15,21 @@
 retain_weight = 2.0
 
 
-def shard_gather_kernel(n, x_ref, out_ref, send_sem, recv_sem):
-    me = lax.axis_index("shard")
-    row = (lax.axis_index("yh"), lax.axis_index("z"), lax.axis_index("core"))
+DP = ("yh", "z", "core")
+ALL_AXES = DP + ("shard",)
+
+
+def device_on(axis, index):
+    return tuple(index if a == axis else lax.axis_index(a) for a in ALL_AXES)
+
+
+def gather_kernel(axis, n, x_ref, out_ref, send_sem, recv_sem):
+    me = lax.axis_index(axis)
 
     barrier = pltpu.get_barrier_semaphore()
     for off in range(1, n):
         peer = lax.rem(me + off, n)
-        pl.semaphore_signal(barrier, inc=1, device_id=row + (peer,), device_id_type=MESH)
+        pl.semaphore_signal(barrier, inc=1, device_id=device_on(axis, peer), device_id_type=MESH)
     pl.semaphore_wait(barrier, n - 1)
 
     local = pltpu.make_async_copy(x_ref, out_ref.at[me], recv_sem.at[me])
@@ -35,7 +42,7 @@
             dst_ref=out_ref.at[me],
             send_sem=send_sem.at[off - 1],
             recv_sem=recv_sem.at[me],
-            device_id=row + (peer,),
+            device_id=device_on(axis, peer),
             device_id_type=MESH,
         )
         copy.start()
@@ -50,32 +57,59 @@
             dst_ref=out_ref.at[src],
             send_sem=send_sem.at[off - 1],
             recv_sem=recv_sem.at[src],
-            device_id=row + (src,),
+            device_id=device_on(axis, src),
             device_id_type=MESH,
         )
         arrival.wait_recv()
 
 
-def shard_gather(x):
-    n = lax.axis_size("shard")
-    out = pl.pallas_call(
-        functools.partial(shard_gather_kernel, n),
+def gather_along(x, axis, collective_id):
+    n = lax.axis_size(axis)
+    return pl.pallas_call(
+        functools.partial(gather_kernel, axis, n),
         out_shape=jax.ShapeDtypeStruct((n,) + x.shape, x.dtype),
         in_specs=[pl.BlockSpec(memory_space=pl.ANY)],
         out_specs=pl.BlockSpec(memory_space=pl.ANY),
         scratch_shapes=[pltpu.SemaphoreType.DMA((n - 1,)), pltpu.SemaphoreType.DMA((n,))],
-        compiler_params=pltpu.CompilerParams(collective_id=0, has_side_effects=True),
+        compiler_params=pltpu.CompilerParams(collective_id=collective_id, has_side_effects=True),
     )(x)
-    return out.reshape((n * x.shape[0],) + x.shape[1:])
 
 
-DP = ("yh", "z", "core")
+def swap_kernel(x_ref, out_ref, send_sem, recv_sem):
+    me = lax.axis_index("core")
+    partner = device_on("core", 1 - me)
+
+    barrier = pltpu.get_barrier_semaphore()
+    pl.semaphore_signal(barrier, inc=1, device_id=partner, device_id_type=MESH)
+    pl.semaphore_wait(barrier, 1)
+
+    copy = pltpu.make_async_remote_copy(
+        src_ref=x_ref.at[1 - me],
+        dst_ref=out_ref,
+        send_sem=send_sem,
+        recv_sem=recv_sem,
+        device_id=partner,
+        device_id_type=MESH,
+    )
+    copy.start()
+    copy.wait()
+
+
+def swap_halves(x, collective_id):
+    return pl.pallas_call(
+        swap_kernel,
+        out_shape=jax.ShapeDtypeStruct(x.shape[1:], x.dtype),
+        in_specs=[pl.BlockSpec(memory_space=pl.ANY)],
+        out_specs=pl.BlockSpec(memory_space=pl.ANY),
+        scratch_shapes=[pltpu.SemaphoreType.DMA(()), pltpu.SemaphoreType.DMA(())],
+        compiler_params=pltpu.CompilerParams(collective_id=collective_id, has_side_effects=True),
+    )(x)
 
 
 def per_device(resid_in, hidden, w_down, frozen, steer, forget_flags):
     n_yh, n_z, n_c = (lax.axis_size(a) for a in DP)
     tok_rows, d_cols = resid_in.shape
-    whole_hidden = shard_gather(hidden)
+    whole_hidden = gather_along(hidden, "shard", 0).reshape(-1, hidden.shape[1])
     total_tokens, ff_rows = whole_hidden.shape
     hp = (
         whole_hidden.reshape(n_yh, n_z, n_c, tok_rows, ff_rows)
@@ -83,7 +117,8 @@
         .reshape(total_tokens, ff_rows)
     )
     partial = jnp.dot(hp, w_down, preferred_element_type=jnp.float32)
-    partial = lax.psum_scatter(partial, "core", scatter_dimension=0, tiled=True)
+    halves = partial.reshape((n_c, total_tokens // n_c) + partial.shape[1:])
+    partial = halves[lax.axis_index("core")] + swap_halves(halves, 2)
     partial = lax.psum_scatter(partial, "z", scatter_dimension=0, tiled=True)
     mlp_out = lax.psum_scatter(partial, "yh", scatter_dimension=0, tiled=True)
     residual = resid_in.astype(jnp.float32) + mlp_out
@@ -103,7 +138,7 @@
     )
     gathered = lax.all_gather(slopes, "yh", axis=0, tiled=True)
     gathered = lax.all_gather(gathered, "z", axis=0, tiled=True)
-    all_slopes = lax.all_gather(gathered, "core", axis=0, tiled=True)
+    all_slopes = gather_along(gathered, "core", 1).reshape(total_tokens, d_cols)
     grad_down = lax.dot_general(
         hp, all_slopes, (((0,), (0,)), ((), ())), preferred_element_type=jnp.float32
     )

time: 437 us -> 530 us (1.21)
  Pallas kernels: 129 us -> 272 us
  waiting for transfers between devices: 237 us -> 175 us
  other arithmetic: 2.04 us -> 14 us
    pallas_call x1 -> x3, Pallas kernels: 129 us -> 272 us  [the longest x2 257 us: gather_along(): pl.pallas_call(functools.partial(gather_kernel, axis, n), out_shape=jax.S...]
    reduce_scatter x1 -> x0, waiting for transfers between devices: 35.4 us -> none  [per_device(): partial = lax.psum_scatter(partial, 'core', scatter_dimension=0, tiled=True)]
    all_gather x1 -> x0, waiting for transfers between devices: 25.9 us -> none  [per_device(): all_slopes = lax.all_gather(gathered, 'core', axis=0, tiled=True)]
    add x0 -> x1, other arithmetic: none -> 12 us  [per_device(): partial = halves[lax.axis_index('core')] + swap_halves(halves, 2)]
  transfers between devices with their start and end apart: 6 -> 4, of which waited for: 6 -> 4; matrix products, arithmetic and copies ran while one was open for 0% -> 0% of each run, Pallas kernels for 0% -> 0%
where the time goes in v5:
time: 530 us; the launch traced here: 528 us
  Pallas kernels  272 us (51%)
  waiting for transfers between devices  175 us (33%)
  matrix products  26.5 us (5%)
  other arithmetic  14 us (3%)
  between operations  13.8 us (3%)
  local copies, waits for them, and re-layouts  12.8 us (2%)
  blocking collectives  9.48 us (2%)
    pallas_call x2, Pallas kernels, gather_along(): pl.pallas_call(functools.partial(gather_kernel, axis, n), out_shape=jax.S...  257 us
    reduce_scatter x1, waiting for transfers between devices, per_device(): partial = lax.psum_scatter(partial, 'z', scatter_dimension=0, tiled=True)  97.2 us
    all_gather x1, waiting for transfers between devices, per_device(): gathered = lax.all_gather(gathered, 'z', axis=0, tiled=True)  56.8 us
    reduce_scatter x1, waiting for transfers between devices, per_device(): mlp_out = lax.psum_scatter(partial, 'yh', scatter_dimension=0, tiled=True)  17.1 us
    dot_general x1, matrix products, per_device(): lax.dot_general(hp, all_slopes, (((0,), (0,)), ((), ())), preferred_eleme...  14.7 us
    pallas_call x1, Pallas kernels, swap_halves(): pl.pallas_call(swap_kernel, out_shape=jax.ShapeDtypeStruct(x.shape[1:], x...  14.6 us
    add x1, other arithmetic, per_device(): partial = halves[lax.axis_index('core')] + swap_halves(halves, 2)  12 us
    dot_general x1, matrix products, per_device(): partial = jnp.dot(hp, w_down, preferred_element_type=jnp.float32)  11.7 us
  transfers between devices with their start and end apart: 4, of which 4 were waited for; matrix products, arithmetic and copies ran while one was open for 0% of the time, Pallas kernels for 0%

profile of v5, /device:TPU:29, one launch (start us, length us, event | category | flops | bytes accessed | tf_op | source)
XLA Modules:
  0.0 528.4 jit_solution(9581313597431127314)
XLA Ops:
  7.2 0.0 copy-start
  7.2 0.0 reduce-scatter.3.cloned.1.call-start
  7.2 128.6 %shard_map.77 = bf16[8,512,896]{2,1,0:T(8,128)(2,1)} custom-call(bf16[512,896]{1,0:T(8,128)(2,1)} %x_ref.1), custom_call_target="tpu_custom_call" | custom-call | tf_op jit(solution)/shard_map/pallas_call | solution.py:68
  135.8 4.0 copy.14
  139.9 0.0 copy-start.2
  139.9 3.0 copy-done.2
  142.9 0.0 copy-done
  142.9 11.7 %fusion.x_ref = f32[2,2048,1024]{2,1,0:T(8,128)} fusion(bf16[2,2048,896]{2,1,0:T(8,128)(2,1)S(1)} %bitcast.35, bf16[896,1024]{1,0:T(8,128)(2,1)S(1)} %copy-done), kind=kOutput, calls=%fused_computation.2 | convolution fusion | flops 7516192768 | bytes 25952256 | tf_op jit(solution)/shard_map/dot_general | solution.py:119
  154.6 14.6 %shard_map.78 = f32[2048,1024]{1,0:T(8,128)} custom-call(f32[2,2048,1024]{2,1,0:T(8,128)} %fusion.x_ref), custom_call_target="tpu_custom_call" | custom-call | tf_op jit(solution)/shard_map/pallas_call | solution.py:99
  169.3 12.0 %bitcast_add_fusion = f32[2048,1024]{1,0:T(8,128)} fusion(f32[2048,1024]{1,0:T(8,128)} %shard_map.78, f32[2,2048,1024]{2,1,0:T(8,128)} %fusion.x_ref, s32[]{:T(128)S(6)} %select_n.28), kind=kLoop, calls=%fused_computation | loop fusion | flops 2097152 | bytes 25165828 | tf_op jit(solution)/shard_map/add | solution.py:121
  181.3 0.0 copy-start.3
  181.3 0.0 copy-start.6
  181.3 0.0 copy-start.5
  181.3 0.0 copy-start.4
  181.3 0.0 reduce-scatter.3.cloned.1.call-update
  181.3 0.0 reduce-scatter.5.cloned.1.call-start
  181.3 97.2 %reduce-scatter.3.cloned.1.call-done = f32[256,1024]{1,0:T(8,128)} async-done(((f32[2048,1024]{1,0:T(8,128)}), f32[256,1024]{1,0:T(8,128)}) %reduce-scatter.3.cloned.1.call-update) | async-done | bytes 1048592 | tf_op jit(solution)/shard_map/reduce_scatter | solution.py:122
  278.6 0.0 reduce-scatter.5.cloned.1.call-update
  278.6 0.0 copy-done.3
  278.6 0.7 copy.19
  279.3 5.1 all-to-all-start
  284.5 0.0 all-gather.2.cloned.1.call-start
  284.5 0.0 copy-done.6
  284.5 0.1 select_reduce_fusion
  284.6 0.0 copy-done.5
  284.6 3.4 all-to-all-done
  288.0 17.1 %reduce-scatter.5.cloned.1.call-done = f32[128,1024]{1,0:T(8,128)} async-done(((f32[256,1024]{1,0:T(8,128)}), f32[128,1024]{1,0:T(8,128)}) %reduce-scatter.5.cloned.1.call-update) | async-done | bytes 524304 | tf_op jit(solution)/shard_map/reduce_scatter | solution.py:123
  305.0 0.0 copy-done.4
  305.0 1.9 fusion.5
  307.0 9.5 %all_gather.6 = bf16[256,1024]{1,0:T(8,128)(2,1)} all-gather(bf16[128,1024]{1,0:T(8,128)(2,1)S(1)} %get-tuple-element.8), channel_id=1, replica_groups=mesh['yh'=2,'z'=8,'core'=2,'shard'=8] {'yh'}, dimensions={0}, use_global_device_ids=true | all-gather | bytes 786432 | tf_op jit(solution)/shard_map/all_gather | solution.py:139
  316.5 0.0 all-gather.2.cloned.1.call-update
  316.5 56.8 %all-gather.2.cloned.1.call-done.x_ref = bf16[2048,1024]{1,0:T(8,128)(2,1)} async-done(((bf16[256,1024]{1,0:T(8,128)(2,1)}), bf16[2048,1024]{1,0:T(8,128)(2,1)}) %all-gather.2.cloned.1.call-update) | async-done | bytes 4194320 | tf_op jit(solution)/shard_map/all_gather | solution.py:140
  373.3 128.9 %shard_map.79 = bf16[2,2048,1024]{2,1,0:T(8,128)(2,1)} custom-call(bf16[2048,1024]{1,0:T(8,128)(2,1)} %all-gather.2.cloned.1.call-done.x_ref), custom_call_target="tpu_custom_call" | custom-call | tf_op jit(solution)/shard_map/pallas_call | solution.py:68
  502.2 0.0 copy-start.1
  502.2 14.7 %convolution_bitcast_fusion = f32[896,1024]{0,1:T(8,128)} fusion(bf16[4096,1024]{1,0:T(8,128)(2,1)} %bitcast.34, bf16[4096,896]{1,0:T(8,128)(2,1)} %bitcast.36), kind=kOutput, calls=%fused_computation.1 | convolution fusion | flops 7516192768 | bytes 19398656 | tf_op jit(solution)/shard_map/dot_general | solution.py:142
  516.9 5.0 copy.16
  521.9 0.0 copy-done.1
  (4 shorter events, 0.0 us)
Async XLA Ops:
  7.2 135.7 %copy-start = (bf16[896,1024]{1,0:T(8,128)(2,1)S(1)}, bf16[896,1024]{1,0:T(8,128)(2,1)}, u32[]{:S(2)}) copy-start(bf16[896,1024]{1,0:T(8,128)(2,1)} %param.8) | copy-start | bytes 5505028
  7.2 271.4 %reduce-scatter.3.cloned.1.call-start = ((), (), s32[]{:S(2)}) async-start(), calls=%async_computation.3 | async-start | bytes 9437184 | tf_op jit(solution)/shard_map/reduce_scatter | solution.py:122
  139.9 3.0 copy-start.2
  181.3 97.3 %copy-start.3 = (bf16[16,8192]{1,0:T(8,128)(2,1)S(1)}, bf16[16,8192]{1,0:T(8,128)(2,1)}, u32[]{:S(2)}) copy-start(bf16[16,8192]{1,0:T(8,128)(2,1)} %param.9) | copy-start | bytes 786436
  181.3 103.2 %copy-start.6 = (s32[16]{0:T(128)S(1)}, s32[16]{0:T(128)}, u32[]{:S(2)}) copy-start(s32[16]{0:T(128)} %param.11) | copy-start | bytes 196
  181.3 103.3 %copy-start.5 = (bf16[1024]{0:T(1024)(128)(2,1)S(1)}, bf16[1024]{0:T(1024)(128)(2,1)}, u32[]{:S(2)}) copy-start(bf16[1024]{0:T(1024)(128)(2,1)} %param.10) | copy-start | bytes 6148
  181.3 123.8 %copy-start.4 = (bf16[128,1024]{1,0:T(8,128)(2,1)S(1)}, bf16[128,1024]{1,0:T(8,128)(2,1)}, u32[]{:S(2)}) copy-start(bf16[128,1024]{1,0:T(8,128)(2,1)} %param.6) | copy-start | bytes 786436
  181.3 123.8 %reduce-scatter.5.cloned.1.call-start = ((), (), s32[]{:S(2)}) async-start(), calls=%async_computation.4 | async-start | bytes 1572864 | tf_op jit(solution)/shard_map/reduce_scatter | solution.py:123
  279.3 8.6 %all-to-all-start = ((bf16[16,8,1024]{2,0,1:T(8,128)(2,1)}), bf16[16,8,1024]{2,0,1:T(8,128)(2,1)S(1)}, u32[]{:S(2)}, u32[]{:S(2)}) async-start(bf16[16,8,1024]{2,0,1:T(8,128)(2,1)} %bitcast.32), calls=%async_computation.2 | async-start | bytes 524288 | tf_op jit(solution)/shard_map/all_to_all | solution.py:126
  284.5 88.9 %all-gather.2.cloned.1.call-start = ((), (), s32[]{:S(2)}) async-start(), calls=%async_computation.5 | async-start | bytes 4718592 | tf_op jit(solution)/shard_map/all_gather | solution.py:140
  502.2 19.7 %copy-start.1 = (bf16[896,1024]{1,0:T(8,128)(2,1)S(1)}, bf16[896,1024]{1,0:T(8,128)(2,1)}, u32[]{:S(2)}) copy-start(bf16[896,1024]{1,0:T(8,128)(2,1)} %param.8) | copy-start | bytes 5505028
Sparse Core Ops, SparseCore 0:
  181.4 97.0 reduce-scatter.2
  281.1 23.9 reduce-scatter.4
  316.6 56.6 all-gather.1

commit v6 on v5

--- a/solution.py
+++ b/solution.py
@@ -32,8 +32,6 @@
         pl.semaphore_signal(barrier, inc=1, device_id=device_on(axis, peer), device_id_type=MESH)
     pl.semaphore_wait(barrier, n - 1)
 
-    local = pltpu.make_async_copy(x_ref, out_ref.at[me], recv_sem.at[me])
-    local.start()
     copies = []
     for off in range(1, n):
         peer = lax.rem(me + off, n)
@@ -49,7 +47,6 @@
         copies.append(copy)
     for copy in copies:
         copy.wait_send()
-    local.wait()
     for off in range(1, n):
         src = lax.rem(me + n - off, n)
         arrival = pltpu.make_async_remote_copy(
@@ -65,7 +62,7 @@
 
 def gather_along(x, axis, collective_id):
     n = lax.axis_size(axis)
-    return pl.pallas_call(
+    received = pl.pallas_call(
         functools.partial(gather_kernel, axis, n),
         out_shape=jax.ShapeDtypeStruct((n,) + x.shape, x.dtype),
         in_specs=[pl.BlockSpec(memory_space=pl.ANY)],
@@ -73,9 +70,10 @@
         scratch_shapes=[pltpu.SemaphoreType.DMA((n - 1,)), pltpu.SemaphoreType.DMA((n,))],
         compiler_params=pltpu.CompilerParams(collective_id=collective_id, has_side_effects=True),
     )(x)
+    return lax.dynamic_update_index_in_dim(received, x, lax.axis_index(axis), 0)
 
 
-def swap_kernel(x_ref, out_ref, send_sem, recv_sem):
+def swap_kernel(halves, x_ref, out_ref, send_sem, recv_sem):
     me = lax.axis_index("core")
     partner = device_on("core", 1 - me)
 
@@ -84,7 +82,7 @@
     pl.semaphore_wait(barrier, 1)
 
     copy = pltpu.make_async_remote_copy(
-        src_ref=x_ref.at[1 - me],
+        src_ref=x_ref.at[1 - me] if halves else x_ref,
         dst_ref=out_ref,
         send_sem=send_sem,
         recv_sem=recv_sem,
@@ -95,10 +93,10 @@
     copy.wait()
 
 
-def swap_halves(x, collective_id):
+def swap_with_partner(x, collective_id, halves):
     return pl.pallas_call(
-        swap_kernel,
-        out_shape=jax.ShapeDtypeStruct(x.shape[1:], x.dtype),
+        functools.partial(swap_kernel, halves),
+        out_shape=jax.ShapeDtypeStruct(x.shape[1:] if halves else x.shape, x.dtype),
         in_specs=[pl.BlockSpec(memory_space=pl.ANY)],
         out_specs=pl.BlockSpec(memory_space=pl.ANY),
         scratch_shapes=[pltpu.SemaphoreType.DMA(()), pltpu.SemaphoreType.DMA(())],
@@ -118,7 +116,7 @@
     )
     partial = jnp.dot(hp, w_down, preferred_element_type=jnp.float32)
     halves = partial.reshape((n_c, total_tokens // n_c) + partial.shape[1:])
-    partial = halves[lax.axis_index("core")] + swap_halves(halves, 2)
+    partial = halves[lax.axis_index("core")] + swap_with_partner(halves, 2, True)
     partial = lax.psum_scatter(partial, "z", scatter_dimension=0, tiled=True)
     mlp_out = lax.psum_scatter(partial, "yh", scatter_dimension=0, tiled=True)
     residual = resid_in.astype(jnp.float32) + mlp_out
@@ -138,9 +136,20 @@
     )
     gathered = lax.all_gather(slopes, "yh", axis=0, tiled=True)
     gathered = lax.all_gather(gathered, "z", axis=0, tiled=True)
-    all_slopes = gather_along(gathered, "core", 1).reshape(total_tokens, d_cols)
+    partner_slopes = swap_with_partner(gathered, 1, False)
+    me_c = lax.axis_index("core")
+    hp_halves = hp.reshape(n_c, total_tokens // n_c, ff_rows)
+    contract = (((0,), (0,)), ((), ()))
     grad_down = lax.dot_general(
-        hp, all_slopes, (((0,), (0,)), ((), ())), preferred_element_type=jnp.float32
+        lax.dynamic_index_in_dim(hp_halves, me_c, keepdims=False),
+        gathered,
+        contract,
+        preferred_element_type=jnp.float32,
+    ) + lax.dot_general(
+        lax.dynamic_index_in_dim(hp_halves, 1 - me_c, keepdims=False),
+        partner_slopes,
+        contract,
+        preferred_element_type=jnp.float32,
     )
     return (updated, grad_down)
 

time: 530 us -> 405 us (0.76)
  Pallas kernels: 272 us -> 151 us
    pallas_call x2 -> x1, Pallas kernels: 257 us -> 129 us  [gather_along(): pl.pallas_call(functools.partial(gather_kernel, axis, n), out_shape=jax.S...]
    pallas_call x1 -> x2, Pallas kernels: 14.6 us -> 22.5 us  [swap_with_partner(): pl.pallas_call(functools.partial(swap_kernel, halves), out_shape=jax.Shap...]
    dot_general x1 -> x2, matrix products: 14.7 us -> 15.3 us  [the longest x1 8.23 us: per_device(): lax.dot_general(lax.dynamic_index_in_dim(hp_halves, me_c, keepdims=False)...]
where the time goes in v6:
time: 405 us; the launch traced here: 404 us
  waiting for transfers between devices  175 us (43%)
  Pallas kernels  151 us (37%)
  matrix products  27 us (7%)
  other arithmetic  14 us (3%)
  between operations  13.9 us (3%)
  blocking collectives  9.44 us (2%)
  local copies, waits for them, and re-layouts  8.84 us (2%)
  starting transfers between devices  5.22 us (1%)
    pallas_call x1, Pallas kernels, gather_along(): pl.pallas_call(functools.partial(gather_kernel, axis, n), out_shape=jax.S...  129 us
    reduce_scatter x1, waiting for transfers between devices, per_device(): partial = lax.psum_scatter(partial, 'z', scatter_dimension=0, tiled=True)  97.2 us
    all_gather x1, waiting for transfers between devices, per_device(): gathered = lax.all_gather(gathered, 'z', axis=0, tiled=True)  56.9 us
    pallas_call x2, Pallas kernels, swap_with_partner(): pl.pallas_call(functools.partial(swap_kernel, halves), out_shape=jax.Shap...  22.5 us
    reduce_scatter x1, waiting for transfers between devices, per_device(): mlp_out = lax.psum_scatter(partial, 'yh', scatter_dimension=0, tiled=True)  17 us
    add x1, other arithmetic, per_device(): halves[lax.axis_index('core')] + swap_with_partner(halves, 2, True)  12 us
    dot_general x1, matrix products, per_device(): partial = jnp.dot(hp, w_down, preferred_element_type=jnp.float32)  11.7 us
    all_gather x1, blocking collectives, per_device(): gathered = lax.all_gather(slopes, 'yh', axis=0, tiled=True)  9.44 us
  transfers between devices with their start and end apart: 4, of which 4 were waited for; matrix products, arithmetic and copies ran while one was open for 0% of the time, Pallas kernels for 0%

profile of v6, /device:TPU:29, one launch (start us, length us, event | category | flops | bytes accessed | tf_op | source)
XLA Modules:
  0.0 404.0 jit_solution(5375461660292447097)
XLA Ops:
  7.2 0.0 copy-start
  7.2 0.0 copy-start.4
  7.2 0.0 reduce-scatter.3.cloned.1.call-start
  7.2 128.6 %shard_map.77 = bf16[8,512,896]{2,1,0:T(8,128)(2,1)} custom-call(bf16[512,896]{1,0:T(8,128)(2,1)} %x_ref.1), custom_call_target="tpu_custom_call" | custom-call | tf_op jit(solution)/shard_map/pallas_call | solution.py:65
  135.8 0.0 copy-done.4
  135.9 1.1 bitcast_dynamic-update-slice_fusion
  136.9 4.0 copy.10
  140.9 0.0 copy-start.2
  141.0 3.0 copy-done.2
  143.9 0.0 copy-done
  144.0 11.7 %fusion.6.x_ref = f32[2,2048,1024]{2,1,0:T(8,128)} fusion(bf16[2,2048,896]{2,1,0:T(8,128)(2,1)S(1)} %bitcast.39, bf16[896,1024]{1,0:T(8,128)(2,1)S(1)} %copy-done), kind=kOutput, calls=%fused_computation.7 | convolution fusion | flops 7516192768 | bytes 25952256 | tf_op jit(solution)/shard_map/dot_general | solution.py:117
  155.7 14.6 %shard_map.78 = f32[2048,1024]{1,0:T(8,128)} custom-call(f32[2,2048,1024]{2,1,0:T(8,128)} %fusion.6.x_ref), custom_call_target="tpu_custom_call" | custom-call | tf_op jit(solution)/shard_map/pallas_call | solution.py:97
  170.3 12.0 %bitcast_add_fusion = f32[2048,1024]{1,0:T(8,128)} fusion(f32[2048,1024]{1,0:T(8,128)} %shard_map.78, f32[2,2048,1024]{2,1,0:T(8,128)} %fusion.6.x_ref, s32[]{:T(128)S(6)} %select_n.38), kind=kLoop, calls=%fused_computation | loop fusion | flops 2097152 | bytes 25165828 | tf_op jit(solution)/shard_map/add | solution.py:119
  182.3 0.0 copy-start.5
  182.3 0.0 copy-start.8
  182.3 0.0 copy-start.7
  182.3 0.0 copy-start.6
  182.3 0.0 reduce-scatter.3.cloned.1.call-update
  182.3 0.0 reduce-scatter.5.cloned.1.call-start
  182.4 97.2 %reduce-scatter.3.cloned.1.call-done = f32[256,1024]{1,0:T(8,128)} async-done(((f32[2048,1024]{1,0:T(8,128)}), f32[256,1024]{1,0:T(8,128)}) %reduce-scatter.3.cloned.1.call-update) | async-done | bytes 1048592 | tf_op jit(solution)/shard_map/reduce_scatter | solution.py:120
  279.6 0.0 reduce-scatter.5.cloned.1.call-update
  279.7 0.0 copy-done.5
  279.7 0.7 copy.14
  280.4 5.1 %all-to-all-start = ((bf16[16,8,1024]{2,0,1:T(8,128)(2,1)}), bf16[16,8,1024]{2,0,1:T(8,128)(2,1)S(1)}, u32[]{:S(2)}, u32[]{:S(2)}) async-start(bf16[16,8,1024]{2,0,1:T(8,128)(2,1)} %bitcast.37), calls=%async_computation.2 | async-start | bytes 524288 | tf_op jit(solution)/shard_map/all_to_all | solution.py:124
  285.5 0.0 all-gather.2.cloned.1.call-start
  285.5 0.0 copy-done.8
  285.6 0.1 select_reduce_fusion
  285.7 0.0 copy-done.7
  285.7 3.4 all-to-all-done
  289.1 17.0 %reduce-scatter.5.cloned.1.call-done = f32[128,1024]{1,0:T(8,128)} async-done(((f32[256,1024]{1,0:T(8,128)}), f32[128,1024]{1,0:T(8,128)}) %reduce-scatter.5.cloned.1.call-update) | async-done | bytes 524304 | tf_op jit(solution)/shard_map/reduce_scatter | solution.py:121
  306.1 0.0 copy-done.6
  306.1 1.9 fusion.14
  308.0 9.4 %all_gather.6 = bf16[256,1024]{1,0:T(8,128)(2,1)} all-gather(bf16[128,1024]{1,0:T(8,128)(2,1)S(1)} %get-tuple-element.2), channel_id=1, replica_groups=mesh['yh'=2,'z'=8,'core'=2,'shard'=8] {'yh'}, dimensions={0}, use_global_device_ids=true | all-gather | bytes 786432 | tf_op jit(solution)/shard_map/all_gather | solution.py:137
  317.5 0.0 all-gather.2.cloned.1.call-update
  317.5 56.9 %all-gather.2.cloned.1.call-done.x_ref = bf16[2048,1024]{1,0:T(8,128)(2,1)} async-done(((bf16[256,1024]{1,0:T(8,128)(2,1)}), bf16[2048,1024]{1,0:T(8,128)(2,1)}) %all-gather.2.cloned.1.call-update) | async-done | bytes 4194320 | tf_op jit(solution)/shard_map/all_gather | solution.py:138
  374.4 7.8 %shard_map.79 = bf16[2048,1024]{1,0:T(8,128)(2,1)} custom-call(bf16[2048,1024]{1,0:T(8,128)(2,1)} %all-gather.2.cloned.1.call-done.x_ref), custom_call_target="tpu_custom_call" | custom-call | tf_op jit(solution)/shard_map/pallas_call | solution.py:97
  382.2 0.0 copy-start.3
  382.2 7.0 %fusion = f32[896,1024]{1,0:T(8,128)S(1)} fusion(bf16[2048,1024]{1,0:T(8,128)(2,1)} %shard_map.79, bf16[2,2048,896]{2,1,0:T(8,128)(2,1)} %bitcast.40, s32[]{:T(128)S(6)} %select_n.43), kind=kOutput, calls=%fused_computation.1 | convolution fusion | flops 3758096384 | bytes 11534340 | tf_op jit(solution)/shard_map/dot_general | solution.py:148
  389.2 0.0 copy-done.3
  389.3 0.0 copy-start.1
  389.3 8.2 %fusion.8 = f32[896,1024]{1,0:T(8,128)} fusion(f32[896,1024]{1,0:T(8,128)S(1)} %fusion, bf16[2048,1024]{1,0:T(8,128)(2,1)S(1)} %copy-done.3, bf16[2,2048,896]{2,1,0:T(8,128)(2,1)} %bitcast.41, s32[]{:T(128)S(6)} %select_n.38), kind=kOutput, calls=%fused_computation.9 | convolution fusion | flops 3759013888 | bytes 15204356 | tf_op jit(solution)/shard_map/dot_general | solution.py:143
  397.5 0.0 copy-done.1
  (4 shorter events, 0.0 us)
Async XLA Ops:
  7.2 136.8 %copy-start = (bf16[896,1024]{1,0:T(8,128)(2,1)S(1)}, bf16[896,1024]{1,0:T(8,128)(2,1)}, u32[]{:S(2)}) copy-start(bf16[896,1024]{1,0:T(8,128)(2,1)} %param.8) | copy-start | bytes 5505028
  7.2 128.7 %copy-start.4 = (bf16[512,896]{1,0:T(8,128)(2,1)S(1)}, bf16[512,896]{1,0:T(8,128)(2,1)}, u32[]{:S(2)}) copy-start(bf16[512,896]{1,0:T(8,128)(2,1)} %x_ref.1) | copy-start | bytes 2752516
  7.2 272.4 %reduce-scatter.3.cloned.1.call-start = ((), (), s32[]{:S(2)}) async-start(), calls=%async_computation.3 | async-start | bytes 9437184 | tf_op jit(solution)/shard_map/reduce_scatter | solution.py:120
  140.9 3.0 copy-start.2
  182.3 97.4 %copy-start.5 = (bf16[16,8192]{1,0:T(8,128)(2,1)S(1)}, bf16[16,8192]{1,0:T(8,128)(2,1)}, u32[]{:S(2)}) copy-start(bf16[16,8192]{1,0:T(8,128)(2,1)} %param.9) | copy-start | bytes 786436
  182.3 103.2 %copy-start.8 = (s32[16]{0:T(128)S(1)}, s32[16]{0:T(128)}, u32[]{:S(2)}) copy-start(s32[16]{0:T(128)} %param.11) | copy-start | bytes 196
  182.3 103.3 %copy-start.7 = (bf16[1024]{0:T(1024)(128)(2,1)S(1)}, bf16[1024]{0:T(1024)(128)(2,1)}, u32[]{:S(2)}) copy-start(bf16[1024]{0:T(1024)(128)(2,1)} %param.10) | copy-start | bytes 6148
  182.3 123.8 %copy-start.6 = (bf16[128,1024]{1,0:T(8,128)(2,1)S(1)}, bf16[128,1024]{1,0:T(8,128)(2,1)}, u32[]{:S(2)}) copy-start(bf16[128,1024]{1,0:T(8,128)(2,1)} %param.6) | copy-start | bytes 786436
  182.3 123.8 %reduce-scatter.5.cloned.1.call-start = ((), (), s32[]{:S(2)}) async-start(), calls=%async_computation.4 | async-start | bytes 1572864 | tf_op jit(solution)/shard_map/reduce_scatter | solution.py:121
  280.4 8.7 %all-to-all-start = ((bf16[16,8,1024]{2,0,1:T(8,128)(2,1)}), bf16[16,8,1024]{2,0,1:T(8,128)(2,1)S(1)}, u32[]{:S(2)}, u32[]{:S(2)}) async-start(bf16[16,8,1024]{2,0,1:T(8,128)(2,1)} %bitcast.37), calls=%async_computation.2 | async-start | bytes 524288 | tf_op jit(solution)/shard_map/all_to_all | solution.py:124
  285.5 88.8 %all-gather.2.cloned.1.call-start = ((), (), s32[]{:S(2)}) async-start(), calls=%async_computation.5 | async-start | bytes 4718592 | tf_op jit(solution)/shard_map/all_gather | solution.py:138
  382.2 7.1 %copy-start.3 = (bf16[2048,1024]{1,0:T(8,128)(2,1)S(1)}, bf16[2048,1024]{1,0:T(8,128)(2,1)}, u32[]{:S(2)}) copy-start(bf16[2048,1024]{1,0:T(8,128)(2,1)} %all-gather.2.cloned.1.call-done.x_ref) | copy-start | bytes 12582916
  389.3 8.2 %copy-start.1 = (bf16[896,1024]{1,0:T(8,128)(2,1)S(1)}, bf16[896,1024]{1,0:T(8,128)(2,1)}, u32[]{:S(2)}) copy-start(bf16[896,1024]{1,0:T(8,128)(2,1)} %param.8) | copy-start | bytes 5505028
Sparse Core Ops, SparseCore 0:
  182.5 97.1 reduce-scatter.2
  282.1 23.9 reduce-scatter.4
  317.6 56.7 all-gather.1

commit v7 on v6

--- a/solution.py
+++ b/solution.py
@@ -23,7 +23,7 @@
     return tuple(index if a == axis else lax.axis_index(a) for a in ALL_AXES)
 
 
-def gather_kernel(axis, n, x_ref, out_ref, send_sem, recv_sem):
+def gather_kernel(axis, n, part, x_ref, out_ref, send_sem, recv_sem):
     me = lax.axis_index(axis)
 
     barrier = pltpu.get_barrier_semaphore()
@@ -36,7 +36,7 @@
     for off in range(1, n):
         peer = lax.rem(me + off, n)
         copy = pltpu.make_async_remote_copy(
-            src_ref=x_ref,
+            src_ref=x_ref.at[part],
             dst_ref=out_ref.at[me],
             send_sem=send_sem.at[off - 1],
             recv_sem=recv_sem.at[me],
@@ -50,7 +50,7 @@
     for off in range(1, n):
         src = lax.rem(me + n - off, n)
         arrival = pltpu.make_async_remote_copy(
-            src_ref=x_ref,
+            src_ref=x_ref.at[part],
             dst_ref=out_ref.at[src],
             send_sem=send_sem.at[off - 1],
             recv_sem=recv_sem.at[src],
@@ -60,17 +60,21 @@
         arrival.wait_recv()
 
 
-def gather_along(x, axis, collective_id):
-    n = lax.axis_size(axis)
+def gather_part(xt, part, collective_id):
+    n = lax.axis_size("shard")
+    block = xt.shape[1:]
     received = pl.pallas_call(
-        functools.partial(gather_kernel, axis, n),
-        out_shape=jax.ShapeDtypeStruct((n,) + x.shape, x.dtype),
+        functools.partial(gather_kernel, "shard", n, part),
+        out_shape=jax.ShapeDtypeStruct((n,) + block, xt.dtype),
         in_specs=[pl.BlockSpec(memory_space=pl.ANY)],
         out_specs=pl.BlockSpec(memory_space=pl.ANY),
         scratch_shapes=[pltpu.SemaphoreType.DMA((n - 1,)), pltpu.SemaphoreType.DMA((n,))],
         compiler_params=pltpu.CompilerParams(collective_id=collective_id, has_side_effects=True),
-    )(x)
-    return lax.dynamic_update_index_in_dim(received, x, lax.axis_index(axis), 0)
+        cost_estimate=pl.CostEstimate(
+            flops=0, bytes_accessed=2 * n * xt[part].nbytes, transcendentals=0
+        ),
+    )(xt)
+    return lax.dynamic_update_index_in_dim(received, xt[part], lax.axis_index("shard"), 0)
 
 
 def swap_kernel(halves, x_ref, out_ref, send_sem, recv_sem):
@@ -107,22 +111,34 @@
 def per_device(resid_in, hidden, w_down, frozen, steer, forget_flags):
     n_yh, n_z, n_c = (lax.axis_size(a) for a in DP)
     tok_rows, d_cols = resid_in.shape
-    whole_hidden = gather_along(hidden, "shard", 0).reshape(-1, hidden.shape[1])
-    total_tokens, ff_rows = whole_hidden.shape
-    hp = (
-        whole_hidden.reshape(n_yh, n_z, n_c, tok_rows, ff_rows)
-        .transpose(2, 1, 0, 3, 4)
-        .reshape(total_tokens, ff_rows)
-    )
-    partial = jnp.dot(hp, w_down, preferred_element_type=jnp.float32)
-    halves = partial.reshape((n_c, total_tokens // n_c) + partial.shape[1:])
-    partial = halves[lax.axis_index("core")] + swap_with_partner(halves, 2, True)
-    partial = lax.psum_scatter(partial, "z", scatter_dimension=0, tiled=True)
-    mlp_out = lax.psum_scatter(partial, "yh", scatter_dimension=0, tiled=True)
+    own_tokens, ff_rows = hidden.shape
+    n_parts = 2
+    sub = tok_rows // n_parts
+    blocks = own_tokens // tok_rows
+    total_tokens = own_tokens * lax.axis_size("shard")
+    me_c = lax.axis_index("core")
+    xt = hidden.reshape(blocks, n_parts, sub, ff_rows).swapaxes(0, 1)
+    hp_parts, mlp_parts = [], []
+    for part in range(n_parts):
+        if part > 0:
+            xt, _ = lax.optimization_barrier((xt, reduced))
+        got = gather_part(xt, part, 2 * part)
+        hp = (
+            got.reshape(n_yh, n_z, n_c, sub, ff_rows)
+            .transpose(2, 1, 0, 3, 4)
+            .reshape(n_c, n_z * n_yh * sub, ff_rows)
+        )
+        hp_parts.append(hp)
+        partial = jnp.dot(hp.reshape(-1, ff_rows), w_down, preferred_element_type=jnp.float32)
+        halves = partial.reshape((n_c, -1, d_cols))
+        reduced = halves[me_c] + swap_with_partner(halves, 2 * part + 1, True)
+        reduced_z = lax.psum_scatter(reduced, "z", scatter_dimension=0, tiled=True)
+        mlp_parts.append(lax.psum_scatter(reduced_z, "yh", scatter_dimension=0, tiled=True))
+    mlp_out = jnp.concatenate(mlp_parts, axis=0)
     residual = resid_in.astype(jnp.float32) + mlp_out
     updated = residual.astype(jnp.bfloat16)
     target_rows = lax.all_to_all(frozen, "shard", split_axis=1, concat_axis=0, tiled=True)
-    row_block = (lax.axis_index("yh") * n_z + lax.axis_index("z")) * n_c + lax.axis_index("core")
+    row_block = (lax.axis_index("yh") * n_z + lax.axis_index("z")) * n_c + me_c
     start_row = row_block * tok_rows
     seq_ids = (start_row + jnp.arange(tok_rows, dtype=jnp.int32)) // SEQ_LEN
     seq_match = seq_ids[:, None] == jnp.arange(forget_flags.shape[0], dtype=jnp.int32)[None, :]
@@ -136,21 +152,19 @@
     )
     gathered = lax.all_gather(slopes, "yh", axis=0, tiled=True)
     gathered = lax.all_gather(gathered, "z", axis=0, tiled=True)
-    partner_slopes = swap_with_partner(gathered, 1, False)
-    me_c = lax.axis_index("core")
-    hp_halves = hp.reshape(n_c, total_tokens // n_c, ff_rows)
+    partner_slopes = swap_with_partner(gathered, 2 * n_parts + 1, False)
     contract = (((0,), (0,)), ((), ()))
-    grad_down = lax.dot_general(
-        lax.dynamic_index_in_dim(hp_halves, me_c, keepdims=False),
-        gathered,
-        contract,
-        preferred_element_type=jnp.float32,
-    ) + lax.dot_general(
-        lax.dynamic_index_in_dim(hp_halves, 1 - me_c, keepdims=False),
-        partner_slopes,
-        contract,
-        preferred_element_type=jnp.float32,
-    )
+    grad_down = None
+    for part in range(n_parts):
+        for rows, got in ((me_c, gathered), (1 - me_c, partner_slopes)):
+            s_part = got.reshape(n_z * n_yh, n_parts, sub, d_cols)[:, part].reshape(-1, d_cols)
+            term = lax.dot_general(
+                lax.dynamic_index_in_dim(hp_parts[part], rows, keepdims=False),
+                s_part,
+                contract,
+                preferred_element_type=jnp.float32,
+            )
+            grad_down = term if grad_down is None else grad_down + term
     return (updated, grad_down)
 
 

time: 405 us -> 392 us (0.968)
  waiting for transfers between devices: 175 us -> 152 us
  local copies, waits for them, and re-layouts: 8.84 us -> 17.2 us
    reduce_scatter x2 -> x4, waiting for transfers between devices: 114 us -> 91.3 us  [the longest x2 56.9 us: per_device(): reduced_z = lax.psum_scatter(reduced, 'z', scatter_dimension=0, tiled=True)]
    dot_general x3 -> x6, matrix products: 27 us -> 24.2 us  [the longest x2 13.4 us: per_device(): jnp.dot(hp.reshape(-1, ff_rows), w_down, preferred_element_type=jnp.float32)]
    pallas_call x2 -> x3, Pallas kernels: 22.5 us -> 24.9 us  [swap_with_partner(): pl.pallas_call(functools.partial(swap_kernel, halves), out_shape=jax.Shap...]
    add x1 -> x2, other arithmetic: 12 us -> 13.6 us  [per_device(): reduced = halves[me_c] + swap_with_partner(halves, 2 * part + 1, True)]
    pallas_call x1 -> x2, Pallas kernels: 129 us -> 128 us  [gather_part(): pl.pallas_call(functools.partial(gather_kernel, 'shard', n, part), out_sh...]
  transfers between devices with their start and end apart: 4 -> 6, of which waited for: 4 -> 5; matrix products, arithmetic and copies ran while one was open for 0% -> 4% of each run, Pallas kernels for 0% -> 18%
where the time goes in v7:
time: 392 us; the launch traced here: 391 us
  Pallas kernels  152 us (39%)
  waiting for transfers between devices  152 us (39%)
  matrix products  24.2 us (6%)
  local copies, waits for them, and re-layouts  17.2 us (4%)
  other arithmetic  15.6 us (4%)
  between operations  14 us (4%)
  blocking collectives  9.62 us (2%)
  starting transfers between devices  5.3 us (1%)
    pallas_call x2, Pallas kernels, gather_part(): pl.pallas_call(functools.partial(gather_kernel, 'shard', n, part), out_sh...  128 us
    reduce_scatter x2, waiting for transfers between devices, per_device(): reduced_z = lax.psum_scatter(reduced, 'z', scatter_dimension=0, tiled=True)  56.9 us
    all_gather x1, waiting for transfers between devices, per_device(): gathered = lax.all_gather(gathered, 'z', axis=0, tiled=True)  56.9 us
    reduce_scatter x2, waiting for transfers between devices, per_device(): lax.psum_scatter(reduced_z, 'yh', scatter_dimension=0, tiled=True)  34.4 us
    pallas_call x3, Pallas kernels, swap_with_partner(): pl.pallas_call(functools.partial(swap_kernel, halves), out_shape=jax.Shap...  24.9 us
    add x2, other arithmetic, per_device(): reduced = halves[me_c] + swap_with_partner(halves, 2 * part + 1, True)  13.6 us
    dot_general x2, matrix products, per_device(): jnp.dot(hp.reshape(-1, ff_rows), w_down, preferred_element_type=jnp.float32)  13.4 us
    dot_general x4, matrix products, per_device(): lax.dot_general(lax.dynamic_index_in_dim(hp_parts[part], rows, keepdims=F...  10.8 us
  transfers between devices with their start and end apart: 6, of which 5 were waited for; matrix products, arithmetic and copies ran while one was open for 4% of the time, Pallas kernels for 18%

profile of v7, /device:TPU:29, one launch (start us, length us, event | category | flops | bytes accessed | tf_op | source)
XLA Modules:
  0.0 390.5 jit_solution(862453062501029783)
XLA Ops:
  7.2 0.0 copy-start
  7.2 0.0 reduce-scatter.5.cloned.1.call-start
  7.2 2.3 copy.22
  9.5 64.3 %shard_map.77 = bf16[8,4,64,896]{3,2,1,0:T(8,128)(2,1)} custom-call(bf16[2,4,64,896]{3,2,1,0:T(8,128)(2,1)} %bitcast.67), custom_call_target="tpu_custom_call" | custom-call | bytes 7340032 | tf_op jit(solution)/shard_map/pallas_call | solution.py:66
  73.8 0.8 slice_dynamic-update-slice_fusion
  74.6 2.4 copy.16
  77.1 1.8 copy-done.5
  78.9 6.7 %fusion.10.x_ref = f32[2,1024,1024]{2,1,0:T(8,128)} fusion(bf16[2,1024,896]{2,1,0:T(8,128)(2,1)S(1)} %bitcast.71, bf16[896,1024]{1,0:T(8,128)(2,1)S(1)} %copy-done), kind=kOutput, calls=%fused_computation.13 | convolution fusion | flops 3758096384 | bytes 13893632 | tf_op jit(solution)/shard_map/dot_general | solution.py:132
  85.5 8.6 %shard_map.78 = f32[1024,1024]{1,0:T(8,128)} custom-call(f32[2,1024,1024]{2,1,0:T(8,128)} %fusion.10.x_ref), custom_call_target="tpu_custom_call" | custom-call | tf_op jit(solution)/shard_map/pallas_call | solution.py:101
  94.2 6.8 %bitcast_add_fusion.1 = f32[1024,1024]{1,0:T(8,128)} fusion(f32[1024,1024]{1,0:T(8,128)} %shard_map.78, f32[2,1024,1024]{2,1,0:T(8,128)} %fusion.10.x_ref, s32[]{:T(128)S(6)} %select_n.42), kind=kLoop, calls=%fused_computation.1 | loop fusion | flops 1048576 | bytes 12582916 | tf_op jit(solution)/shard_map/add | solution.py:134
  101.0 0.0 reduce-scatter.5.cloned.1.call-update
  101.0 0.0 reduce-scatter.9.cloned.1.call-start
  101.0 63.3 %shard_map.79 = bf16[8,4,64,896]{3,2,1,0:T(8,128)(2,1)} custom-call(bf16[2,4,64,896]{3,2,1,0:T(8,128)(2,1)} %bitcast.68), custom_call_target="tpu_custom_call" | custom-call | bytes 7340032 | tf_op jit(solution)/shard_map/pallas_call | solution.py:66
  164.3 0.8 slice_dynamic-update-slice_fusion.1
  165.1 2.4 copy.17
  167.5 0.0 copy-start.7
  167.6 1.8 copy-done.7
  169.4 6.7 %fusion.8.x_ref = f32[2,1024,1024]{2,1,0:T(8,128)} fusion(bf16[2,1024,896]{2,1,0:T(8,128)(2,1)S(1)} %bitcast.74, bf16[896,1024]{1,0:T(8,128)(2,1)S(1)} %copy-done), kind=kOutput, calls=%fused_computation.11 | convolution fusion | flops 3758096384 | bytes 13893632 | tf_op jit(solution)/shard_map/dot_general | solution.py:132
  176.1 8.4 %shard_map.80 = f32[1024,1024]{1,0:T(8,128)} custom-call(f32[2,1024,1024]{2,1,0:T(8,128)} %fusion.8.x_ref), custom_call_target="tpu_custom_call" | custom-call | tf_op jit(solution)/shard_map/pallas_call | solution.py:101
  184.5 6.8 %bitcast_add_fusion = f32[1024,1024]{1,0:T(8,128)} fusion(f32[1024,1024]{1,0:T(8,128)} %shard_map.80, f32[2,1024,1024]{2,1,0:T(8,128)} %fusion.8.x_ref, s32[]{:T(128)S(6)} %select_n.42), kind=kLoop, calls=%fused_computation | loop fusion | flops 1048576 | bytes 12582916 | tf_op jit(solution)/shard_map/add | solution.py:134
  191.3 0.0 reduce-scatter.9.cloned.1.call-update
  191.3 0.0 reduce-scatter.7.cloned.1.call-start
  191.4 0.0 reduce-scatter.5.cloned.1.call-done
  191.4 0.7 reduce-scatter.7.cloned.1.call-update
  192.1 0.0 reduce-scatter.11.cloned.1.call-start
  192.1 56.9 %reduce-scatter.9.cloned.1.call-done = f32[128,1024]{1,0:T(8,128)} async-done(((f32[1024,1024]{1,0:T(8,128)}), f32[128,1024]{1,0:T(8,128)}) %reduce-scatter.9.cloned.1.call-update) | async-done | bytes 524304 | tf_op jit(solution)/shard_map/reduce_scatter | solution.py:135
  249.0 0.0 reduce-scatter.11.cloned.1.call-update
  249.0 0.7 copy.23
  249.8 5.1 %all-to-all-start = ((bf16[16,8,1024]{2,0,1:T(8,128)(2,1)}), bf16[16,8,1024]{2,0,1:T(8,128)(2,1)S(1)}, u32[]{:S(2)}, u32[]{:S(2)}) async-start(bf16[16,8,1024]{2,0,1:T(8,128)(2,1)} %bitcast.62), calls=%async_computation.4 | async-start | bytes 524288 | tf_op jit(solution)/shard_map/all_to_all | solution.py:140
  254.9 0.1 select_reduce_fusion
  255.0 3.4 all-to-all-done
  258.4 11.3 %reduce-scatter.7.cloned.1.call-done = f32[64,1024]{1,0:T(8,128)} async-done(((f32[128,1024]{1,0:T(8,128)}), f32[64,1024]{1,0:T(8,128)}) %reduce-scatter.7.cloned.1.call-update) | async-done | bytes 262160 | tf_op jit(solution)/shard_map/reduce_scatter | solution.py:136
  269.7 23.1 %reduce-scatter.11.cloned.1.call-done = f32[64,1024]{1,0:T(8,128)} async-done(((f32[128,1024]{1,0:T(8,128)}), f32[64,1024]{1,0:T(8,128)}) %reduce-scatter.11.cloned.1.call-update) | async-done | bytes 262160 | tf_op jit(solution)/shard_map/reduce_scatter | solution.py:136
  292.8 1.9 fusion.21
  294.7 9.6 %all_gather.6 = bf16[256,1024]{1,0:T(8,128)(2,1)} all-gather(bf16[128,1024]{1,0:T(8,128)(2,1)S(1)} %get-tuple-element.8), channel_id=1, replica_groups=mesh['yh'=2,'z'=8,'core'=2,'shard'=8] {'yh'}, dimensions={0}, use_global_device_ids=true | all-gather | bytes 786432 | tf_op jit(solution)/shard_map/all_gather | solution.py:153
  304.4 0.0 all-gather.2.cloned.1.call-update
  304.4 56.9 %all-gather.2.cloned.1.call-done.x_ref = bf16[2048,1024]{1,0:T(8,128)(2,1)} async-done(((bf16[256,1024]{1,0:T(8,128)(2,1)}), bf16[2048,1024]{1,0:T(8,128)(2,1)}) %all-gather.2.cloned.1.call-update) | async-done | bytes 4194320 | tf_op jit(solution)/shard_map/all_gather | solution.py:154
  361.2 7.8 %shard_map.81 = bf16[2048,1024]{1,0:T(8,128)(2,1)} custom-call(bf16[2048,1024]{1,0:T(8,128)(2,1)} %all-gather.2.cloned.1.call-done.x_ref), custom_call_target="tpu_custom_call" | custom-call | tf_op jit(solution)/shard_map/pallas_call | solution.py:101
  369.1 0.0 copy-start.8
  369.1 2.9 fusion.28
  372.0 0.4 copy-done.8
  372.4 2.1 fusion
  374.5 2.1 fusion.4
  376.7 0.1 copy-done.2
  376.7 0.7 fusion.27
  377.4 2.1 fusion.2
  379.5 0.0 copy-start.1
  379.6 4.4 %add_add_fusion = f32[896,1024]{1,0:T(8,128)} fusion(f32[896,1024]{1,0:T(8,128)S(1)} %fusion, f32[896,1024]{1,0:T(8,128)S(1)} %fusion.2, f32[896,1024]{1,0:T(8,128)S(1)} %fusion.4, bf16[1024,1024]{1,0:T(8,128)(2,1)S(1)} %bitcast.77, bf16[2,1024,896]{2,1,0:T(8,128)(2,1)S(1)} %bitcast.73, s32[]{:T(128)S(6)} %select_n.42), kind=kOutput, calls=%fused_computation.2 | convolution fusion | flops 1881800704 | bytes 18612228 | tf_op jit(solution)/shard_map/dot_general | solution.py:161
  (23 shorter events, 0.1 us)
Async XLA Ops:
  7.2 71.7 %copy-start = (bf16[896,1024]{1,0:T(8,128)(2,1)S(1)}, bf16[896,1024]{1,0:T(8,128)(2,1)}, u32[]{:S(2)}) copy-start(bf16[896,1024]{1,0:T(8,128)(2,1)} %param.8) | copy-start | bytes 5505028
  7.2 184.2 %reduce-scatter.5.cloned.1.call-start = ((), (), s32[]{:S(2)}) async-start(), calls=%async_computation.5 | async-start | bytes 4718592 | tf_op jit(solution)/shard_map/reduce_scatter | solution.py:135
  9.5 64.3 %copy-start.3 = (bf16[4,2,64,896]{3,2,0,1:T(8,128)(2,1)S(1)}, bf16[4,2,64,896]{3,2,0,1:T(8,128)(2,1)}, u32[]{:S(2)}) copy-start(bf16[4,2,64,896]{3,2,0,1:T(8,128)(2,1)} %copy.22) | copy-start | bytes 2752516
  77.1 1.8 copy-start.5
  101.0 63.3 %copy-start.4 = (bf16[4,2,64,896]{3,2,0,1:T(8,128)(2,1)S(1)}, bf16[4,2,64,896]{3,2,0,1:T(8,128)(2,1)}, u32[]{:S(2)}) copy-start(bf16[4,2,64,896]{3,2,0,1:T(8,128)(2,1)} %copy.22) | copy-start | bytes 2752516
  101.0 148.0 %reduce-scatter.9.cloned.1.call-start = ((), (), s32[]{:S(2)}) async-start(), calls=%async_computation.7 | async-start | bytes 4718592 | tf_op jit(solution)/shard_map/reduce_scatter | solution.py:135
  167.5 1.8 copy-start.7
  191.3 57.7 %copy-start.9 = (bf16[16,8192]{1,0:T(8,128)(2,1)S(1)}, bf16[16,8192]{1,0:T(8,128)(2,1)}, u32[]{:S(2)}) copy-start(bf16[16,8192]{1,0:T(8,128)(2,1)} %param.9) | copy-start | bytes 786436
  191.3 63.6 %copy-start.12 = (s32[16]{0:T(128)S(1)}, s32[16]{0:T(128)}, u32[]{:S(2)}) copy-start(s32[16]{0:T(128)} %param.11) | copy-start | bytes 196
  191.3 63.7 %copy-start.11 = (bf16[1024]{0:T(1024)(128)(2,1)S(1)}, bf16[1024]{0:T(1024)(128)(2,1)}, u32[]{:S(2)}) copy-start(bf16[1024]{0:T(1024)(128)(2,1)} %param.10) | copy-start | bytes 6148
  191.3 101.5 %copy-start.10 = (bf16[128,1024]{1,0:T(8,128)(2,1)S(1)}, bf16[128,1024]{1,0:T(8,128)(2,1)}, u32[]{:S(2)}) copy-start(bf16[128,1024]{1,0:T(8,128)(2,1)} %param.6) | copy-start | bytes 786436
  191.3 78.3 %reduce-scatter.7.cloned.1.call-start = ((), (), s32[]{:S(2)}) async-start(), calls=%async_computation.6 | async-start | bytes 786432 | tf_op jit(solution)/shard_map/reduce_scatter | solution.py:136
  192.1 100.7 %reduce-scatter.11.cloned.1.call-start = ((), (), s32[]{:S(2)}) async-start(), calls=%async_computation.8 | async-start | bytes 786432 | tf_op jit(solution)/shard_map/reduce_scatter | solution.py:136
  249.8 8.7 %all-to-all-start = ((bf16[16,8,1024]{2,0,1:T(8,128)(2,1)}), bf16[16,8,1024]{2,0,1:T(8,128)(2,1)S(1)}, u32[]{:S(2)}, u32[]{:S(2)}) async-start(bf16[16,8,1024]{2,0,1:T(8,128)(2,1)} %bitcast.62), calls=%async_computation.4 | async-start | bytes 524288 | tf_op jit(solution)/shard_map/all_to_all | solution.py:140
  254.9 106.4 %all-gather.2.cloned.1.call-start = ((), (), s32[]{:S(2)}) async-start(), calls=%async_computation.9 | async-start | bytes 4718592 | tf_op jit(solution)/shard_map/all_gather | solution.py:154
  369.1 3.3 copy-start.8
  372.4 2.1 copy-start.6
  374.5 2.2 copy-start.2
  379.5 4.5 %copy-start.1 = (bf16[896,1024]{1,0:T(8,128)(2,1)S(1)}, bf16[896,1024]{1,0:T(8,128)(2,1)}, u32[]{:S(2)}) copy-start(bf16[896,1024]{1,0:T(8,128)(2,1)} %param.8) | copy-start | bytes 5505028
Sparse Core Ops, SparseCore 0:
  101.1 57.5 reduce-scatter.4
  191.4 57.5 reduce-scatter.8
  251.5 18.1 reduce-scatter.6
  272.2 20.5 reduce-scatter.10
  304.5 56.7 all-gather.1

commit v8 on v7

--- a/solution.py
+++ b/solution.py
@@ -77,9 +77,9 @@
     return lax.dynamic_update_index_in_dim(received, xt[part], lax.axis_index("shard"), 0)
 
 
-def swap_kernel(halves, x_ref, out_ref, send_sem, recv_sem):
-    me = lax.axis_index("core")
-    partner = device_on("core", 1 - me)
+def swap_kernel(axis, halves, x_ref, out_ref, send_sem, recv_sem):
+    me = lax.axis_index(axis)
+    partner = device_on(axis, 1 - me)
 
     barrier = pltpu.get_barrier_semaphore()
     pl.semaphore_signal(barrier, inc=1, device_id=partner, device_id_type=MESH)
@@ -97,9 +97,9 @@
     copy.wait()
 
 
-def swap_with_partner(x, collective_id, halves):
+def swap_with_partner(x, collective_id, halves, axis="core"):
     return pl.pallas_call(
-        functools.partial(swap_kernel, halves),
+        functools.partial(swap_kernel, axis, halves),
         out_shape=jax.ShapeDtypeStruct(x.shape[1:] if halves else x.shape, x.dtype),
         in_specs=[pl.BlockSpec(memory_space=pl.ANY)],
         out_specs=pl.BlockSpec(memory_space=pl.ANY),
@@ -117,6 +117,7 @@
     blocks = own_tokens // tok_rows
     total_tokens = own_tokens * lax.axis_size("shard")
     me_c = lax.axis_index("core")
+    me_yh = lax.axis_index("yh")
     xt = hidden.reshape(blocks, n_parts, sub, ff_rows).swapaxes(0, 1)
     hp_parts, mlp_parts = [], []
     for part in range(n_parts):
@@ -133,7 +134,8 @@
         halves = partial.reshape((n_c, -1, d_cols))
         reduced = halves[me_c] + swap_with_partner(halves, 2 * part + 1, True)
         reduced_z = lax.psum_scatter(reduced, "z", scatter_dimension=0, tiled=True)
-        mlp_parts.append(lax.psum_scatter(reduced_z, "yh", scatter_dimension=0, tiled=True))
+        by_yh = reduced_z.reshape((n_yh, -1, d_cols))
+        mlp_parts.append(by_yh[me_yh] + swap_with_partner(by_yh, 6 + part, True, "yh"))
     mlp_out = jnp.concatenate(mlp_parts, axis=0)
     residual = resid_in.astype(jnp.float32) + mlp_out
     updated = residual.astype(jnp.bfloat16)
@@ -150,7 +152,12 @@
     slopes = (loss_weight[:, None] * (residual - target) * (1.0 / math.sqrt(total_tokens))).astype(
         jnp.bfloat16
     )
-    gathered = lax.all_gather(slopes, "yh", axis=0, tiled=True)
+    other_yh = swap_with_partner(slopes, 6 + n_parts, False, "yh")
+    gathered = jnp.where(
+        me_yh == 0,
+        jnp.concatenate([slopes, other_yh], axis=0),
+        jnp.concatenate([other_yh, slopes], axis=0),
+    )
     gathered = lax.all_gather(gathered, "z", axis=0, tiled=True)
     partner_slopes = swap_with_partner(gathered, 2 * n_parts + 1, False)
     contract = (((0,), (0,)), ((), ()))

time: 392 us -> 359 us (0.916)
  waiting for transfers between devices: 152 us -> 97.3 us
  Pallas kernels: 152 us -> 178 us
  blocking collectives: 9.62 us -> 0 us
    reduce_scatter x2 -> x0, waiting for transfers between devices: 34.4 us -> none  [per_device(): lax.psum_scatter(reduced_z, 'yh', scatter_dimension=0, tiled=True)]
    pallas_call x3 -> x6, Pallas kernels: 24.9 us -> 51 us  [swap_with_partner(): pl.pallas_call(functools.partial(swap_kernel, axis, halves), out_shape=ja...]
    reduce_scatter x2, waiting for transfers between devices: 56.9 us -> 41.9 us  [per_device(): reduced_z = lax.psum_scatter(reduced, 'z', scatter_dimension=0, tiled=True)]
    all_gather x1 -> x0, blocking collectives: 9.62 us -> none  [per_device(): gathered = lax.all_gather(slopes, 'yh', axis=0, tiled=True)]
  transfers between devices with their start and end apart: 6 -> 4, of which waited for: 5 -> 2; matrix products, arithmetic and copies ran while one was open for 4% -> 6% of each run, Pallas kernels for 18% -> 25%
where the time goes in v8:
time: 359 us; the launch traced here: 358 us
  Pallas kernels  178 us (50%)
  waiting for transfers between devices  97.3 us (27%)
  matrix products  24.2 us (7%)
  local copies, waits for them, and re-layouts  19.5 us (5%)
  other arithmetic  19 us (5%)
  between operations  14 us (4%)
  starting transfers between devices  5.22 us (1%)
    pallas_call x2, Pallas kernels, gather_part(): pl.pallas_call(functools.partial(gather_kernel, 'shard', n, part), out_sh...  128 us
    all_gather x1, waiting for transfers between devices, per_device(): gathered = lax.all_gather(gathered, 'z', axis=0, tiled=True)  55.4 us
    pallas_call x6, Pallas kernels, swap_with_partner(): pl.pallas_call(functools.partial(swap_kernel, axis, halves), out_shape=ja...  51 us
    reduce_scatter x2, waiting for transfers between devices, per_device(): reduced_z = lax.psum_scatter(reduced, 'z', scatter_dimension=0, tiled=True)  41.9 us
    add x2, other arithmetic, per_device(): reduced = halves[me_c] + swap_with_partner(halves, 2 * part + 1, True)  13.6 us
    dot_general x2, matrix products, per_device(): jnp.dot(hp.reshape(-1, ff_rows), w_down, preferred_element_type=jnp.float32)  13.4 us
    dot_general x4, matrix products, per_device(): lax.dot_general(lax.dynamic_index_in_dim(hp_parts[part], rows, keepdims=F...  10.8 us
  transfers between devices with their start and end apart: 4, of which 2 were waited for; matrix products, arithmetic and copies ran while one was open for 6% of the time, Pallas kernels for 25%

profile of v8, /device:TPU:29, one launch (start us, length us, event | category | flops | bytes accessed | tf_op | source)
XLA Modules:
  0.0 357.7 jit_solution(6077761164795972462)
XLA Ops:
  7.2 0.0 copy-start
  7.2 0.0 reduce-scatter.3.cloned.1.call-start
  7.2 2.3 copy.22
  9.5 64.3 %shard_map.77 = bf16[8,4,64,896]{3,2,1,0:T(8,128)(2,1)} custom-call(bf16[2,4,64,896]{3,2,1,0:T(8,128)(2,1)} %bitcast.73), custom_call_target="tpu_custom_call" | custom-call | bytes 7340032 | tf_op jit(solution)/shard_map/pallas_call | solution.py:66
  73.8 0.8 slice_dynamic-update-slice_fusion
  74.6 2.4 copy.16
  77.1 1.8 copy-done.5
  78.9 6.7 %fusion.10.x_ref = f32[2,1024,1024]{2,1,0:T(8,128)} fusion(bf16[2,1024,896]{2,1,0:T(8,128)(2,1)S(1)} %bitcast.77, bf16[896,1024]{1,0:T(8,128)(2,1)S(1)} %copy-done), kind=kOutput, calls=%fused_computation.13 | convolution fusion | flops 3758096384 | bytes 13893632 | tf_op jit(solution)/shard_map/dot_general | solution.py:133
  85.5 8.6 %shard_map.78 = f32[1024,1024]{1,0:T(8,128)} custom-call(f32[2,1024,1024]{2,1,0:T(8,128)} %fusion.10.x_ref), custom_call_target="tpu_custom_call" | custom-call | tf_op jit(solution)/shard_map/pallas_call | solution.py:101
  94.2 6.8 %bitcast_add_fusion.1 = f32[1024,1024]{1,0:T(8,128)} fusion(f32[1024,1024]{1,0:T(8,128)} %shard_map.78, f32[2,1024,1024]{2,1,0:T(8,128)} %fusion.10.x_ref, s32[]{:T(128)S(6)} %select_n.54), kind=kLoop, calls=%fused_computation.1 | loop fusion | flops 1048576 | bytes 12582916 | tf_op jit(solution)/shard_map/add | solution.py:135
  101.0 0.0 reduce-scatter.3.cloned.1.call-update
  101.0 0.0 reduce-scatter.5.cloned.1.call-start
  101.0 63.3 %shard_map.80 = bf16[8,4,64,896]{3,2,1,0:T(8,128)(2,1)} custom-call(bf16[2,4,64,896]{3,2,1,0:T(8,128)(2,1)} %bitcast.74), custom_call_target="tpu_custom_call" | custom-call | bytes 7340032 | tf_op jit(solution)/shard_map/pallas_call | solution.py:66
  164.3 0.8 slice_dynamic-update-slice_fusion.1
  165.1 2.4 copy.17
  167.5 0.0 copy-start.7
  167.6 1.8 copy-done.7
  169.4 6.7 %fusion.8.x_ref = f32[2,1024,1024]{2,1,0:T(8,128)} fusion(bf16[2,1024,896]{2,1,0:T(8,128)(2,1)S(1)} %bitcast.80, bf16[896,1024]{1,0:T(8,128)(2,1)S(1)} %copy-done), kind=kOutput, calls=%fused_computation.11 | convolution fusion | flops 3758096384 | bytes 13893632 | tf_op jit(solution)/shard_map/dot_general | solution.py:133
  176.1 8.4 %shard_map.81 = f32[1024,1024]{1,0:T(8,128)} custom-call(f32[2,1024,1024]{2,1,0:T(8,128)} %fusion.8.x_ref), custom_call_target="tpu_custom_call" | custom-call | tf_op jit(solution)/shard_map/pallas_call | solution.py:101
  184.5 6.8 %bitcast_add_fusion = f32[1024,1024]{1,0:T(8,128)} fusion(f32[1024,1024]{1,0:T(8,128)} %shard_map.81, f32[2,1024,1024]{2,1,0:T(8,128)} %fusion.8.x_ref, s32[]{:T(128)S(6)} %select_n.54), kind=kLoop, calls=%fused_computation | loop fusion | flops 1048576 | bytes 12582916 | tf_op jit(solution)/shard_map/add | solution.py:135
  191.3 0.0 reduce-scatter.5.cloned.1.call-update
  191.3 0.9 copy-done.9
  192.2 0.7 copy.23
  193.0 5.1 %all-to-all-start = ((bf16[16,8,1024]{2,0,1:T(8,128)(2,1)}), bf16[16,8,1024]{2,0,1:T(8,128)(2,1)S(1)}, u32[]{:S(2)}, u32[]{:S(2)}) async-start(bf16[16,8,1024]{2,0,1:T(8,128)(2,1)} %bitcast.68), calls=%async_computation.2 | async-start | bytes 524288 | tf_op jit(solution)/shard_map/all_to_all | solution.py:142
  198.1 0.0 all-gather.2.cloned.1.call-start
  198.2 0.1 select_reduce_fusion
  198.3 0.0 reduce-scatter.3.cloned.1.call-done
  198.3 8.9 %shard_map.79 = f32[64,1024]{1,0:T(8,128)} custom-call(f32[2,64,1024]{2,1,0:T(8,128)} %bitcast.87), custom_call_target="tpu_custom_call" | custom-call | tf_op jit(solution)/shard_map/pallas_call | solution.py:101
  207.2 41.8 %reduce-scatter.5.cloned.1.call-done = f32[128,1024]{1,0:T(8,128)} async-done(((f32[1024,1024]{1,0:T(8,128)}), f32[128,1024]{1,0:T(8,128)}) %reduce-scatter.5.cloned.1.call-update) | async-done | bytes 524304 | tf_op jit(solution)/shard_map/reduce_scatter | solution.py:136
  249.0 9.1 %shard_map.82 = f32[64,1024]{1,0:T(8,128)} custom-call(f32[2,64,1024]{2,1,0:T(8,128)} %bitcast.89), custom_call_target="tpu_custom_call" | custom-call | tf_op jit(solution)/shard_map/pallas_call | solution.py:101
  258.1 1.1 bitcast_add_fusion.3
  259.1 1.1 bitcast_add_fusion.2
  260.2 0.0 all-to-all-done
  260.2 1.0 fusion.21
  261.2 8.1 %shard_map.83 = bf16[128,1024]{1,0:T(8,128)(2,1)} custom-call(bf16[128,1024]{1,0:T(8,128)(2,1)} %get-tuple-element.8.x_ref), custom_call_target="tpu_custom_call" | custom-call | tf_op jit(solution)/shard_map/pallas_call | solution.py:101
  269.4 2.2 maximum_select_fusion
  271.6 0.0 all-gather.2.cloned.1.call-update
  271.6 55.4 %all-gather.2.cloned.1.call-done.x_ref = bf16[2048,1024]{1,0:T(8,128)(2,1)} async-done(((bf16[256,1024]{1,0:T(8,128)(2,1)}), bf16[2048,1024]{1,0:T(8,128)(2,1)}) %all-gather.2.cloned.1.call-update) | async-done | bytes 4194320 | tf_op jit(solution)/shard_map/all_gather | solution.py:161
  327.0 7.8 %shard_map.84 = bf16[2048,1024]{1,0:T(8,128)(2,1)} custom-call(bf16[2048,1024]{1,0:T(8,128)(2,1)} %all-gather.2.cloned.1.call-done.x_ref), custom_call_target="tpu_custom_call" | custom-call | tf_op jit(solution)/shard_map/pallas_call | solution.py:101
  334.8 2.9 fusion.28
  337.7 0.5 copy-done.2
  338.3 0.7 fusion.27
  339.0 1.3 copy-done.8
  340.3 2.1 fusion.2
  342.4 2.1 fusion.4
  344.6 2.1 fusion
  346.7 0.0 copy-start.1
  346.7 4.4 %add_add_fusion = f32[896,1024]{1,0:T(8,128)} fusion(f32[896,1024]{1,0:T(8,128)S(1)} %fusion, f32[896,1024]{1,0:T(8,128)S(1)} %fusion.2, f32[896,1024]{1,0:T(8,128)S(1)} %fusion.4, bf16[1024,1024]{1,0:T(8,128)(2,1)S(1)} %bitcast.83, bf16[2,1024,896]{2,1,0:T(8,128)(2,1)S(1)} %bitcast.79, s32[]{:T(128)S(6)} %select_n.54), kind=kOutput, calls=%fused_computation.2 | convolution fusion | flops 1881800704 | bytes 18612228 | tf_op jit(solution)/shard_map/dot_general | solution.py:168
  (22 shorter events, 0.1 us)
Async XLA Ops:
  7.2 71.7 %copy-start = (bf16[896,1024]{1,0:T(8,128)(2,1)S(1)}, bf16[896,1024]{1,0:T(8,128)(2,1)}, u32[]{:S(2)}) copy-start(bf16[896,1024]{1,0:T(8,128)(2,1)} %param.8) | copy-start | bytes 5505028
  7.2 191.1 %reduce-scatter.3.cloned.1.call-start = ((), (), s32[]{:S(2)}) async-start(), calls=%async_computation.3 | async-start | bytes 4718592 | tf_op jit(solution)/shard_map/reduce_scatter | solution.py:136
  9.5 64.3 %copy-start.3 = (bf16[4,2,64,896]{3,2,0,1:T(8,128)(2,1)S(1)}, bf16[4,2,64,896]{3,2,0,1:T(8,128)(2,1)}, u32[]{:S(2)}) copy-start(bf16[4,2,64,896]{3,2,0,1:T(8,128)(2,1)} %copy.22) | copy-start | bytes 2752516
  77.1 1.8 copy-start.5
  101.0 63.3 %copy-start.4 = (bf16[4,2,64,896]{3,2,0,1:T(8,128)(2,1)S(1)}, bf16[4,2,64,896]{3,2,0,1:T(8,128)(2,1)}, u32[]{:S(2)}) copy-start(bf16[4,2,64,896]{3,2,0,1:T(8,128)(2,1)} %copy.22) | copy-start | bytes 2752516
  101.0 148.0 %reduce-scatter.5.cloned.1.call-start = ((), (), s32[]{:S(2)}) async-start(), calls=%async_computation.4 | async-start | bytes 4718592 | tf_op jit(solution)/shard_map/reduce_scatter | solution.py:136
  167.5 1.8 copy-start.7
  191.3 0.9 copy-start.9
  191.3 6.8 %copy-start.11 = (bf16[1024]{0:T(1024)(128)(2,1)S(1)}, bf16[1024]{0:T(1024)(128)(2,1)}, u32[]{:S(2)}) copy-start(bf16[1024]{0:T(1024)(128)(2,1)} %param.10) | copy-start | bytes 6148
  191.3 6.9 %copy-start.12 = (s32[16]{0:T(128)S(1)}, s32[16]{0:T(128)}, u32[]{:S(2)}) copy-start(s32[16]{0:T(128)} %param.11) | copy-start | bytes 196
  191.3 68.9 %copy-start.10 = (bf16[128,1024]{1,0:T(8,128)(2,1)S(1)}, bf16[128,1024]{1,0:T(8,128)(2,1)}, u32[]{:S(2)}) copy-start(bf16[128,1024]{1,0:T(8,128)(2,1)} %param.6) | copy-start | bytes 786436
  193.0 67.3 %all-to-all-start = ((bf16[16,8,1024]{2,0,1:T(8,128)(2,1)}), bf16[16,8,1024]{2,0,1:T(8,128)(2,1)S(1)}, u32[]{:S(2)}, u32[]{:S(2)}) async-start(bf16[16,8,1024]{2,0,1:T(8,128)(2,1)} %bitcast.68), calls=%async_computation.2 | async-start | bytes 524288 | tf_op jit(solution)/shard_map/all_to_all | solution.py:142
  198.1 128.9 %all-gather.2.cloned.1.call-start = ((), (), s32[]{:S(2)}) async-start(), calls=%async_computation.5 | async-start | bytes 4718592 | tf_op jit(solution)/shard_map/all_gather | solution.py:161
  334.8 3.5 copy-start.2
  338.3 2.0 copy-start.8
  340.3 2.1 copy-start.6
  346.7 4.5 %copy-start.1 = (bf16[896,1024]{1,0:T(8,128)(2,1)S(1)}, bf16[896,1024]{1,0:T(8,128)(2,1)}, u32[]{:S(2)}) copy-start(bf16[896,1024]{1,0:T(8,128)(2,1)} %param.8) | copy-start | bytes 5505028
Sparse Core Ops, SparseCore 0:
  101.1 57.5 reduce-scatter.2
  191.4 57.5 reduce-scatter.4
  271.7 55.2 all-gather.1

commit v9 on v8

--- a/solution.py
+++ b/solution.py
@@ -120,6 +120,7 @@
     me_yh = lax.axis_index("yh")
     xt = hidden.reshape(blocks, n_parts, sub, ff_rows).swapaxes(0, 1)
     hp_parts, mlp_parts = [], []
+    pair_w = jnp.concatenate([w_down, swap_with_partner(w_down, 9, False)], axis=0)
     for part in range(n_parts):
         if part > 0:
             xt, _ = lax.optimization_barrier((xt, reduced))
@@ -130,9 +131,9 @@
             .reshape(n_c, n_z * n_yh * sub, ff_rows)
         )
         hp_parts.append(hp)
-        partial = jnp.dot(hp.reshape(-1, ff_rows), w_down, preferred_element_type=jnp.float32)
-        halves = partial.reshape((n_c, -1, d_cols))
-        reduced = halves[me_c] + swap_with_partner(halves, 2 * part + 1, True)
+        from_partner = swap_with_partner(hp, 2 * part + 1, True)
+        pair_rows = jnp.concatenate([hp[me_c], from_partner], axis=1)
+        reduced = jnp.dot(pair_rows, pair_w, preferred_element_type=jnp.float32)
         reduced_z = lax.psum_scatter(reduced, "z", scatter_dimension=0, tiled=True)
         by_yh = reduced_z.reshape((n_yh, -1, d_cols))
         mlp_parts.append(by_yh[me_yh] + swap_with_partner(by_yh, 6 + part, True, "yh"))

time: 359 us -> 349 us (0.972)
  other arithmetic: 19 us -> 5.41 us
  local copies, waits for them, and re-layouts: 19.5 us -> 24.5 us
    add x2 -> x0, other arithmetic: 13.6 us -> none  [per_device(): reduced = halves[me_c] + swap_with_partner(halves, 2 * part + 1, True)]
    reshape x0 -> x2, local copies, waits for them, and re-layouts: none -> 8.52 us  [per_device(): got.reshape(n_yh, n_z, n_c, sub, ff_rows).transpose(2, 1, 0, 3, 4)]
    transpose x2 -> x0, local copies, waits for them, and re-layouts: 4.81 us -> none  [per_device(): hp = got.reshape(n_yh, n_z, n_c, sub, ff_rows).transpose(2, 1, 0, 3, 4).r...]
    squeeze x0 -> x2, local copies, waits for them, and re-layouts: none -> 3.6 us  [per_device(): pair_rows = jnp.concatenate([hp[me_c], from_partner], axis=1)]
    pallas_call x6 -> x7, Pallas kernels: 51 us -> 51.2 us  [swap_with_partner(): pl.pallas_call(functools.partial(swap_kernel, axis, halves), out_shape=ja...]
  transfers between devices with their start and end apart: 4 -> 4, of which waited for: 2 -> 2; matrix products, arithmetic and copies ran while one was open for 6% -> 5% of each run, Pallas kernels for 25% -> 26%
where the time goes in v9:
time: 349 us; the launch traced here: 347 us
  Pallas kernels  179 us (51%)
  waiting for transfers between devices  94.5 us (27%)
  local copies, waits for them, and re-layouts  24.5 us (7%)
  matrix products  24.3 us (7%)
  between operations  14 us (4%)
  other arithmetic  5.41 us (2%)
  starting transfers between devices  5.22 us (1%)
    pallas_call x2, Pallas kernels, gather_part(): pl.pallas_call(functools.partial(gather_kernel, 'shard', n, part), out_sh...  128 us
    all_gather x1, waiting for transfers between devices, per_device(): gathered = lax.all_gather(gathered, 'z', axis=0, tiled=True)  55.4 us
    pallas_call x7, Pallas kernels, swap_with_partner(): pl.pallas_call(functools.partial(swap_kernel, axis, halves), out_shape=ja...  51.2 us
    reduce_scatter x2, waiting for transfers between devices, per_device(): reduced_z = lax.psum_scatter(reduced, 'z', scatter_dimension=0, tiled=True)  39.1 us
    dot_general x2, matrix products, per_device(): reduced = jnp.dot(pair_rows, pair_w, preferred_element_type=jnp.float32)  13.4 us
    dot_general x4, matrix products, per_device(): lax.dot_general(lax.dynamic_index_in_dim(hp_parts[part], rows, keepdims=F...  10.9 us
    reshape x2, local copies, waits for them, and re-layouts, per_device(): got.reshape(n_yh, n_z, n_c, sub, ff_rows).transpose(2, 1, 0, 3, 4)  8.52 us
  transfers between devices with their start and end apart: 4, of which 2 were waited for; matrix products, arithmetic and copies ran while one was open for 5% of the time, Pallas kernels for 26%

profile of v9, /device:TPU:29, one launch (start us, length us, event | category | flops | bytes accessed | tf_op | source)
XLA Modules:
  0.0 347.3 jit_solution(17244293482811183553)
XLA Ops:
  7.2 0.0 reduce-scatter.3.cloned.1.call-start
  7.2 2.2 copy.22
  9.4 4.4 %shard_map.79 = bf16[896,1024]{1,0:T(8,128)(2,1)} custom-call(bf16[896,1024]{1,0:T(8,128)(2,1)} %x_ref.1), custom_call_target="tpu_custom_call" | custom-call | tf_op jit(solution)/shard_map/pallas_call | solution.py:101
  13.9 64.9 %shard_map.77 = bf16[8,4,64,896]{3,2,1,0:T(8,128)(2,1)} custom-call(bf16[2,4,64,896]{3,2,1,0:T(8,128)(2,1)} %bitcast.66), custom_call_target="tpu_custom_call" | custom-call | bytes 7340032 | tf_op jit(solution)/shard_map/pallas_call | solution.py:66
  78.7 0.8 slice_dynamic-update-slice_fusion
  79.6 4.3 %copy.16 = bf16[2,8,2,64,896]{4,3,0,1,2:T(8,128)(2,1)} copy(bf16[2,8,2,64,896]{4,3,2,1,0:T(8,128)(2,1)} %bitcast.64) | data formatting | bytes 7340032 | tf_op jit(solution)/shard_map/reshape | solution.py:129
  83.8 5.0 %shard_map.78 = bf16[1024,896]{1,0:T(8,128)(2,1)} custom-call(bf16[2,1024,896]{2,1,0:T(8,128)(2,1)} %bitcast.56), custom_call_target="tpu_custom_call" | custom-call | tf_op jit(solution)/shard_map/pallas_call | solution.py:101
  88.9 1.8 dynamic-slice_bitcast_fusion.1
  90.7 1.3 copy-done.9
  92.0 5.9 %fusion = f32[1024,1024]{1,0:T(8,128)} fusion(bf16[1024,896]{1,0:T(8,128)(2,1)S(1)} %copy-done.11, bf16[1024,896]{1,0:T(8,128)(2,1)S(1)} %dynamic-slice_bitcast_fusion.1, bf16[896,1024]{1,0:T(8,128)(2,1)S(1)} %copy-done.7, bf16[896,1024]{1,0:T(8,128)(2,1)S(1)} %copy-done.5), kind=kOutput, calls=%fused_computation | convolution fusion | flops 3772776448 | bytes 11534336 | tf_op jit(solution)/shard_map/dot_general | solution.py:136
  97.9 0.0 reduce-scatter.3.cloned.1.call-update
  97.9 0.0 reduce-scatter.5.cloned.1.call-start
  98.0 63.3 %shard_map.81 = bf16[8,4,64,896]{3,2,1,0:T(8,128)(2,1)} custom-call(bf16[2,4,64,896]{3,2,1,0:T(8,128)(2,1)} %bitcast.67), custom_call_target="tpu_custom_call" | custom-call | bytes 7340032 | tf_op jit(solution)/shard_map/pallas_call | solution.py:66
  161.3 0.8 slice_dynamic-update-slice_fusion.1
  162.1 4.3 %copy.17 = bf16[2,8,2,64,896]{4,3,0,1,2:T(8,128)(2,1)} copy(bf16[2,8,2,64,896]{4,3,2,1,0:T(8,128)(2,1)} %bitcast.65) | data formatting | bytes 7340032 | tf_op jit(solution)/shard_map/reshape | solution.py:129
  166.4 5.0 %shard_map.82 = bf16[1024,896]{1,0:T(8,128)(2,1)} custom-call(bf16[2,1024,896]{2,1,0:T(8,128)(2,1)} %bitcast.59), custom_call_target="tpu_custom_call" | custom-call | tf_op jit(solution)/shard_map/pallas_call | solution.py:101
  171.4 0.0 copy-start.6
  171.4 1.8 dynamic-slice_bitcast_fusion
  173.2 0.2 copy-done.6
  173.5 0.6 copy-done.8
  174.0 7.5 %fusion.4 = f32[1024,1024]{1,0:T(8,128)} fusion(bf16[1024,896]{1,0:T(8,128)(2,1)} %shard_map.82, bf16[1024,896]{1,0:T(8,128)(2,1)S(1)} %dynamic-slice_bitcast_fusion, bf16[896,1024]{1,0:T(8,128)(2,1)S(1)} %copy-done.8, bf16[896,1024]{1,0:T(8,128)(2,1)S(1)} %copy-done.6), kind=kOutput, calls=%fused_computation.5 | convolution fusion | flops 3772776448 | bytes 11534336 | tf_op jit(solution)/shard_map/dot_general | solution.py:136
  181.5 0.0 reduce-scatter.5.cloned.1.call-update
  181.5 0.9 copy-done.12
  182.4 0.7 copy.23
  183.1 5.1 %all-to-all-start = ((bf16[16,8,1024]{2,0,1:T(8,128)(2,1)}), bf16[16,8,1024]{2,0,1:T(8,128)(2,1)S(1)}, u32[]{:S(2)}, u32[]{:S(2)}) async-start(bf16[16,8,1024]{2,0,1:T(8,128)(2,1)} %bitcast.55), calls=%async_computation.2 | async-start | bytes 524288 | tf_op jit(solution)/shard_map/all_to_all | solution.py:143
  188.3 0.0 all-gather.2.cloned.1.call-start
  188.3 0.1 select_reduce_fusion
  188.4 0.0 reduce-scatter.3.cloned.1.call-done
  188.5 11.7 %shard_map.80 = f32[64,1024]{1,0:T(8,128)} custom-call(f32[2,64,1024]{2,1,0:T(8,128)} %bitcast.74), custom_call_target="tpu_custom_call" | custom-call | tf_op jit(solution)/shard_map/pallas_call | solution.py:101
  200.1 39.0 %reduce-scatter.5.cloned.1.call-done = f32[128,1024]{1,0:T(8,128)} async-done(((f32[1024,1024]{1,0:T(8,128)}), f32[128,1024]{1,0:T(8,128)}) %reduce-scatter.5.cloned.1.call-update) | async-done | bytes 524304 | tf_op jit(solution)/shard_map/reduce_scatter | solution.py:137
  239.2 9.1 %shard_map.83 = f32[64,1024]{1,0:T(8,128)} custom-call(f32[2,64,1024]{2,1,0:T(8,128)} %bitcast.76), custom_call_target="tpu_custom_call" | custom-call | tf_op jit(solution)/shard_map/pallas_call | solution.py:101
  248.3 1.1 bitcast_add_fusion.1
  249.3 1.1 bitcast_add_fusion
  250.4 1.0 fusion.17
  251.4 8.1 %shard_map.84 = bf16[128,1024]{1,0:T(8,128)(2,1)} custom-call(bf16[128,1024]{1,0:T(8,128)(2,1)} %get-tuple-element.8.x_ref), custom_call_target="tpu_custom_call" | custom-call | tf_op jit(solution)/shard_map/pallas_call | solution.py:101
  259.5 2.2 maximum_select_fusion
  261.7 0.0 all-gather.2.cloned.1.call-update
  261.8 55.4 %all-gather.2.cloned.1.call-done.x_ref = bf16[2048,1024]{1,0:T(8,128)(2,1)} async-done(((bf16[256,1024]{1,0:T(8,128)(2,1)}), bf16[2048,1024]{1,0:T(8,128)(2,1)}) %all-gather.2.cloned.1.call-update) | async-done | bytes 4194320 | tf_op jit(solution)/shard_map/all_gather | solution.py:162
  317.1 7.8 %shard_map.85 = bf16[2048,1024]{1,0:T(8,128)(2,1)} custom-call(bf16[2048,1024]{1,0:T(8,128)(2,1)} %all-gather.2.cloned.1.call-done.x_ref), custom_call_target="tpu_custom_call" | custom-call | tf_op jit(solution)/shard_map/pallas_call | solution.py:101
  325.0 2.9 fusion.24
  327.9 0.4 copy-done
  328.3 2.1 fusion.10
  330.4 2.1 fusion.8
  332.6 0.0 copy-done.2
  332.6 0.7 fusion.23
  333.3 0.8 copy-done.10
  334.1 2.1 fusion.25
  336.2 4.5 %add_add_fusion = f32[896,1024]{1,0:T(8,128)} fusion(f32[896,1024]{1,0:T(8,128)S(1)} %fusion.8, f32[896,1024]{1,0:T(8,128)S(1)} %fusion.25, f32[896,1024]{1,0:T(8,128)S(1)} %fusion.10, bf16[1024,896]{1,0:T(8,128)(2,1)S(1)} %dynamic-slice_bitcast_fusion, bf16[1024,1024]{1,0:T(8,128)(2,1)S(1)} %bitcast.70), kind=kOutput, calls=%fused_computation.9 | convolution fusion | flops 1881800704 | bytes 18612224 | tf_op jit(solution)/shard_map/dot_general | solution.py:169
  (29 shorter events, 0.1 us)
Async XLA Ops:
  7.2 181.3 %reduce-scatter.3.cloned.1.call-start = ((), (), s32[]{:S(2)}) async-start(), calls=%async_computation.3 | async-start | bytes 4718592 | tf_op jit(solution)/shard_map/reduce_scatter | solution.py:137
  9.4 69.3 %copy-start.3 = (bf16[4,2,64,896]{3,2,0,1:T(8,128)(2,1)S(1)}, bf16[4,2,64,896]{3,2,0,1:T(8,128)(2,1)}, u32[]{:S(2)}) copy-start(bf16[4,2,64,896]{3,2,0,1:T(8,128)(2,1)} %copy.22) | copy-start | bytes 2752516
  83.8 8.2 %copy-start.5 = (bf16[896,1024]{1,0:T(8,128)(2,1)S(1)}, bf16[896,1024]{1,0:T(8,128)(2,1)}, u32[]{:S(2)}) copy-start(bf16[896,1024]{1,0:T(8,128)(2,1)} %x_ref.1) | copy-start | bytes 5505028
  88.9 3.1 copy-start.7
  88.9 3.1 copy-start.11
  90.7 1.3 copy-start.9
  97.9 63.3 %copy-start.4 = (bf16[4,2,64,896]{3,2,0,1:T(8,128)(2,1)S(1)}, bf16[4,2,64,896]{3,2,0,1:T(8,128)(2,1)}, u32[]{:S(2)}) copy-start(bf16[4,2,64,896]{3,2,0,1:T(8,128)(2,1)} %copy.22) | copy-start | bytes 2752516
  97.9 141.2 %reduce-scatter.5.cloned.1.call-start = ((), (), s32[]{:S(2)}) async-start(), calls=%async_computation.4 | async-start | bytes 4718592 | tf_op jit(solution)/shard_map/reduce_scatter | solution.py:137
  171.4 2.1 copy-start.6
  171.4 2.6 copy-start.8
  181.5 0.9 copy-start.12
  181.5 6.8 %copy-start.14 = (bf16[1024]{0:T(1024)(128)(2,1)S(1)}, bf16[1024]{0:T(1024)(128)(2,1)}, u32[]{:S(2)}) copy-start(bf16[1024]{0:T(1024)(128)(2,1)} %param.10) | copy-start | bytes 6148
  181.5 6.9 %copy-start.15 = (s32[16]{0:T(128)S(1)}, s32[16]{0:T(128)}, u32[]{:S(2)}) copy-start(s32[16]{0:T(128)} %param.11) | copy-start | bytes 196
  181.5 68.9 %copy-start.13 = (bf16[128,1024]{1,0:T(8,128)(2,1)S(1)}, bf16[128,1024]{1,0:T(8,128)(2,1)}, u32[]{:S(2)}) copy-start(bf16[128,1024]{1,0:T(8,128)(2,1)} %param.6) | copy-start | bytes 786436
  183.1 67.2 %all-to-all-start = ((bf16[16,8,1024]{2,0,1:T(8,128)(2,1)}), bf16[16,8,1024]{2,0,1:T(8,128)(2,1)S(1)}, u32[]{:S(2)}, u32[]{:S(2)}) async-start(bf16[16,8,1024]{2,0,1:T(8,128)(2,1)} %bitcast.55), calls=%async_computation.2 | async-start | bytes 524288 | tf_op jit(solution)/shard_map/all_to_all | solution.py:143
  188.3 128.9 %all-gather.2.cloned.1.call-start = ((), (), s32[]{:S(2)}) async-start(), calls=%async_computation.5 | async-start | bytes 4718592 | tf_op jit(solution)/shard_map/all_gather | solution.py:162
  325.0 3.3 copy-start
  328.3 2.1 copy-start.1
  330.4 2.2 copy-start.2
  332.6 1.5 copy-start.10
Sparse Core Ops, SparseCore 0:
  98.1 57.5 reduce-scatter.2
  181.6 57.5 reduce-scatter.4
  261.9 55.2 all-gather.1

commit v10 on v9

--- a/solution.py
+++ b/solution.py
@@ -106,6 +106,64 @@
         scratch_shapes=[pltpu.SemaphoreType.DMA(()), pltpu.SemaphoreType.DMA(())],
         compiler_params=pltpu.CompilerParams(collective_id=collective_id, has_side_effects=True),
     )(x)
+
+
+def ring_gather_kernel(axis, n, x_ref, out_ref, send_sem, recv_sem):
+    me = lax.axis_index(axis)
+    right, left = lax.rem(me + 1, n), lax.rem(me + n - 1, n)
+
+    barrier = pltpu.get_barrier_semaphore()
+    for neighbour in (left, right):
+        pl.semaphore_signal(barrier, inc=1, device_id=device_on(axis, neighbour), device_id_type=MESH)
+    pl.semaphore_wait(barrier, 2)
+
+    def arrival(slot):
+        return pltpu.make_async_remote_copy(
+            src_ref=x_ref,
+            dst_ref=out_ref.at[slot],
+            send_sem=send_sem.at[0, 0],
+            recv_sem=recv_sem.at[slot],
+            device_id=device_on(axis, left),
+            device_id_type=MESH,
+        )
+
+    copies = []
+    steps = (n // 2, (n - 1) // 2)
+    for k in range(max(steps)):
+        for ring, (sign, target) in enumerate(((-1, right), (1, left))):
+            if k >= steps[ring]:
+                continue
+            slot = lax.rem(me + sign * k + n, n)
+            if k > 0:
+                arrival(slot).wait_recv()
+            copy = pltpu.make_async_remote_copy(
+                src_ref=x_ref if k == 0 else out_ref.at[slot],
+                dst_ref=out_ref.at[slot],
+                send_sem=send_sem.at[ring, k],
+                recv_sem=recv_sem.at[slot],
+                device_id=device_on(axis, target),
+                device_id_type=MESH,
+            )
+            copy.start()
+            copies.append(copy)
+    arrival(lax.rem(me - steps[0] + n, n)).wait_recv()
+    arrival(lax.rem(me + steps[1], n)).wait_recv()
+    for copy in copies:
+        copy.wait_send()
+
+
+def ring_gather(x, axis, collective_id):
+    n = lax.axis_size(axis)
+    received = pl.pallas_call(
+        functools.partial(ring_gather_kernel, axis, n),
+        out_shape=jax.ShapeDtypeStruct((n,) + x.shape, x.dtype),
+        in_specs=[pl.BlockSpec(memory_space=pl.ANY)],
+        out_specs=pl.BlockSpec(memory_space=pl.ANY),
+        scratch_shapes=[pltpu.SemaphoreType.DMA((2, n // 2)), pltpu.SemaphoreType.DMA((n,))],
+        compiler_params=pltpu.CompilerParams(collective_id=collective_id, has_side_effects=True),
+    )(x)
+    whole = lax.dynamic_update_index_in_dim(received, x, lax.axis_index(axis), 0)
+    return whole.reshape((n * x.shape[0],) + x.shape[1:])
 
 
 def per_device(resid_in, hidden, w_down, frozen, steer, forget_flags):
@@ -159,7 +217,7 @@
         jnp.concatenate([slopes, other_yh], axis=0),
         jnp.concatenate([other_yh, slopes], axis=0),
     )
-    gathered = lax.all_gather(gathered, "z", axis=0, tiled=True)
+    gathered = ring_gather(gathered, "z", 10)
     partner_slopes = swap_with_partner(gathered, 2 * n_parts + 1, False)
     contract = (((0,), (0,)), ((), ()))
     grad_down = None

time: 349 us -> 344 us (0.986)
  waiting for transfers between devices: 94.5 us -> 39.1 us
  Pallas kernels: 179 us -> 228 us
    all_gather x1 -> x0, waiting for transfers between devices: 55.4 us -> none  [per_device(): gathered = lax.all_gather(gathered, 'z', axis=0, tiled=True)]
    pallas_call x0 -> x1, Pallas kernels: none -> 44.2 us  [ring_gather(): pl.pallas_call(functools.partial(ring_gather_kernel, axis, n), out_shape=...]
    pallas_call x7, Pallas kernels: 51.2 us -> 56 us  [swap_with_partner(): pl.pallas_call(functools.partial(swap_kernel, axis, halves), out_shape=ja...]
  transfers between devices with their start and end apart: 4 -> 3, of which waited for: 2 -> 1; matrix products, arithmetic and copies ran while one was open for 5% -> 5% of each run, Pallas kernels for 26% -> 26%
where the time goes in v10:
time: 344 us; the launch traced here: 342 us
  Pallas kernels  228 us (66%)
  waiting for transfers between devices  39.1 us (11%)
  local copies, waits for them, and re-layouts  24.5 us (7%)
  matrix products  24.2 us (7%)
  between operations  14.3 us (4%)
  other arithmetic  6.41 us (2%)
  starting transfers between devices  5.22 us (2%)
    pallas_call x2, Pallas kernels, gather_part(): pl.pallas_call(functools.partial(gather_kernel, 'shard', n, part), out_sh...  128 us
    pallas_call x7, Pallas kernels, swap_with_partner(): pl.pallas_call(functools.partial(swap_kernel, axis, halves), out_shape=ja...  56 us
    pallas_call x1, Pallas kernels, ring_gather(): pl.pallas_call(functools.partial(ring_gather_kernel, axis, n), out_shape=...  44.2 us
    reduce_scatter x2, waiting for transfers between devices, per_device(): reduced_z = lax.psum_scatter(reduced, 'z', scatter_dimension=0, tiled=True)  39.1 us
    dot_general x2, matrix products, per_device(): reduced = jnp.dot(pair_rows, pair_w, preferred_element_type=jnp.float32)  13.4 us
    dot_general x4, matrix products, per_device(): lax.dot_general(lax.dynamic_index_in_dim(hp_parts[part], rows, keepdims=F...  10.9 us
    reshape x2, local copies, waits for them, and re-layouts, per_device(): got.reshape(n_yh, n_z, n_c, sub, ff_rows).transpose(2, 1, 0, 3, 4)  8.51 us
  transfers between devices with their start and end apart: 3, of which 1 were waited for; matrix products, arithmetic and copies ran while one was open for 5% of the time, Pallas kernels for 26%

profile of v10, /device:TPU:29, one launch (start us, length us, event | category | flops | bytes accessed | tf_op | source)
XLA Modules:
  0.0 342.2 jit_solution(15825161601609955063)
XLA Ops:
  7.2 0.0 reduce-scatter.3.cloned.1.call-start
  7.2 2.2 copy.22
  9.4 4.4 %shard_map.79 = bf16[896,1024]{1,0:T(8,128)(2,1)} custom-call(bf16[896,1024]{1,0:T(8,128)(2,1)} %x_ref.1), custom_call_target="tpu_custom_call" | custom-call | tf_op jit(solution)/shard_map/pallas_call | solution.py:101
  13.9 64.9 %shard_map.77 = bf16[8,4,64,896]{3,2,1,0:T(8,128)(2,1)} custom-call(bf16[2,4,64,896]{3,2,1,0:T(8,128)(2,1)} %bitcast.70), custom_call_target="tpu_custom_call" | custom-call | bytes 7340032 | tf_op jit(solution)/shard_map/pallas_call | solution.py:66
  78.7 0.8 slice_dynamic-update-slice_fusion
  79.6 4.2 %copy.16 = bf16[2,8,2,64,896]{4,3,0,1,2:T(8,128)(2,1)} copy(bf16[2,8,2,64,896]{4,3,2,1,0:T(8,128)(2,1)} %bitcast.68) | data formatting | bytes 7340032 | tf_op jit(solution)/shard_map/reshape | solution.py:187
  83.8 5.0 %shard_map.78 = bf16[1024,896]{1,0:T(8,128)(2,1)} custom-call(bf16[2,1024,896]{2,1,0:T(8,128)(2,1)} %bitcast.61), custom_call_target="tpu_custom_call" | custom-call | tf_op jit(solution)/shard_map/pallas_call | solution.py:101
  88.9 1.8 dynamic-slice_bitcast_fusion.1
  90.7 1.3 copy-done.11
  92.0 5.9 %fusion = f32[1024,1024]{1,0:T(8,128)} fusion(bf16[1024,896]{1,0:T(8,128)(2,1)S(1)} %copy-done.13, bf16[1024,896]{1,0:T(8,128)(2,1)S(1)} %dynamic-slice_bitcast_fusion.1, bf16[896,1024]{1,0:T(8,128)(2,1)S(1)} %copy-done.9, bf16[896,1024]{1,0:T(8,128)(2,1)S(1)} %copy-done.7), kind=kOutput, calls=%fused_computation | convolution fusion | flops 3772776448 | bytes 11534336 | tf_op jit(solution)/shard_map/dot_general | solution.py:194
  97.9 0.0 reduce-scatter.3.cloned.1.call-update
  97.9 0.0 reduce-scatter.5.cloned.1.call-start
  98.0 63.3 %shard_map.81 = bf16[8,4,64,896]{3,2,1,0:T(8,128)(2,1)} custom-call(bf16[2,4,64,896]{3,2,1,0:T(8,128)(2,1)} %bitcast.71), custom_call_target="tpu_custom_call" | custom-call | bytes 7340032 | tf_op jit(solution)/shard_map/pallas_call | solution.py:66
  161.3 0.8 slice_dynamic-update-slice_fusion.1
  162.1 4.3 %copy.17 = bf16[2,8,2,64,896]{4,3,0,1,2:T(8,128)(2,1)} copy(bf16[2,8,2,64,896]{4,3,2,1,0:T(8,128)(2,1)} %bitcast.69) | data formatting | bytes 7340032 | tf_op jit(solution)/shard_map/reshape | solution.py:187
  166.4 5.0 %shard_map.82 = bf16[1024,896]{1,0:T(8,128)(2,1)} custom-call(bf16[2,1024,896]{2,1,0:T(8,128)(2,1)} %bitcast.64), custom_call_target="tpu_custom_call" | custom-call | tf_op jit(solution)/shard_map/pallas_call | solution.py:101
  171.4 0.0 copy-start.8
  171.4 1.8 dynamic-slice_bitcast_fusion
  173.2 0.2 copy-done.8
  173.5 0.6 copy-done.10
  174.0 7.5 %fusion.4 = f32[1024,1024]{1,0:T(8,128)} fusion(bf16[1024,896]{1,0:T(8,128)(2,1)} %shard_map.82, bf16[1024,896]{1,0:T(8,128)(2,1)S(1)} %dynamic-slice_bitcast_fusion, bf16[896,1024]{1,0:T(8,128)(2,1)S(1)} %copy-done.10, bf16[896,1024]{1,0:T(8,128)(2,1)S(1)} %copy-done.8), kind=kOutput, calls=%fused_computation.5 | convolution fusion | flops 3772776448 | bytes 11534336 | tf_op jit(solution)/shard_map/dot_general | solution.py:194
  181.5 0.0 reduce-scatter.5.cloned.1.call-update
  181.5 0.9 copy-done.14
  182.4 0.7 copy.23
  183.1 5.1 %all-to-all-start = ((bf16[16,8,1024]{2,0,1:T(8,128)(2,1)}), bf16[16,8,1024]{2,0,1:T(8,128)(2,1)S(1)}, u32[]{:S(2)}, u32[]{:S(2)}) async-start(bf16[16,8,1024]{2,0,1:T(8,128)(2,1)} %bitcast.58), calls=%async_computation.2 | async-start | bytes 524288 | tf_op jit(solution)/shard_map/all_to_all | solution.py:201
  188.3 0.1 select_reduce_fusion
  188.4 0.0 reduce-scatter.3.cloned.1.call-done
  188.5 11.7 %shard_map.80 = f32[64,1024]{1,0:T(8,128)} custom-call(f32[2,64,1024]{2,1,0:T(8,128)} %bitcast.80), custom_call_target="tpu_custom_call" | custom-call | tf_op jit(solution)/shard_map/pallas_call | solution.py:101
  200.1 39.0 %reduce-scatter.5.cloned.1.call-done = f32[128,1024]{1,0:T(8,128)} async-done(((f32[1024,1024]{1,0:T(8,128)}), f32[128,1024]{1,0:T(8,128)}) %reduce-scatter.5.cloned.1.call-update) | async-done | bytes 524304 | tf_op jit(solution)/shard_map/reduce_scatter | solution.py:195
  239.2 9.1 %shard_map.83 = f32[64,1024]{1,0:T(8,128)} custom-call(f32[2,64,1024]{2,1,0:T(8,128)} %bitcast.82), custom_call_target="tpu_custom_call" | custom-call | tf_op jit(solution)/shard_map/pallas_call | solution.py:101
  248.3 1.1 bitcast_add_fusion.1
  249.3 1.1 bitcast_add_fusion
  250.4 0.0 all-to-all-done
  250.4 1.0 fusion.18
  251.4 8.1 %shard_map.84 = bf16[128,1024]{1,0:T(8,128)(2,1)} custom-call(bf16[128,1024]{1,0:T(8,128)(2,1)} %get-tuple-element.8.x_ref), custom_call_target="tpu_custom_call" | custom-call | tf_op jit(solution)/shard_map/pallas_call | solution.py:101
  259.6 2.2 maximum_select_fusion.x_ref
  261.8 44.2 %shard_map.85 = bf16[8,256,1024]{2,1,0:T(8,128)(2,1)} custom-call(bf16[256,1024]{1,0:T(8,128)(2,1)} %maximum_select_fusion.x_ref), custom_call_target="tpu_custom_call" | custom-call | tf_op jit(solution)/shard_map/pallas_call | solution.py:157
  306.1 0.9 fusion.14
  307.0 12.7 %shard_map.86 = bf16[2048,1024]{1,0:T(8,128)(2,1)} custom-call(bf16[2048,1024]{1,0:T(8,128)(2,1)} %bitcast.59), custom_call_target="tpu_custom_call" | custom-call | tf_op jit(solution)/shard_map/pallas_call | solution.py:101
  319.7 2.9 fusion.25
  322.6 0.4 copy-done.1
  323.0 2.1 fusion.10
  325.1 2.1 fusion.8
  327.2 0.0 copy-done
  327.3 0.7 fusion.24
  328.0 0.8 copy-done.12
  328.8 2.1 fusion.26
  330.9 4.5 %add_add_fusion = f32[896,1024]{1,0:T(8,128)} fusion(f32[896,1024]{1,0:T(8,128)S(1)} %fusion.8, f32[896,1024]{1,0:T(8,128)S(1)} %fusion.26, f32[896,1024]{1,0:T(8,128)S(1)} %fusion.10, bf16[1024,896]{1,0:T(8,128)(2,1)S(1)} %dynamic-slice_bitcast_fusion, bf16[1024,1024]{1,0:T(8,128)(2,1)S(1)} %bitcast.74), kind=kOutput, calls=%fused_computation.9 | convolution fusion | flops 1881800704 | bytes 18612224 | tf_op jit(solution)/shard_map/dot_general | solution.py:227
  (32 shorter events, 0.1 us)
Async XLA Ops:
  7.2 181.3 %reduce-scatter.3.cloned.1.call-start = ((), (), s32[]{:S(2)}) async-start(), calls=%async_computation.3 | async-start | bytes 4718592 | tf_op jit(solution)/shard_map/reduce_scatter | solution.py:195
  9.4 69.3 %copy-start.3 = (bf16[4,2,64,896]{3,2,0,1:T(8,128)(2,1)S(1)}, bf16[4,2,64,896]{3,2,0,1:T(8,128)(2,1)}, u32[]{:S(2)}) copy-start(bf16[4,2,64,896]{3,2,0,1:T(8,128)(2,1)} %copy.22) | copy-start | bytes 2752516
  83.8 8.2 %copy-start.7 = (bf16[896,1024]{1,0:T(8,128)(2,1)S(1)}, bf16[896,1024]{1,0:T(8,128)(2,1)}, u32[]{:S(2)}) copy-start(bf16[896,1024]{1,0:T(8,128)(2,1)} %x_ref.1) | copy-start | bytes 5505028
  88.9 3.1 copy-start.9
  88.9 3.1 copy-start.13
  90.7 1.3 copy-start.11
  97.9 63.3 %copy-start.4 = (bf16[4,2,64,896]{3,2,0,1:T(8,128)(2,1)S(1)}, bf16[4,2,64,896]{3,2,0,1:T(8,128)(2,1)}, u32[]{:S(2)}) copy-start(bf16[4,2,64,896]{3,2,0,1:T(8,128)(2,1)} %copy.22) | copy-start | bytes 2752516
  97.9 141.2 %reduce-scatter.5.cloned.1.call-start = ((), (), s32[]{:S(2)}) async-start(), calls=%async_computation.4 | async-start | bytes 4718592 | tf_op jit(solution)/shard_map/reduce_scatter | solution.py:195
  171.4 2.1 copy-start.8
  171.4 2.6 copy-start.10
  181.5 0.9 copy-start.14
  181.5 6.8 %copy-start.16 = (bf16[1024]{0:T(1024)(128)(2,1)S(1)}, bf16[1024]{0:T(1024)(128)(2,1)}, u32[]{:S(2)}) copy-start(bf16[1024]{0:T(1024)(128)(2,1)} %param.10) | copy-start | bytes 6148
  181.5 6.8 %copy-start.17 = (s32[16]{0:T(128)S(1)}, s32[16]{0:T(128)}, u32[]{:S(2)}) copy-start(s32[16]{0:T(128)} %param.11) | copy-start | bytes 196
  181.5 68.9 %copy-start.15 = (bf16[128,1024]{1,0:T(8,128)(2,1)S(1)}, bf16[128,1024]{1,0:T(8,128)(2,1)}, u32[]{:S(2)}) copy-start(bf16[128,1024]{1,0:T(8,128)(2,1)} %param.6) | copy-start | bytes 786436
  183.1 67.2 %all-to-all-start = ((bf16[16,8,1024]{2,0,1:T(8,128)(2,1)}), bf16[16,8,1024]{2,0,1:T(8,128)(2,1)S(1)}, u32[]{:S(2)}, u32[]{:S(2)}) async-start(bf16[16,8,1024]{2,0,1:T(8,128)(2,1)} %bitcast.58), calls=%async_computation.2 | async-start | bytes 524288 | tf_op jit(solution)/shard_map/all_to_all | solution.py:201
  251.4 54.6 %copy-start.5 = (bf16[128,1024]{1,0:T(8,128)(2,1)S(1)}, bf16[128,1024]{1,0:T(8,128)(2,1)}, u32[]{:S(2)}) copy-start(bf16[128,1024]{1,0:T(8,128)(2,1)} %get-tuple-element.8.x_ref) | copy-start | bytes 786436
  259.6 46.5 %copy-start.6 = (bf16[128,1024]{1,0:T(8,128)(2,1)S(1)}, bf16[128,1024]{1,0:T(8,128)(2,1)}, u32[]{:S(2)}) copy-start(bf16[128,1024]{1,0:T(8,128)(2,1)} %shard_map.84) | copy-start | bytes 786436
  319.7 3.3 copy-start.1
  323.0 2.1 copy-start.2
  325.1 2.2 copy-start
  327.3 1.5 copy-start.12
Sparse Core Ops, SparseCore 0:
  98.1 57.5 reduce-scatter.2
  181.6 57.5 reduce-scatter.4

commit v11 on v10

--- a/solution.py
+++ b/solution.py
@@ -60,12 +60,52 @@
         arrival.wait_recv()
 
 
-def gather_part(xt, part, collective_id):
+def placed_gather_kernel(n, n_zhi, part, x_ref, out_ref, send_sem, recv_sem):
+    me = lax.axis_index("shard")
+
+    def where(j):
+        return out_ref.at[:, pl.ds(2 * lax.rem(j, n_zhi), 2), pl.ds(j // n_zhi, 1)]
+
+    barrier = pltpu.get_barrier_semaphore()
+    for off in range(1, n):
+        peer = lax.rem(me + off, n)
+        pl.semaphore_signal(barrier, inc=1, device_id=device_on("shard", peer), device_id_type=MESH)
+    pl.semaphore_wait(barrier, n - 1)
+
+    copies = []
+    for off in range(1, n):
+        peer = lax.rem(me + off, n)
+        copy = pltpu.make_async_remote_copy(
+            src_ref=x_ref.at[part],
+            dst_ref=where(me),
+            send_sem=send_sem.at[off - 1],
+            recv_sem=recv_sem.at[me],
+            device_id=device_on("shard", peer),
+            device_id_type=MESH,
+        )
+        copy.start()
+        copies.append(copy)
+    for copy in copies:
+        copy.wait_send()
+    for off in range(1, n):
+        src = lax.rem(me + n - off, n)
+        arrival = pltpu.make_async_remote_copy(
+            src_ref=x_ref.at[part],
+            dst_ref=where(src),
+            send_sem=send_sem.at[off - 1],
+            recv_sem=recv_sem.at[src],
+            device_id=device_on("shard", src),
+            device_id_type=MESH,
+        )
+        arrival.wait_recv()
+
+
+def gather_part(xt, part, collective_id, out_dims):
     n = lax.axis_size("shard")
-    block = xt.shape[1:]
+    n_zhi = out_dims[1] // 2
     received = pl.pallas_call(
-        functools.partial(gather_kernel, "shard", n, part),
-        out_shape=jax.ShapeDtypeStruct((n,) + block, xt.dtype),
+        functools.partial(placed_gather_kernel, n, n_zhi, part),
+        out_shape=jax.ShapeDtypeStruct(out_dims, xt.dtype),
         in_specs=[pl.BlockSpec(memory_space=pl.ANY)],
         out_specs=pl.BlockSpec(memory_space=pl.ANY),
         scratch_shapes=[pltpu.SemaphoreType.DMA((n - 1,)), pltpu.SemaphoreType.DMA((n,))],
@@ -74,7 +114,9 @@
             flops=0, bytes_accessed=2 * n * xt[part].nbytes, transcendentals=0
         ),
     )(xt)
-    return lax.dynamic_update_index_in_dim(received, xt[part], lax.axis_index("shard"), 0)
+    me = lax.axis_index("shard")
+    at = (0, 2 * lax.rem(me, n_zhi), me // n_zhi, 0, 0)
+    return lax.dynamic_update_slice(received, xt[part], at)
 
 
 def swap_kernel(axis, halves, x_ref, out_ref, send_sem, recv_sem):
@@ -176,18 +218,14 @@
     total_tokens = own_tokens * lax.axis_size("shard")
     me_c = lax.axis_index("core")
     me_yh = lax.axis_index("yh")
-    xt = hidden.reshape(blocks, n_parts, sub, ff_rows).swapaxes(0, 1)
+    xt = hidden.reshape(blocks // n_c, n_c, n_parts, 1, sub, ff_rows).transpose(2, 1, 0, 3, 4, 5)
     hp_parts, mlp_parts = [], []
     pair_w = jnp.concatenate([w_down, swap_with_partner(w_down, 9, False)], axis=0)
     for part in range(n_parts):
         if part > 0:
             xt, _ = lax.optimization_barrier((xt, reduced))
-        got = gather_part(xt, part, 2 * part)
-        hp = (
-            got.reshape(n_yh, n_z, n_c, sub, ff_rows)
-            .transpose(2, 1, 0, 3, 4)
-            .reshape(n_c, n_z * n_yh * sub, ff_rows)
-        )
+        got = gather_part(xt, part, 2 * part, (n_c, n_z, n_yh, sub, ff_rows))
+        hp = got.reshape(n_c, n_z * n_yh * sub, ff_rows)
         hp_parts.append(hp)
         from_partner = swap_with_partner(hp, 2 * part + 1, True)
         pair_rows = jnp.concatenate([hp[me_c], from_partner], axis=1)

time: 344 us -> 335 us (0.974)
  local copies, waits for them, and re-layouts: 24.5 us -> 16 us
    reshape x3 -> x1, local copies, waits for them, and re-layouts: 10.7 us -> 2.21 us  [per_device(): hidden.reshape(blocks // n_c, n_c, n_parts, 1, sub, ff_rows)]
  transfers between devices with their start and end apart: 3 -> 3, of which waited for: 1 -> 1; matrix products, arithmetic and copies ran while one was open for 5% -> 4% of each run, Pallas kernels for 26% -> 27%
where the time goes in v11:
time: 335 us; the launch traced here: 334 us
  Pallas kernels  228 us (68%)
  waiting for transfers between devices  39.1 us (12%)
  matrix products  24.3 us (7%)
  local copies, waits for them, and re-layouts  16 us (5%)
  between operations  14.4 us (4%)
  other arithmetic  6.41 us (2%)
  starting transfers between devices  5.22 us (2%)
    pallas_call x2, Pallas kernels, gather_part(): pl.pallas_call(functools.partial(placed_gather_kernel, n, n_zhi, part), o...  128 us
    pallas_call x7, Pallas kernels, swap_with_partner(): pl.pallas_call(functools.partial(swap_kernel, axis, halves), out_shape=ja...  56.3 us
    pallas_call x1, Pallas kernels, ring_gather(): pl.pallas_call(functools.partial(ring_gather_kernel, axis, n), out_shape=...  43.9 us
    reduce_scatter x2, waiting for transfers between devices, per_device(): reduced_z = lax.psum_scatter(reduced, 'z', scatter_dimension=0, tiled=True)  39.1 us
    dot_general x2, matrix products, per_device(): reduced = jnp.dot(pair_rows, pair_w, preferred_element_type=jnp.float32)  13.4 us
    dot_general x4, matrix products, per_device(): lax.dot_general(lax.dynamic_index_in_dim(hp_parts[part], rows, keepdims=F...  10.9 us
  transfers between devices with their start and end apart: 3, of which 1 were waited for; matrix products, arithmetic and copies ran while one was open for 4% of the time, Pallas kernels for 27%

profile of v11, /device:TPU:29, one launch (start us, length us, event | category | flops | bytes accessed | tf_op | source)
XLA Modules:
  0.0 333.7 jit_solution(8841452163751642378)
XLA Ops:
  7.2 0.0 reduce-scatter.3.cloned.1.call-start
  7.2 2.2 copy.22
  9.4 4.4 %shard_map.79 = bf16[896,1024]{1,0:T(8,128)(2,1)} custom-call(bf16[896,1024]{1,0:T(8,128)(2,1)} %x_ref.1), custom_call_target="tpu_custom_call" | custom-call | tf_op jit(solution)/shard_map/pallas_call | solution.py:143
  13.9 64.9 %shard_map.77 = bf16[2,8,2,64,896]{4,3,2,1,0:T(8,128)(2,1)} custom-call(bf16[2,2,2,1,64,896]{5,4,3,2,1,0:T(8,128)(2,1)} %bitcast.72), custom_call_target="tpu_custom_call" | custom-call | bytes 7340032 | tf_op jit(solution)/shard_map/pallas_call | solution.py:106
  78.8 0.8 fusion.19
  79.6 5.0 %shard_map.78 = bf16[1024,896]{1,0:T(8,128)(2,1)} custom-call(bf16[2,1024,896]{2,1,0:T(8,128)(2,1)} %bitcast.65), custom_call_target="tpu_custom_call" | custom-call | tf_op jit(solution)/shard_map/pallas_call | solution.py:143
  84.7 1.8 dynamic-slice_bitcast_fusion.1
  86.5 0.0 copy-start.11
  86.5 1.2 copy-done.11
  87.7 0.0 copy-done.7
  87.7 5.9 %fusion = f32[1024,1024]{1,0:T(8,128)} fusion(bf16[1024,896]{1,0:T(8,128)(2,1)S(1)} %copy-done.13, bf16[1024,896]{1,0:T(8,128)(2,1)S(1)} %dynamic-slice_bitcast_fusion.1, bf16[896,1024]{1,0:T(8,128)(2,1)S(1)} %copy-done.9, bf16[896,1024]{1,0:T(8,128)(2,1)S(1)} %copy-done.7), kind=kOutput, calls=%fused_computation | convolution fusion | flops 3772776448 | bytes 11534336 | tf_op jit(solution)/shard_map/dot_general | solution.py:232
  93.7 0.0 reduce-scatter.3.cloned.1.call-update
  93.7 0.0 reduce-scatter.5.cloned.1.call-start
  93.7 63.3 %shard_map.81 = bf16[2,8,2,64,896]{4,3,2,1,0:T(8,128)(2,1)} custom-call(bf16[2,2,2,1,64,896]{5,4,3,2,1,0:T(8,128)(2,1)} %bitcast.73), custom_call_target="tpu_custom_call" | custom-call | bytes 7340032 | tf_op jit(solution)/shard_map/pallas_call | solution.py:106
  157.0 0.9 bitcast_dynamic-update-slice_fusion
  157.9 5.0 %shard_map.82 = bf16[1024,896]{1,0:T(8,128)(2,1)} custom-call(bf16[2,1024,896]{2,1,0:T(8,128)(2,1)} %bitcast.68), custom_call_target="tpu_custom_call" | custom-call | tf_op jit(solution)/shard_map/pallas_call | solution.py:143
  162.9 0.0 copy-start.8
  162.9 1.8 dynamic-slice_bitcast_fusion
  164.7 0.2 copy-done.8
  165.0 0.6 copy-done.10
  165.5 7.5 %fusion.4 = f32[1024,1024]{1,0:T(8,128)} fusion(bf16[1024,896]{1,0:T(8,128)(2,1)} %shard_map.82, bf16[1024,896]{1,0:T(8,128)(2,1)S(1)} %dynamic-slice_bitcast_fusion, bf16[896,1024]{1,0:T(8,128)(2,1)S(1)} %copy-done.10, bf16[896,1024]{1,0:T(8,128)(2,1)S(1)} %copy-done.8), kind=kOutput, calls=%fused_computation.5 | convolution fusion | flops 3772776448 | bytes 11534336 | tf_op jit(solution)/shard_map/dot_general | solution.py:232
  173.0 0.0 reduce-scatter.5.cloned.1.call-update
  173.0 0.9 copy-done.14
  173.9 0.7 copy.23
  174.6 5.1 %all-to-all-start = ((bf16[16,8,1024]{2,0,1:T(8,128)(2,1)}), bf16[16,8,1024]{2,0,1:T(8,128)(2,1)S(1)}, u32[]{:S(2)}, u32[]{:S(2)}) async-start(bf16[16,8,1024]{2,0,1:T(8,128)(2,1)} %bitcast.62), calls=%async_computation.2 | async-start | bytes 524288 | tf_op jit(solution)/shard_map/all_to_all | solution.py:239
  179.8 0.1 select_reduce_fusion
  179.9 0.0 reduce-scatter.3.cloned.1.call-done
  179.9 11.7 %shard_map.80 = f32[64,1024]{1,0:T(8,128)} custom-call(f32[2,64,1024]{2,1,0:T(8,128)} %bitcast.82), custom_call_target="tpu_custom_call" | custom-call | tf_op jit(solution)/shard_map/pallas_call | solution.py:143
  191.6 39.0 %reduce-scatter.5.cloned.1.call-done = f32[128,1024]{1,0:T(8,128)} async-done(((f32[1024,1024]{1,0:T(8,128)}), f32[128,1024]{1,0:T(8,128)}) %reduce-scatter.5.cloned.1.call-update) | async-done | bytes 524304 | tf_op jit(solution)/shard_map/reduce_scatter | solution.py:233
  230.7 9.1 %shard_map.83 = f32[64,1024]{1,0:T(8,128)} custom-call(f32[2,64,1024]{2,1,0:T(8,128)} %bitcast.84), custom_call_target="tpu_custom_call" | custom-call | tf_op jit(solution)/shard_map/pallas_call | solution.py:143
  239.7 1.1 bitcast_add_fusion.1
  240.8 1.1 bitcast_add_fusion
  241.9 0.0 all-to-all-done
  241.9 1.0 fusion.18
  242.9 8.1 %shard_map.84 = bf16[128,1024]{1,0:T(8,128)(2,1)} custom-call(bf16[128,1024]{1,0:T(8,128)(2,1)} %get-tuple-element.8.x_ref), custom_call_target="tpu_custom_call" | custom-call | tf_op jit(solution)/shard_map/pallas_call | solution.py:143
  251.1 2.2 maximum_select_fusion.x_ref
  253.3 43.9 %shard_map.85 = bf16[8,256,1024]{2,1,0:T(8,128)(2,1)} custom-call(bf16[256,1024]{1,0:T(8,128)(2,1)} %maximum_select_fusion.x_ref), custom_call_target="tpu_custom_call" | custom-call | tf_op jit(solution)/shard_map/pallas_call | solution.py:199
  297.3 0.9 fusion.14
  298.2 12.9 %shard_map.86 = bf16[2048,1024]{1,0:T(8,128)(2,1)} custom-call(bf16[2048,1024]{1,0:T(8,128)(2,1)} %bitcast.63), custom_call_target="tpu_custom_call" | custom-call | tf_op jit(solution)/shard_map/pallas_call | solution.py:143
  311.2 2.9 fusion.26
  314.0 0.4 copy-done.1
  314.4 2.1 fusion.10
  316.6 2.1 fusion.8
  318.7 0.0 copy-done
  318.8 0.7 fusion.25
  319.5 0.8 copy-done.12
  320.3 2.1 fusion.27
  322.4 4.5 %add_add_fusion = f32[896,1024]{1,0:T(8,128)} fusion(f32[896,1024]{1,0:T(8,128)S(1)} %fusion.8, f32[896,1024]{1,0:T(8,128)S(1)} %fusion.27, f32[896,1024]{1,0:T(8,128)S(1)} %fusion.10, bf16[1024,896]{1,0:T(8,128)(2,1)S(1)} %dynamic-slice_bitcast_fusion, bf16[1024,1024]{1,0:T(8,128)(2,1)S(1)} %bitcast.76), kind=kOutput, calls=%fused_computation.9 | convolution fusion | flops 1881800704 | bytes 18612224 | tf_op jit(solution)/shard_map/dot_general | solution.py:265
  (30 shorter events, 0.1 us)
Async XLA Ops:
  7.2 172.8 %reduce-scatter.3.cloned.1.call-start = ((), (), s32[]{:S(2)}) async-start(), calls=%async_computation.3 | async-start | bytes 4718592 | tf_op jit(solution)/shard_map/reduce_scatter | solution.py:233
  9.4 69.4 %copy-start.3 = (bf16[2,2,2,1,64,896]{5,4,3,0,1,2:T(8,128)(2,1)S(1)}, bf16[2,2,2,1,64,896]{5,4,3,0,1,2:T(8,128)(2,1)}, u32[]{:S(2)}) copy-start(bf16[2,2,2,1,64,896]{5,4,3,0,1,2:T(8,128)(2,1)} %copy.22) | copy-start | bytes 2752516
  79.6 8.1 %copy-start.7 = (bf16[896,1024]{1,0:T(8,128)(2,1)S(1)}, bf16[896,1024]{1,0:T(8,128)(2,1)}, u32[]{:S(2)}) copy-start(bf16[896,1024]{1,0:T(8,128)(2,1)} %x_ref.1) | copy-start | bytes 5505028
  84.7 3.1 copy-start.9
  84.7 3.1 copy-start.13
  86.5 1.2 copy-start.11
  93.7 63.3 %copy-start.4 = (bf16[2,2,2,1,64,896]{5,4,3,0,1,2:T(8,128)(2,1)S(1)}, bf16[2,2,2,1,64,896]{5,4,3,0,1,2:T(8,128)(2,1)}, u32[]{:S(2)}) copy-start(bf16[2,2,2,1,64,896]{5,4,3,0,1,2:T(8,128)(2,1)} %copy.22) | copy-start | bytes 2752516
  93.7 137.0 %reduce-scatter.5.cloned.1.call-start = ((), (), s32[]{:S(2)}) async-start(), calls=%async_computation.4 | async-start | bytes 4718592 | tf_op jit(solution)/shard_map/reduce_scatter | solution.py:233
  162.9 2.1 copy-start.8
  162.9 2.6 copy-start.10
  173.0 0.9 copy-start.14
  173.0 6.8 %copy-start.16 = (bf16[1024]{0:T(1024)(128)(2,1)S(1)}, bf16[1024]{0:T(1024)(128)(2,1)}, u32[]{:S(2)}) copy-start(bf16[1024]{0:T(1024)(128)(2,1)} %param.10) | copy-start | bytes 6148
  173.0 6.8 %copy-start.17 = (s32[16]{0:T(128)S(1)}, s32[16]{0:T(128)}, u32[]{:S(2)}) copy-start(s32[16]{0:T(128)} %param.11) | copy-start | bytes 196
  173.0 68.9 %copy-start.15 = (bf16[128,1024]{1,0:T(8,128)(2,1)S(1)}, bf16[128,1024]{1,0:T(8,128)(2,1)}, u32[]{:S(2)}) copy-start(bf16[128,1024]{1,0:T(8,128)(2,1)} %param.6) | copy-start | bytes 786436
  174.6 67.2 %all-to-all-start = ((bf16[16,8,1024]{2,0,1:T(8,128)(2,1)}), bf16[16,8,1024]{2,0,1:T(8,128)(2,1)S(1)}, u32[]{:S(2)}, u32[]{:S(2)}) async-start(bf16[16,8,1024]{2,0,1:T(8,128)(2,1)} %bitcast.62), calls=%async_computation.2 | async-start | bytes 524288 | tf_op jit(solution)/shard_map/all_to_all | solution.py:239
  242.9 54.3 %copy-start.5 = (bf16[128,1024]{1,0:T(8,128)(2,1)S(1)}, bf16[128,1024]{1,0:T(8,128)(2,1)}, u32[]{:S(2)}) copy-start(bf16[128,1024]{1,0:T(8,128)(2,1)} %get-tuple-element.8.x_ref) | copy-start | bytes 786436
  251.1 46.2 %copy-start.6 = (bf16[128,1024]{1,0:T(8,128)(2,1)S(1)}, bf16[128,1024]{1,0:T(8,128)(2,1)}, u32[]{:S(2)}) copy-start(bf16[128,1024]{1,0:T(8,128)(2,1)} %shard_map.84) | copy-start | bytes 786436
  311.1 3.3 copy-start.1
  314.4 2.1 copy-start.2
  316.6 2.2 copy-start
  318.8 1.5 copy-start.12
Sparse Core Ops, SparseCore 0:
  93.8 57.5 reduce-scatter.2
  173.1 57.5 reduce-scatter.4

commit v12 on v11

--- a/solution.py
+++ b/solution.py
@@ -208,6 +208,78 @@
     return whole.reshape((n * x.shape[0],) + x.shape[1:])
 
 
+def ring_scatter_kernel(axis, n, x_ref, out_ref, recv, send, send_sem, recv_sem, credit):
+    me = lax.axis_index(axis)
+    right, left = lax.rem(me + 1, n), lax.rem(me + n - 1, n)
+    half = out_ref.shape[1] // 2
+
+    barrier = pltpu.get_barrier_semaphore()
+    for neighbour in (left, right):
+        pl.semaphore_signal(barrier, inc=1, device_id=device_on(axis, neighbour), device_id_type=MESH)
+    pl.semaphore_wait(barrier, 2)
+
+    rings = ((1, right, left), (-1, left, right))
+
+    def transfer(ring, slot, target):
+        return pltpu.make_async_remote_copy(
+            src_ref=send.at[ring, slot],
+            dst_ref=recv.at[ring, slot],
+            send_sem=send_sem.at[ring, slot],
+            recv_sem=recv_sem.at[ring, slot],
+            device_id=device_on(axis, target),
+            device_id_type=MESH,
+        )
+
+    pending = {}
+    for k in range(n - 1):
+        slot = k % 2
+        for ring, (sign, target, source) in enumerate(rings):
+            cols = pl.ds(ring * half, half)
+            dest = lax.rem(me - sign * (k + 1) + 2 * n, n)
+            if k >= 2:
+                pending[ring, slot].wait_send()
+                pl.semaphore_wait(credit.at[ring], 1)
+            own = x_ref[dest, :, cols]
+            if k == 0:
+                send[ring, slot] = own
+            else:
+                transfer(ring, 1 - slot, target).wait_recv()
+                send[ring, slot] = recv[ring, 1 - slot] + own
+                if k < n - 2:
+                    pl.semaphore_signal(credit.at[ring], inc=1, device_id=device_on(axis, source), device_id_type=MESH)
+            copy = transfer(ring, slot, target)
+            copy.start()
+            pending[ring, slot] = copy
+    last = (n - 2) % 2
+    for ring, (sign, target, source) in enumerate(rings):
+        cols = pl.ds(ring * half, half)
+        transfer(ring, last, target).wait_recv()
+        out_ref[:, cols] = recv[ring, last] + x_ref[me, :, cols]
+    for copy in pending.values():
+        copy.wait_send()
+
+
+def ring_scatter(x, axis, collective_id):
+    n = x.shape[0]
+    rows, cols = x.shape[1:]
+    return pl.pallas_call(
+        functools.partial(ring_scatter_kernel, axis, n),
+        out_shape=jax.ShapeDtypeStruct((rows, cols), x.dtype),
+        in_specs=[pl.BlockSpec(memory_space=pltpu.VMEM)],
+        out_specs=pl.BlockSpec(memory_space=pltpu.VMEM),
+        scratch_shapes=[
+            pltpu.VMEM((2, 2, rows, cols // 2), x.dtype),
+            pltpu.VMEM((2, 2, rows, cols // 2), x.dtype),
+            pltpu.SemaphoreType.DMA((2, 2)),
+            pltpu.SemaphoreType.DMA((2, 2)),
+            pltpu.SemaphoreType.REGULAR((2,)),
+        ],
+        compiler_params=pltpu.CompilerParams(
+            collective_id=collective_id, has_side_effects=True, vmem_limit_bytes=48 * 1024 * 1024
+        ),
+    )(x)
+
+
 def per_device(resid_in, hidden, w_down, frozen, steer, forget_flags):
     n_yh, n_z, n_c = (lax.axis_size(a) for a in DP)
     tok_rows, d_cols = resid_in.shape
@@ -230,7 +302,10 @@
         from_partner = swap_with_partner(hp, 2 * part + 1, True)
         pair_rows = jnp.concatenate([hp[me_c], from_partner], axis=1)
         reduced = jnp.dot(pair_rows, pair_w, preferred_element_type=jnp.float32)
-        reduced_z = lax.psum_scatter(reduced, "z", scatter_dimension=0, tiled=True)
+        if part == 0:
+            reduced_z = lax.psum_scatter(reduced, "z", scatter_dimension=0, tiled=True)
+        else:
+            reduced_z = ring_scatter(reduced.reshape((n_z, -1, d_cols)), "z", 11)
         by_yh = reduced_z.reshape((n_yh, -1, d_cols))
         mlp_parts.append(by_yh[me_yh] + swap_with_partner(by_yh, 6 + part, True, "yh"))
     mlp_out = jnp.concatenate(mlp_parts, axis=0)

time: 335 us -> 348 us (1.039)
  Pallas kernels: 228 us -> 282 us
  waiting for transfers between devices: 39.1 us -> 0.04 us
    pallas_call x0 -> x1, Pallas kernels: none -> 49.1 us  [ring_scatter(): pl.pallas_call(functools.partial(ring_scatter_kernel, axis, n), out_shape...]
    reduce_scatter x2 -> x1, waiting for transfers between devices: 39.1 us -> 0.02 us  [per_device(): reduced_z = lax.psum_scatter(reduced, 'z', scatter_dimension=0, tiled=True)]
  transfers between devices with their start and end apart: 3 -> 2, of which waited for: 1 -> 0; matrix products, arithmetic and copies ran while one was open for 4% -> 3% of each run, Pallas kernels for 27% -> 39%
where the time goes in v12:
time: 348 us; the launch traced here: 347 us
  Pallas kernels  282 us (81%)
  matrix products  22.2 us (6%)
  local copies, waits for them, and re-layouts  16.7 us (5%)
  between operations  14.4 us (4%)
  other arithmetic  6.4 us (2%)
  starting transfers between devices  5.18 us (1%)
    pallas_call x2, Pallas kernels, gather_part(): pl.pallas_call(functools.partial(placed_gather_kernel, n, n_zhi, part), o...  130 us
    pallas_call x7, Pallas kernels, swap_with_partner(): pl.pallas_call(functools.partial(swap_kernel, axis, halves), out_shape=ja...  59.3 us
    pallas_call x1, Pallas kernels, ring_scatter(): pl.pallas_call(functools.partial(ring_scatter_kernel, axis, n), out_shape...  49.1 us
    pallas_call x1, Pallas kernels, ring_gather(): pl.pallas_call(functools.partial(ring_gather_kernel, axis, n), out_shape=...  44.2 us
    dot_general x2, matrix products, per_device(): reduced = jnp.dot(pair_rows, pair_w, preferred_element_type=jnp.float32)  11.4 us
    dot_general x4, matrix products, per_device(): lax.dot_general(lax.dynamic_index_in_dim(hp_parts[part], rows, keepdims=F...  10.9 us
  transfers between devices with their start and end apart: 2, of which 0 were waited for; matrix products, arithmetic and copies ran while one was open for 3% of the time, Pallas kernels for 39%

profile of v12, /device:TPU:29, one launch (start us, length us, event | category | flops | bytes accessed | tf_op | source)
XLA Modules:
  0.0 347.2 jit_solution(2262878821121055299)
XLA Ops:
  7.2 0.0 reduce-scatter.2.cloned.1.call-start
  7.2 2.2 copy.22
  9.4 4.4 %shard_map.79 = bf16[896,1024]{1,0:T(8,128)(2,1)} custom-call(bf16[896,1024]{1,0:T(8,128)(2,1)} %x_ref.1), custom_call_target="tpu_custom_call" | custom-call | tf_op jit(solution)/shard_map/pallas_call | solution.py:143
  13.9 64.9 %shard_map.77 = bf16[2,8,2,64,896]{4,3,2,1,0:T(8,128)(2,1)} custom-call(bf16[2,2,2,1,64,896]{5,4,3,2,1,0:T(8,128)(2,1)} %bitcast.76), custom_call_target="tpu_custom_call" | custom-call | bytes 7340032 | tf_op jit(solution)/shard_map/pallas_call | solution.py:106
  78.8 0.8 fusion.19
  79.6 5.0 %shard_map.78 = bf16[1024,896]{1,0:T(8,128)(2,1)} custom-call(bf16[2,1024,896]{2,1,0:T(8,128)(2,1)} %bitcast.69), custom_call_target="tpu_custom_call" | custom-call | tf_op jit(solution)/shard_map/pallas_call | solution.py:143
  84.7 1.8 dynamic-slice_bitcast_fusion.1
  86.5 0.0 copy-start.12
  86.5 1.2 copy-done.12
  87.7 5.9 %fusion = f32[1024,1024]{1,0:T(8,128)} fusion(bf16[1024,896]{1,0:T(8,128)(2,1)S(1)} %copy-done.14, bf16[1024,896]{1,0:T(8,128)(2,1)S(1)} %dynamic-slice_bitcast_fusion.1, bf16[896,1024]{1,0:T(8,128)(2,1)S(1)} %copy-done.10, bf16[896,1024]{1,0:T(8,128)(2,1)S(1)} %copy-done.8), kind=kOutput, calls=%fused_computation | convolution fusion | flops 3772776448 | bytes 11534336 | tf_op jit(solution)/shard_map/dot_general | solution.py:304
  93.6 0.0 reduce-scatter.2.cloned.1.call-update
  93.7 0.9 copy-done.15
  94.6 0.7 copy.23
  95.3 5.1 %all-to-all-start = ((bf16[16,8,1024]{2,0,1:T(8,128)(2,1)}), bf16[16,8,1024]{2,0,1:T(8,128)(2,1)S(1)}, u32[]{:S(2)}, u32[]{:S(2)}) async-start(bf16[16,8,1024]{2,0,1:T(8,128)(2,1)} %bitcast.63), calls=%async_computation.1 | async-start | bytes 524288 | tf_op jit(solution)/shard_map/all_to_all | solution.py:314
  100.5 64.7 %shard_map.81 = bf16[2,8,2,64,896]{4,3,2,1,0:T(8,128)(2,1)} custom-call(bf16[2,2,2,1,64,896]{5,4,3,2,1,0:T(8,128)(2,1)} %bitcast.77), custom_call_target="tpu_custom_call" | custom-call | bytes 7340032 | tf_op jit(solution)/shard_map/pallas_call | solution.py:106
  165.2 0.8 bitcast_dynamic-update-slice_fusion
  166.0 5.5 %shard_map.82 = bf16[1024,896]{1,0:T(8,128)(2,1)} custom-call(bf16[2,1024,896]{2,1,0:T(8,128)(2,1)} %bitcast.72), custom_call_target="tpu_custom_call" | custom-call | tf_op jit(solution)/shard_map/pallas_call | solution.py:143
  171.6 0.0 copy-start.9
  171.6 1.8 dynamic-slice_bitcast_fusion
  173.4 0.2 copy-done.9
  173.6 0.6 copy-done.11
  174.2 5.4 %fusion.4 = f32[1024,1024]{1,0:T(8,128)S(1)} fusion(bf16[1024,896]{1,0:T(8,128)(2,1)} %shard_map.82, bf16[1024,896]{1,0:T(8,128)(2,1)S(1)} %dynamic-slice_bitcast_fusion, bf16[896,1024]{1,0:T(8,128)(2,1)S(1)} %copy-done.11, bf16[896,1024]{1,0:T(8,128)(2,1)S(1)} %copy-done.9), kind=kOutput, calls=%fused_computation.5 | convolution fusion | flops 3772776448 | bytes 11534336 | tf_op jit(solution)/shard_map/dot_general | solution.py:304
  179.6 0.0 copy-start.18
  179.6 0.0 copy-start.16
  179.6 49.1 %shard_map.83 = f32[128,1024]{1,0:T(8,128)S(1)} custom-call(f32[8,128,1024]{2,1,0:T(8,128)S(1)} %bitcast.64), custom_call_target="tpu_custom_call" | custom-call | tf_op jit(solution)/shard_map/pallas_call | solution.py:265
  228.7 0.8 copy-done
  229.5 7.1 %shard_map.84 = f32[64,1024]{1,0:T(8,128)} custom-call(f32[2,64,1024]{2,1,0:T(8,128)} %bitcast.65), custom_call_target="tpu_custom_call" | custom-call | tf_op jit(solution)/shard_map/pallas_call | solution.py:143
  236.6 0.1 select_reduce_fusion
  236.7 1.1 bitcast_add_fusion
  237.8 0.0 reduce-scatter.2.cloned.1.call-done
  237.8 7.4 %shard_map.80 = f32[64,1024]{1,0:T(8,128)} custom-call(f32[2,64,1024]{2,1,0:T(8,128)} %bitcast.86), custom_call_target="tpu_custom_call" | custom-call | tf_op jit(solution)/shard_map/pallas_call | solution.py:143
  245.2 1.1 bitcast_add_fusion.1
  246.3 0.0 all-to-all-done
  246.3 1.0 fusion.18
  247.3 7.6 %shard_map.85 = bf16[128,1024]{1,0:T(8,128)(2,1)} custom-call(bf16[128,1024]{1,0:T(8,128)(2,1)} %get-tuple-element.8.x_ref), custom_call_target="tpu_custom_call" | custom-call | tf_op jit(solution)/shard_map/pallas_call | solution.py:143
  254.9 2.2 maximum_select_fusion.x_ref
  257.1 44.2 %shard_map.86 = bf16[8,256,1024]{2,1,0:T(8,128)(2,1)} custom-call(bf16[256,1024]{1,0:T(8,128)(2,1)} %maximum_select_fusion.x_ref), custom_call_target="tpu_custom_call" | custom-call | tf_op jit(solution)/shard_map/pallas_call | solution.py:199
  301.4 1.0 fusion.14
  302.3 22.3 %shard_map.87 = bf16[2048,1024]{1,0:T(8,128)(2,1)} custom-call(bf16[2048,1024]{1,0:T(8,128)(2,1)} %bitcast.67), custom_call_target="tpu_custom_call" | custom-call | tf_op jit(solution)/shard_map/pallas_call | solution.py:143
  324.6 2.9 fusion.26
  327.5 0.4 copy-done.2
  327.9 2.1 fusion.10
  330.1 2.1 fusion.8
  332.2 0.0 copy-done.1
  332.2 0.7 fusion.25
  332.9 0.8 copy-done.13
  333.7 2.1 fusion.27
  335.9 4.5 %add_add_fusion = f32[896,1024]{1,0:T(8,128)} fusion(f32[896,1024]{1,0:T(8,128)S(1)} %fusion.8, f32[896,1024]{1,0:T(8,128)S(1)} %fusion.27, f32[896,1024]{1,0:T(8,128)S(1)} %fusion.10, bf16[1024,896]{1,0:T(8,128)(2,1)S(1)} %dynamic-slice_bitcast_fusion, bf16[1024,1024]{1,0:T(8,128)(2,1)S(1)} %bitcast.80), kind=kOutput, calls=%fused_computation.9 | convolution fusion | flops 1881800704 | bytes 18612224 | tf_op jit(solution)/shard_map/dot_general | solution.py:340
  (30 shorter events, 0.1 us)
Async XLA Ops:
  7.2 230.7 %reduce-scatter.2.cloned.1.call-start = ((), (), s32[]{:S(2)}) async-start(), calls=%async_computation.2 | async-start | bytes 4718592 | tf_op jit(solution)/shard_map/reduce_scatter | solution.py:306
  9.4 69.4 %copy-start.4 = (bf16[2,2,2,1,64,896]{5,4,3,0,1,2:T(8,128)(2,1)S(1)}, bf16[2,2,2,1,64,896]{5,4,3,0,1,2:T(8,128)(2,1)}, u32[]{:S(2)}) copy-start(bf16[2,2,2,1,64,896]{5,4,3,0,1,2:T(8,128)(2,1)} %copy.22) | copy-start | bytes 2752516
  79.6 8.1 %copy-start.8 = (bf16[896,1024]{1,0:T(8,128)(2,1)S(1)}, bf16[896,1024]{1,0:T(8,128)(2,1)}, u32[]{:S(2)}) copy-start(bf16[896,1024]{1,0:T(8,128)(2,1)} %x_ref.1) | copy-start | bytes 5505028
  84.7 3.1 copy-start.10
  84.7 3.1 copy-start.14
  86.5 1.2 copy-start.12
  93.6 0.9 copy-start.15
  93.6 6.8 %copy-start.17 = (bf16[1024]{0:T(1024)(128)(2,1)S(1)}, bf16[1024]{0:T(1024)(128)(2,1)}, u32[]{:S(2)}) copy-start(bf16[1024]{0:T(1024)(128)(2,1)} %param.10) | copy-start | bytes 6148
  93.7 71.5 %copy-start.5 = (bf16[2,2,2,1,64,896]{5,4,3,0,1,2:T(8,128)(2,1)S(1)}, bf16[2,2,2,1,64,896]{5,4,3,0,1,2:T(8,128)(2,1)}, u32[]{:S(2)}) copy-start(bf16[2,2,2,1,64,896]{5,4,3,0,1,2:T(8,128)(2,1)} %copy.22) | copy-start | bytes 2752516
  95.3 151.0 %all-to-all-start = ((bf16[16,8,1024]{2,0,1:T(8,128)(2,1)}), bf16[16,8,1024]{2,0,1:T(8,128)(2,1)S(1)}, u32[]{:S(2)}, u32[]{:S(2)}) async-start(bf16[16,8,1024]{2,0,1:T(8,128)(2,1)} %bitcast.63), calls=%async_computation.1 | async-start | bytes 524288 | tf_op jit(solution)/shard_map/all_to_all | solution.py:314
  171.6 2.1 copy-start.9
  171.6 2.6 copy-start.11
  179.6 57.0 %copy-start.18 = (s32[16]{0:T(128)S(1)}, s32[16]{0:T(128)}, u32[]{:S(2)}) copy-start(s32[16]{0:T(128)} %param.11) | copy-start | bytes 196
  179.6 66.7 %copy-start.16 = (bf16[128,1024]{1,0:T(8,128)(2,1)S(1)}, bf16[128,1024]{1,0:T(8,128)(2,1)}, u32[]{:S(2)}) copy-start(bf16[128,1024]{1,0:T(8,128)(2,1)} %param.6) | copy-start | bytes 786436
  228.7 0.8 copy-start
  247.3 54.1 %copy-start.6 = (bf16[128,1024]{1,0:T(8,128)(2,1)S(1)}, bf16[128,1024]{1,0:T(8,128)(2,1)}, u32[]{:S(2)}) copy-start(bf16[128,1024]{1,0:T(8,128)(2,1)} %get-tuple-element.8.x_ref) | copy-start | bytes 786436
  254.9 46.5 %copy-start.7 = (bf16[128,1024]{1,0:T(8,128)(2,1)S(1)}, bf16[128,1024]{1,0:T(8,128)(2,1)}, u32[]{:S(2)}) copy-start(bf16[128,1024]{1,0:T(8,128)(2,1)} %shard_map.85) | copy-start | bytes 786436
  324.6 3.3 copy-start.2
  327.9 2.1 copy-start.3
  330.0 2.2 copy-start.1
  332.2 1.5 copy-start.13
Sparse Core Ops, SparseCore 0:
  93.8 57.5 reduce-scatter.1

commit v13 on v12

--- a/solution.py
+++ b/solution.py
@@ -303,9 +303,13 @@
         pair_rows = jnp.concatenate([hp[me_c], from_partner], axis=1)
         reduced = jnp.dot(pair_rows, pair_w, preferred_element_type=jnp.float32)
         if part == 0:
-            reduced_z = lax.psum_scatter(reduced, "z", scatter_dimension=0, tiled=True)
+            reduced_z = first_z = lax.psum_scatter(reduced, "z", scatter_dimension=0, tiled=True)
         else:
-            reduced_z = ring_scatter(reduced.reshape((n_z, -1, d_cols)), "z", 11)
+            split = d_cols // 2
+            sc_cols, _ = lax.optimization_barrier((reduced[:, :split], first_z))
+            on_sc = lax.psum_scatter(sc_cols, "z", scatter_dimension=0, tiled=True)
+            on_tc = ring_scatter(reduced[:, split:].reshape((n_z, -1, d_cols - split)), "z", 11)
+            reduced_z = jnp.concatenate([on_sc, on_tc], axis=1)
         by_yh = reduced_z.reshape((n_yh, -1, d_cols))
         mlp_parts.append(by_yh[me_yh] + swap_with_partner(by_yh, 6 + part, True, "yh"))
     mlp_out = jnp.concatenate(mlp_parts, axis=0)

time: 348 us -> 344 us (0.989)
  Pallas kernels: 282 us -> 278 us
    pallas_call x7, Pallas kernels: 59.3 us -> 54.2 us  [swap_with_partner(): pl.pallas_call(functools.partial(swap_kernel, axis, halves), out_shape=ja...]
    pallas_call x1, Pallas kernels: 44.2 us -> 48.2 us  [ring_gather(): pl.pallas_call(functools.partial(ring_gather_kernel, axis, n), out_shape=...]
  transfers between devices with their start and end apart: 2 -> 3, of which waited for: 0 -> 0; matrix products, arithmetic and copies ran while one was open for 3% -> 4% of each run, Pallas kernels for 39% -> 38%
where the time goes in v13:
time: 344 us
  Pallas kernels  278 us (81%)
  matrix products  20.7 us (6%)
  local copies, waits for them, and re-layouts  16.8 us (5%)
  between operations  14.4 us (4%)
  other arithmetic  8.12 us (2%)
  starting transfers between devices  5.36 us (2%)
    pallas_call x2, Pallas kernels, gather_part(): pl.pallas_call(functools.partial(placed_gather_kernel, n, n_zhi, part), o...  128 us
    pallas_call x7, Pallas kernels, swap_with_partner(): pl.pallas_call(functools.partial(swap_kernel, axis, halves), out_shape=ja...  54.2 us
    pallas_call x1, Pallas kernels, ring_gather(): pl.pallas_call(functools.partial(ring_gather_kernel, axis, n), out_shape=...  48.2 us
    pallas_call x1, Pallas kernels, ring_scatter(): pl.pallas_call(functools.partial(ring_scatter_kernel, axis, n), out_shape...  47.8 us
    dot_general x4, matrix products, per_device(): lax.dot_general(lax.dynamic_index_in_dim(hp_parts[part], rows, keepdims=F...  10.9 us
    dot_general x2, matrix products, per_device(): reduced = jnp.dot(pair_rows, pair_w, preferred_element_type=jnp.float32)  9.88 us
  transfers between devices with their start and end apart: 3, of which 0 were waited for; matrix products, arithmetic and copies ran while one was open for 4% of the time, Pallas kernels for 38%

profile of v13, /device:TPU:29, one launch (start us, length us, event | category | flops | bytes accessed | tf_op | source)
XLA Modules:
  0.0 343.8 jit_solution(16375018151886015263)
XLA Ops:
  7.2 0.0 reduce-scatter.3.cloned.1.call-start
  7.2 2.2 copy.22
  9.4 4.4 %shard_map.79 = bf16[896,1024]{1,0:T(8,128)(2,1)} custom-call(bf16[896,1024]{1,0:T(8,128)(2,1)} %x_ref.1), custom_call_target="tpu_custom_call" | custom-call | tf_op jit(solution)/shard_map/pallas_call | solution.py:143
  13.9 64.9 %shard_map.77 = bf16[2,8,2,64,896]{4,3,2,1,0:T(8,128)(2,1)} custom-call(bf16[2,2,2,1,64,896]{5,4,3,2,1,0:T(8,128)(2,1)} %bitcast.74), custom_call_target="tpu_custom_call" | custom-call | bytes 7340032 | tf_op jit(solution)/shard_map/pallas_call | solution.py:106
  78.8 0.8 fusion.19
  79.6 5.0 %shard_map.78 = bf16[1024,896]{1,0:T(8,128)(2,1)} custom-call(bf16[2,1024,896]{2,1,0:T(8,128)(2,1)} %bitcast.67), custom_call_target="tpu_custom_call" | custom-call | tf_op jit(solution)/shard_map/pallas_call | solution.py:143
  84.7 1.8 dynamic-slice_bitcast_fusion.1
  86.5 1.2 copy-done.12
  87.7 5.9 %fusion = f32[1024,1024]{1,0:T(8,128)} fusion(bf16[1024,896]{1,0:T(8,128)(2,1)S(1)} %copy-done.14, bf16[1024,896]{1,0:T(8,128)(2,1)S(1)} %dynamic-slice_bitcast_fusion.1, bf16[896,1024]{1,0:T(8,128)(2,1)S(1)} %copy-done.10, bf16[896,1024]{1,0:T(8,128)(2,1)S(1)} %copy-done.9), kind=kOutput, calls=%fused_computation | convolution fusion | flops 3772776448 | bytes 11534336 | tf_op jit(solution)/shard_map/dot_general | solution.py:304
  93.6 0.0 reduce-scatter.3.cloned.1.call-update
  93.7 0.0 reduce-scatter.5.cloned.1.call-start
  93.7 63.3 %shard_map.81 = bf16[2,8,2,64,896]{4,3,2,1,0:T(8,128)(2,1)} custom-call(bf16[2,2,2,1,64,896]{5,4,3,2,1,0:T(8,128)(2,1)} %bitcast.75), custom_call_target="tpu_custom_call" | custom-call | bytes 7340032 | tf_op jit(solution)/shard_map/pallas_call | solution.py:106
  157.0 0.8 bitcast_dynamic-update-slice_fusion
  157.8 5.0 %shard_map.82 = bf16[1024,896]{1,0:T(8,128)(2,1)} custom-call(bf16[2,1024,896]{2,1,0:T(8,128)(2,1)} %bitcast.70), custom_call_target="tpu_custom_call" | custom-call | tf_op jit(solution)/shard_map/pallas_call | solution.py:143
  162.9 1.8 dynamic-slice_bitcast_fusion
  164.7 0.2 copy-done.11
  164.9 0.6 copy-done.15
  165.5 4.0 %fusion.4 = f32[1024,1024]{1,0:T(8,128)S(1)} fusion(bf16[1024,896]{1,0:T(8,128)(2,1)S(1)} %copy-done.15, bf16[1024,896]{1,0:T(8,128)(2,1)S(1)} %dynamic-slice_bitcast_fusion, bf16[896,1024]{1,0:T(8,128)(2,1)S(1)} %copy-done.11, bf16[896,1024]{1,0:T(8,128)(2,1)S(1)} %copy-done.9), kind=kOutput, calls=%fused_computation.5 | convolution fusion | flops 3772776448 | bytes 11534336 | tf_op jit(solution)/shard_map/dot_general | solution.py:304
  169.5 0.0 copy-start.17
  169.5 0.0 copy-start.19
  169.5 1.8 fusion.27
  171.2 0.0 reduce-scatter.5.cloned.1.call-update
  171.3 0.7 copy.23
  172.0 5.3 %all-to-all-start = ((bf16[16,8,1024]{2,0,1:T(8,128)(2,1)}), bf16[16,8,1024]{2,0,1:T(8,128)(2,1)S(1)}, u32[]{:S(2)}, u32[]{:S(2)}) async-start(bf16[16,8,1024]{2,0,1:T(8,128)(2,1)} %bitcast.63), calls=%async_computation.2 | async-start | bytes 524288 | tf_op jit(solution)/shard_map/all_to_all | solution.py:318
  177.3 47.8 %shard_map.83 = f32[128,512]{1,0:T(8,128)S(1)} custom-call(f32[8,128,512]{2,1,0:T(8,128)S(1)} %bitcast.64), custom_call_target="tpu_custom_call" | custom-call | tf_op jit(solution)/shard_map/pallas_call | solution.py:265
  225.1 0.1 select_reduce_fusion
  225.2 7.2 %shard_map.80 = f32[64,1024]{1,0:T(8,128)} custom-call(f32[2,64,1024]{2,1,0:T(8,128)} %bitcast.86), custom_call_target="tpu_custom_call" | custom-call | tf_op jit(solution)/shard_map/pallas_call | solution.py:143
  232.5 1.0 bitcast_add_fusion.1
  233.4 0.0 reduce-scatter.5.cloned.1.call-done
  233.5 1.8 pad_maximum_fusion.3
  235.3 7.1 %shard_map.84 = f32[64,1024]{1,0:T(8,128)} custom-call(f32[2,64,1024]{2,1,0:T(8,128)} %bitcast.80), custom_call_target="tpu_custom_call" | custom-call | tf_op jit(solution)/shard_map/pallas_call | solution.py:143
  242.3 1.1 bitcast_add_fusion
  243.4 0.0 all-to-all-done
  243.4 1.0 fusion.18
  244.4 7.1 %shard_map.85 = bf16[128,1024]{1,0:T(8,128)(2,1)} custom-call(bf16[128,1024]{1,0:T(8,128)(2,1)} %get-tuple-element.12.x_ref), custom_call_target="tpu_custom_call" | custom-call | tf_op jit(solution)/shard_map/pallas_call | solution.py:143
  251.5 2.2 maximum_select_fusion.x_ref
  253.7 48.2 %shard_map.86 = bf16[8,256,1024]{2,1,0:T(8,128)(2,1)} custom-call(bf16[256,1024]{1,0:T(8,128)(2,1)} %maximum_select_fusion.x_ref), custom_call_target="tpu_custom_call" | custom-call | tf_op jit(solution)/shard_map/pallas_call | solution.py:199
  301.9 1.0 fusion.14
  302.9 18.4 %shard_map.87 = bf16[2048,1024]{1,0:T(8,128)(2,1)} custom-call(bf16[2048,1024]{1,0:T(8,128)(2,1)} %bitcast.65), custom_call_target="tpu_custom_call" | custom-call | tf_op jit(solution)/shard_map/pallas_call | solution.py:143
  321.3 2.9 fusion.26
  324.2 0.4 copy-done.1
  324.6 2.1 fusion.10
  326.7 2.1 fusion.8
  328.9 0.0 copy-done
  328.9 0.7 fusion.25
  329.6 0.8 copy-done.13
  330.4 2.1 fusion.28
  332.5 4.5 %add_add_fusion = f32[896,1024]{1,0:T(8,128)} fusion(f32[896,1024]{1,0:T(8,128)S(1)} %fusion.8, f32[896,1024]{1,0:T(8,128)S(1)} %fusion.28, f32[896,1024]{1,0:T(8,128)S(1)} %fusion.10, bf16[1024,896]{1,0:T(8,128)(2,1)S(1)} %copy-done.6, bf16[1024,1024]{1,0:T(8,128)(2,1)S(1)} %bitcast.78), kind=kOutput, calls=%fused_computation.9 | convolution fusion | flops 1881800704 | bytes 18612224 | tf_op jit(solution)/shard_map/dot_general | solution.py:344
  (39 shorter events, 0.1 us)
Async XLA Ops:
  7.2 164.1 %reduce-scatter.3.cloned.1.call-start = ((), (), s32[]{:S(2)}) async-start(), calls=%async_computation.3 | async-start | bytes 4718592 | tf_op jit(solution)/shard_map/reduce_scatter | solution.py:306
  9.4 69.4 %copy-start.3 = (bf16[2,2,2,1,64,896]{5,4,3,0,1,2:T(8,128)(2,1)S(1)}, bf16[2,2,2,1,64,896]{5,4,3,0,1,2:T(8,128)(2,1)}, u32[]{:S(2)}) copy-start(bf16[2,2,2,1,64,896]{5,4,3,0,1,2:T(8,128)(2,1)} %copy.22) | copy-start | bytes 2752516
  79.6 8.1 %copy-start.9 = (bf16[896,1024]{1,0:T(8,128)(2,1)S(1)}, bf16[896,1024]{1,0:T(8,128)(2,1)}, u32[]{:S(2)}) copy-start(bf16[896,1024]{1,0:T(8,128)(2,1)} %x_ref.1) | copy-start | bytes 5505028
  84.7 3.1 copy-start.10
  84.7 3.0 copy-start.14
  86.5 1.2 copy-start.12
  93.6 63.3 %copy-start.4 = (bf16[2,2,2,1,64,896]{5,4,3,0,1,2:T(8,128)(2,1)S(1)}, bf16[2,2,2,1,64,896]{5,4,3,0,1,2:T(8,128)(2,1)}, u32[]{:S(2)}) copy-start(bf16[2,2,2,1,64,896]{5,4,3,0,1,2:T(8,128)(2,1)} %copy.22) | copy-start | bytes 2752516
  93.7 139.8 %reduce-scatter.5.cloned.1.call-start = ((), (), s32[]{:S(2)}) async-start(), calls=%async_computation.4 | async-start | bytes 2359296 | tf_op jit(solution)/shard_map/reduce_scatter | solution.py:310
  162.9 2.1 copy-start.11
  162.9 2.6 copy-start.15
  165.5 4.0 %copy-start.5 = (bf16[1024,896]{1,0:T(8,128)(2,1)}, bf16[1024,896]{1,0:T(8,128)(2,1)S(1)}, u32[]{:S(2)}) copy-start(bf16[1024,896]{1,0:T(8,128)(2,1)S(1)} %dynamic-slice_bitcast_fusion) | copy-start | bytes 5505028
  169.5 1.8 copy-start.17
  169.5 7.8 %copy-start.19 = (bf16[1024]{0:T(1024)(128)(2,1)S(1)}, bf16[1024]{0:T(1024)(128)(2,1)}, u32[]{:S(2)}) copy-start(bf16[1024]{0:T(1024)(128)(2,1)} %param.10) | copy-start | bytes 6148
  171.2 53.9 %copy-start.20 = (s32[16]{0:T(128)S(1)}, s32[16]{0:T(128)}, u32[]{:S(2)}) copy-start(s32[16]{0:T(128)} %param.11) | copy-start | bytes 196
  171.2 61.2 %copy-start.16 = (f32[128,1024]{1,0:T(8,128)S(1)}, f32[128,1024]{1,0:T(8,128)}, u32[]{:S(2)}) copy-start(f32[128,1024]{1,0:T(8,128)} %reduce-scatter.3.cloned.1.call-done) | copy-start | bytes 1572868
  172.0 71.4 %copy-start.18 = (bf16[128,1024]{1,0:T(8,128)(2,1)S(1)}, bf16[128,1024]{1,0:T(8,128)(2,1)}, u32[]{:S(2)}) copy-start(bf16[128,1024]{1,0:T(8,128)(2,1)} %param.6) | copy-start | bytes 786436
  172.0 71.4 %all-to-all-start = ((bf16[16,8,1024]{2,0,1:T(8,128)(2,1)}), bf16[16,8,1024]{2,0,1:T(8,128)(2,1)S(1)}, u32[]{:S(2)}, u32[]{:S(2)}) async-start(bf16[16,8,1024]{2,0,1:T(8,128)(2,1)} %bitcast.63), calls=%async_computation.2 | async-start | bytes 524288 | tf_op jit(solution)/shard_map/all_to_all | solution.py:318
  244.4 57.5 %copy-start.7 = (bf16[128,1024]{1,0:T(8,128)(2,1)S(1)}, bf16[128,1024]{1,0:T(8,128)(2,1)}, u32[]{:S(2)}) copy-start(bf16[128,1024]{1,0:T(8,128)(2,1)} %get-tuple-element.12.x_ref) | copy-start | bytes 786436
  251.5 50.4 %copy-start.8 = (bf16[128,1024]{1,0:T(8,128)(2,1)S(1)}, bf16[128,1024]{1,0:T(8,128)(2,1)}, u32[]{:S(2)}) copy-start(bf16[128,1024]{1,0:T(8,128)(2,1)} %shard_map.85) | copy-start | bytes 786436
  321.3 3.3 copy-start.1
  324.6 2.1 copy-start.2
  326.7 2.2 copy-start
  328.9 1.5 copy-start.13
  330.4 2.1 copy-start.6
Sparse Core Ops, SparseCore 0:
  93.8 57.5 reduce-scatter.2
  171.4 50.0 reduce-scatter.4

commit v14 on v11

--- a/solution.py
+++ b/solution.py
@@ -212,7 +212,7 @@
     n_yh, n_z, n_c = (lax.axis_size(a) for a in DP)
     tok_rows, d_cols = resid_in.shape
     own_tokens, ff_rows = hidden.shape
-    n_parts = 2
+    n_parts = 4
     sub = tok_rows // n_parts
     blocks = own_tokens // tok_rows
     total_tokens = own_tokens * lax.axis_size("shard")
@@ -220,7 +220,7 @@
     me_yh = lax.axis_index("yh")
     xt = hidden.reshape(blocks // n_c, n_c, n_parts, 1, sub, ff_rows).transpose(2, 1, 0, 3, 4, 5)
     hp_parts, mlp_parts = [], []
-    pair_w = jnp.concatenate([w_down, swap_with_partner(w_down, 9, False)], axis=0)
+    pair_w = jnp.concatenate([w_down, swap_with_partner(w_down, 4 * n_parts, False)], axis=0)
     for part in range(n_parts):
         if part > 0:
             xt, _ = lax.optimization_barrier((xt, reduced))
@@ -232,7 +232,7 @@
         reduced = jnp.dot(pair_rows, pair_w, preferred_element_type=jnp.float32)
         reduced_z = lax.psum_scatter(reduced, "z", scatter_dimension=0, tiled=True)
         by_yh = reduced_z.reshape((n_yh, -1, d_cols))
-        mlp_parts.append(by_yh[me_yh] + swap_with_partner(by_yh, 6 + part, True, "yh"))
+        mlp_parts.append(by_yh[me_yh] + swap_with_partner(by_yh, 2 * n_parts + part, True, "yh"))
     mlp_out = jnp.concatenate(mlp_parts, axis=0)
     residual = resid_in.astype(jnp.float32) + mlp_out
     updated = residual.astype(jnp.bfloat16)
@@ -249,14 +249,14 @@
     slopes = (loss_weight[:, None] * (residual - target) * (1.0 / math.sqrt(total_tokens))).astype(
         jnp.bfloat16
     )
-    other_yh = swap_with_partner(slopes, 6 + n_parts, False, "yh")
+    other_yh = swap_with_partner(slopes, 3 * n_parts, False, "yh")
     gathered = jnp.where(
         me_yh == 0,
         jnp.concatenate([slopes, other_yh], axis=0),
         jnp.concatenate([other_yh, slopes], axis=0),
     )
-    gathered = ring_gather(gathered, "z", 10)
-    partner_slopes = swap_with_partner(gathered, 2 * n_parts + 1, False)
+    gathered = ring_gather(gathered, "z", 3 * n_parts + 1)
+    partner_slopes = swap_with_partner(gathered, 3 * n_parts + 2, False)
     contract = (((0,), (0,)), ((), ()))
     grad_down = None
     for part in range(n_parts):

time: 335 us -> 351 us (1.048)
  waiting for transfers between devices: 39.1 us -> 12 us
  matrix products: 24.3 us -> 44.6 us
  Pallas kernels: 228 us -> 244 us
  local copies, waits for them, and re-layouts: 16 us -> 20 us
    reduce_scatter x2 -> x4, waiting for transfers between devices: 39.1 us -> 11.9 us  [per_device(): reduced_z = lax.psum_scatter(reduced, 'z', scatter_dimension=0, tiled=True)]
    pallas_call x7 -> x11, Pallas kernels: 56.3 us -> 68.5 us  [swap_with_partner(): pl.pallas_call(functools.partial(swap_kernel, axis, halves), out_shape=ja...]
    dot_general x4 -> x8, matrix products: 10.9 us -> 22.1 us  [per_device(): lax.dot_general(lax.dynamic_index_in_dim(hp_parts[part], rows, keepdims=F...]
    dot_general x2 -> x4, matrix products: 13.4 us -> 22.5 us  [per_device(): reduced = jnp.dot(pair_rows, pair_w, preferred_element_type=jnp.float32)]
    pallas_call x1, Pallas kernels: 43.9 us -> 49.2 us  [ring_gather(): pl.pallas_call(functools.partial(ring_gather_kernel, axis, n), out_shape=...]
    dynamic_update_slice x2 -> x4, local copies, waits for them, and re-layouts: 1.69 us -> 6.7 us  [gather_part(): return lax.dynamic_update_slice(received, xt[part], at)]
    pallas_call x2 -> x4, Pallas kernels: 128 us -> 126 us  [gather_part(): pl.pallas_call(functools.partial(placed_gather_kernel, n, n_zhi, part), o...]
  transfers between devices with their start and end apart: 3 -> 5, of which waited for: 1 -> 1; matrix products, arithmetic and copies ran while one was open for 4% -> 9% of each run, Pallas kernels for 27% -> 37%
where the time goes in v14:
time: 351 us; the launch traced here: 349 us
  Pallas kernels  244 us (70%)
  matrix products  44.6 us (13%)
  local copies, waits for them, and re-layouts  20 us (6%)
  between operations  14.1 us (4%)
  waiting for transfers between devices  12 us (3%)
  other arithmetic  9.23 us (3%)
  starting transfers between devices  5.31 us (2%)
    pallas_call x4, Pallas kernels, gather_part(): pl.pallas_call(functools.partial(placed_gather_kernel, n, n_zhi, part), o...  126 us
    pallas_call x11, Pallas kernels, swap_with_partner(): pl.pallas_call(functools.partial(swap_kernel, axis, halves), out_shape=ja...  68.5 us
    pallas_call x1, Pallas kernels, ring_gather(): pl.pallas_call(functools.partial(ring_gather_kernel, axis, n), out_shape=...  49.2 us
    dot_general x4, matrix products, per_device(): reduced = jnp.dot(pair_rows, pair_w, preferred_element_type=jnp.float32)  22.5 us
    dot_general x8, matrix products, per_device(): lax.dot_general(lax.dynamic_index_in_dim(hp_parts[part], rows, keepdims=F...  22.1 us
    reduce_scatter x4, waiting for transfers between devices, per_device(): reduced_z = lax.psum_scatter(reduced, 'z', scatter_dimension=0, tiled=True)  11.9 us
  transfers between devices with their start and end apart: 5, of which 1 were waited for; matrix products, arithmetic and copies ran while one was open for 9% of the time, Pallas kernels for 37%

profile of v14, /device:TPU:29, one launch (start us, length us, event | category | flops | bytes accessed | tf_op | source)
XLA Modules:
  0.0 349.3 jit_solution(17848923491969645130)
XLA Ops:
  7.2 2.2 copy.28
  9.4 4.4 %shard_map.79 = bf16[896,1024]{1,0:T(8,128)(2,1)} custom-call(bf16[896,1024]{1,0:T(8,128)(2,1)} %x_ref.1), custom_call_target="tpu_custom_call" | custom-call | tf_op jit(solution)/shard_map/pallas_call | solution.py:143
  13.9 32.8 %shard_map.77 = bf16[2,8,2,32,896]{4,3,2,1,0:T(8,128)(2,1)} custom-call(bf16[4,2,2,1,32,896]{5,4,3,2,1,0:T(8,128)(2,1)} %bitcast.101), custom_call_target="tpu_custom_call" | custom-call | bytes 3670016 | tf_op jit(solution)/shard_map/pallas_call | solution.py:106
  46.8 1.7 fusion.32
  48.4 3.7 %shard_map.78 = bf16[512,896]{1,0:T(8,128)(2,1)} custom-call(bf16[2,512,896]{2,1,0:T(8,128)(2,1)} %bitcast.113), custom_call_target="tpu_custom_call" | custom-call | tf_op jit(solution)/shard_map/pallas_call | solution.py:143
  52.2 1.3 dynamic-slice_bitcast_fusion.3
  53.4 5.2 %fusion = f32[512,1024]{1,0:T(8,128)} fusion(bf16[512,896]{1,0:T(8,128)(2,1)} %shard_map.78, bf16[512,896]{1,0:T(8,128)(2,1)S(1)} %dynamic-slice_bitcast_fusion.3, bf16[896,1024]{1,0:T(8,128)(2,1)} %shard_map.79, bf16[896,1024]{1,0:T(8,128)(2,1)S(1)} %copy-done.9), kind=kOutput, calls=%fused_computation.2 | convolution fusion | flops 1890058240 | bytes 7602176 | tf_op jit(solution)/shard_map/dot_general | solution.py:232
  58.7 31.2 %shard_map.81 = bf16[2,8,2,32,896]{4,3,2,1,0:T(8,128)(2,1)} custom-call(bf16[4,2,2,1,32,896]{5,4,3,2,1,0:T(8,128)(2,1)} %bitcast.103), custom_call_target="tpu_custom_call" | custom-call | bytes 3670016 | tf_op jit(solution)/shard_map/pallas_call | solution.py:106
  89.9 1.7 bitcast_dynamic-update-slice_fusion.2
  91.6 3.7 %shard_map.82 = bf16[512,896]{1,0:T(8,128)(2,1)} custom-call(bf16[2,512,896]{2,1,0:T(8,128)(2,1)} %bitcast.116), custom_call_target="tpu_custom_call" | custom-call | tf_op jit(solution)/shard_map/pallas_call | solution.py:143
  95.3 1.3 dynamic-slice_bitcast_fusion.2
  96.6 5.8 %fusion.4 = f32[512,1024]{1,0:T(8,128)} fusion(bf16[512,896]{1,0:T(8,128)(2,1)} %shard_map.82, bf16[512,896]{1,0:T(8,128)(2,1)S(1)} %dynamic-slice_bitcast_fusion.2, bf16[896,1024]{1,0:T(8,128)(2,1)} %shard_map.79, bf16[896,1024]{1,0:T(8,128)(2,1)} %x_ref.1), kind=kOutput, calls=%fused_computation.6 | convolution fusion | flops 1890058240 | bytes 7602176 | tf_op jit(solution)/shard_map/dot_general | solution.py:232
  102.4 31.2 %shard_map.84 = bf16[2,8,2,32,896]{4,3,2,1,0:T(8,128)(2,1)} custom-call(bf16[4,2,2,1,32,896]{5,4,3,2,1,0:T(8,128)(2,1)} %bitcast.105), custom_call_target="tpu_custom_call" | custom-call | bytes 3670016 | tf_op jit(solution)/shard_map/pallas_call | solution.py:106
  133.6 1.7 bitcast_dynamic-update-slice_fusion.1
  135.3 3.7 %shard_map.85 = bf16[512,896]{1,0:T(8,128)(2,1)} custom-call(bf16[2,512,896]{2,1,0:T(8,128)(2,1)} %bitcast.119), custom_call_target="tpu_custom_call" | custom-call | tf_op jit(solution)/shard_map/pallas_call | solution.py:143
  139.0 1.3 dynamic-slice_bitcast_fusion.1
  140.3 5.8 %fusion.8 = f32[512,1024]{1,0:T(8,128)} fusion(bf16[512,896]{1,0:T(8,128)(2,1)} %shard_map.85, bf16[512,896]{1,0:T(8,128)(2,1)S(1)} %dynamic-slice_bitcast_fusion.1, bf16[896,1024]{1,0:T(8,128)(2,1)} %shard_map.79, bf16[896,1024]{1,0:T(8,128)(2,1)} %x_ref.1), kind=kOutput, calls=%fused_computation.10 | convolution fusion | flops 1890058240 | bytes 7602176 | tf_op jit(solution)/shard_map/dot_general | solution.py:232
  146.1 31.2 %shard_map.87 = bf16[2,8,2,32,896]{4,3,2,1,0:T(8,128)(2,1)} custom-call(bf16[4,2,2,1,32,896]{5,4,3,2,1,0:T(8,128)(2,1)} %bitcast.107), custom_call_target="tpu_custom_call" | custom-call | bytes 3670016 | tf_op jit(solution)/shard_map/pallas_call | solution.py:106
  177.3 1.7 bitcast_dynamic-update-slice_fusion
  179.0 3.7 %shard_map.88 = bf16[512,896]{1,0:T(8,128)(2,1)} custom-call(bf16[2,512,896]{2,1,0:T(8,128)(2,1)} %bitcast.110), custom_call_target="tpu_custom_call" | custom-call | tf_op jit(solution)/shard_map/pallas_call | solution.py:143
  182.7 1.3 dynamic-slice_bitcast_fusion
  184.0 1.0 copy-done.5
  185.0 5.8 %fusion.12 = f32[512,1024]{1,0:T(8,128)} fusion(bf16[512,896]{1,0:T(8,128)(2,1)} %shard_map.88, bf16[512,896]{1,0:T(8,128)(2,1)S(1)} %dynamic-slice_bitcast_fusion, bf16[896,1024]{1,0:T(8,128)(2,1)} %shard_map.79, bf16[896,1024]{1,0:T(8,128)(2,1)} %x_ref.1), kind=kOutput, calls=%fused_computation.14 | convolution fusion | flops 1890058240 | bytes 7602176 | tf_op jit(solution)/shard_map/dot_general | solution.py:232
  191.6 5.1 %all-to-all-start = ((bf16[16,8,1024]{2,0,1:T(8,128)(2,1)}), bf16[16,8,1024]{2,0,1:T(8,128)(2,1)S(1)}, u32[]{:S(2)}, u32[]{:S(2)}) async-start(bf16[16,8,1024]{2,0,1:T(8,128)(2,1)} %bitcast.98), calls=%async_computation.4 | async-start | bytes 524288 | tf_op jit(solution)/shard_map/all_to_all | solution.py:239
  196.9 7.3 %shard_map.80 = f32[32,1024]{1,0:T(8,128)} custom-call(f32[2,32,1024]{2,1,0:T(8,128)} %bitcast.133), custom_call_target="tpu_custom_call" | custom-call | tf_op jit(solution)/shard_map/pallas_call | solution.py:143
  204.2 5.8 %shard_map.83 = f32[32,1024]{1,0:T(8,128)} custom-call(f32[2,32,1024]{2,1,0:T(8,128)} %bitcast.135), custom_call_target="tpu_custom_call" | custom-call | tf_op jit(solution)/shard_map/pallas_call | solution.py:143
  210.0 6.0 %shard_map.86 = f32[32,1024]{1,0:T(8,128)} custom-call(f32[2,32,1024]{2,1,0:T(8,128)} %bitcast.137), custom_call_target="tpu_custom_call" | custom-call | tf_op jit(solution)/shard_map/pallas_call | solution.py:143
  216.0 1.0 bitcast_add_fusion.3
  217.0 1.0 bitcast_add_fusion.2
  218.0 1.0 bitcast_add_fusion.1
  219.0 11.8 %reduce-scatter.11.cloned.1.call-done = f32[64,1024]{1,0:T(8,128)} async-done(((f32[512,1024]{1,0:T(8,128)}), f32[64,1024]{1,0:T(8,128)}) %reduce-scatter.11.cloned.1.call-update) | async-done | bytes 262160 | tf_op jit(solution)/shard_map/reduce_scatter | solution.py:233
  230.9 5.7 %shard_map.89 = f32[32,1024]{1,0:T(8,128)} custom-call(f32[2,32,1024]{2,1,0:T(8,128)} %bitcast.139), custom_call_target="tpu_custom_call" | custom-call | tf_op jit(solution)/shard_map/pallas_call | solution.py:143
  236.5 1.0 bitcast_add_fusion
  237.5 1.9 fusion.31
  239.5 7.1 %shard_map.90 = bf16[128,1024]{1,0:T(8,128)(2,1)} custom-call(bf16[128,1024]{1,0:T(8,128)(2,1)} %get-tuple-element.16.x_ref), custom_call_target="tpu_custom_call" | custom-call | tf_op jit(solution)/shard_map/pallas_call | solution.py:143
  246.5 2.2 maximum_select_fusion.x_ref
  248.8 49.2 %shard_map.91 = bf16[8,256,1024]{2,1,0:T(8,128)(2,1)} custom-call(bf16[256,1024]{1,0:T(8,128)(2,1)} %maximum_select_fusion.x_ref), custom_call_target="tpu_custom_call" | custom-call | tf_op jit(solution)/shard_map/pallas_call | solution.py:199
  298.0 1.0 fusion.27
  299.0 17.4 %shard_map.92 = bf16[2048,1024]{1,0:T(8,128)(2,1)} custom-call(bf16[2048,1024]{1,0:T(8,128)(2,1)} %bitcast.99), custom_call_target="tpu_custom_call" | custom-call | tf_op jit(solution)/shard_map/pallas_call | solution.py:143
  316.4 2.8 fusion.42
  319.2 3.0 fusion.17
  322.2 2.9 fusion.19
  325.1 2.9 fusion.21
  329.2 1.1 fusion.47
  330.4 1.1 fusion.44
  331.5 1.2 fusion.46
  332.7 1.2 fusion.45
  334.2 8.6 %add_add_fusion = f32[896,1024]{1,0:T(8,128)} fusion(f32[896,1024]{1,0:T(8,128)S(1)} %fusion.47, f32[896,1024]{1,0:T(8,128)} %fusion.17, f32[896,1024]{1,0:T(8,128)S(1)} %fusion.46, f32[896,1024]{1,0:T(8,128)} %fusion.19, f32[896,1024]{1,0:T(8,128)S(1)} %fusion.45, f32[896,1024]{1,0:T(8,128)S(1)} %fusion.44, f32[896,1024]{1,0:T(8,128)} %fusion.21, ...), kind=kOutput, calls=%fused_computation.1 | convolution fusion | flops 945946624 | bytes 31326212 | tf_op jit(solution)/shard_map/dot_general | solution.py:265
  (44 shorter events, 2.7 us)
Async XLA Ops:
  7.2 189.7 %reduce-scatter.5.cloned.1.call-start = ((), (), s32[]{:S(2)}) async-start(), calls=%async_computation.5 | async-start | bytes 2359296 | tf_op jit(solution)/shard_map/reduce_scatter | solution.py:233
  13.9 39.5 %copy-start.9 = (bf16[896,1024]{1,0:T(8,128)(2,1)S(1)}, bf16[896,1024]{1,0:T(8,128)(2,1)}, u32[]{:S(2)}) copy-start(bf16[896,1024]{1,0:T(8,128)(2,1)} %x_ref.1) | copy-start | bytes 5505028
  58.6 145.5 %reduce-scatter.7.cloned.1.call-start = ((), (), s32[]{:S(2)}) async-start(), calls=%async_computation.6 | async-start | bytes 2359296 | tf_op jit(solution)/shard_map/reduce_scatter | solution.py:233
  102.3 107.7 %reduce-scatter.9.cloned.1.call-start = ((), (), s32[]{:S(2)}) async-start(), calls=%async_computation.7 | async-start | bytes 2359296 | tf_op jit(solution)/shard_map/reduce_scatter | solution.py:233
  146.1 84.8 %reduce-scatter.11.cloned.1.call-start = ((), (), s32[]{:S(2)}) async-start(), calls=%async_computation.8 | async-start | bytes 2359296 | tf_op jit(solution)/shard_map/reduce_scatter | solution.py:233
  184.0 1.0 copy-start.5
  185.0 5.9 %copy-start.10 = (bf16[16,8192]{1,0:T(8,128)(2,1)S(1)}, bf16[16,8192]{1,0:T(8,128)(2,1)}, u32[]{:S(2)}) copy-start(bf16[16,8192]{1,0:T(8,128)(2,1)} %param.9) | copy-start | bytes 786436
  185.0 11.7 %copy-start.11 = (bf16[1024]{0:T(1024)(128)(2,1)S(1)}, bf16[1024]{0:T(1024)(128)(2,1)}, u32[]{:S(2)}) copy-start(bf16[1024]{0:T(1024)(128)(2,1)} %param.10) | copy-start | bytes 6148
  185.0 11.8 %copy-start.12 = (s32[16]{0:T(128)S(1)}, s32[16]{0:T(128)}, u32[]{:S(2)}) copy-start(s32[16]{0:T(128)} %param.11) | copy-start | bytes 196
  191.6 45.9 %all-to-all-start = ((bf16[16,8,1024]{2,0,1:T(8,128)(2,1)}), bf16[16,8,1024]{2,0,1:T(8,128)(2,1)S(1)}, u32[]{:S(2)}, u32[]{:S(2)}) async-start(bf16[16,8,1024]{2,0,1:T(8,128)(2,1)} %bitcast.98), calls=%async_computation.4 | async-start | bytes 524288 | tf_op jit(solution)/shard_map/all_to_all | solution.py:239
  239.5 58.5 %copy-start.7 = (bf16[128,1024]{1,0:T(8,128)(2,1)S(1)}, bf16[128,1024]{1,0:T(8,128)(2,1)}, u32[]{:S(2)}) copy-start(bf16[128,1024]{1,0:T(8,128)(2,1)} %get-tuple-element.16.x_ref) | copy-start | bytes 786436
  246.5 51.4 %copy-start.8 = (bf16[128,1024]{1,0:T(8,128)(2,1)S(1)}, bf16[128,1024]{1,0:T(8,128)(2,1)}, u32[]{:S(2)}) copy-start(bf16[128,1024]{1,0:T(8,128)(2,1)} %shard_map.90) | copy-start | bytes 786436
  316.3 2.8 copy-start.4
  319.2 3.0 copy-start.3
  322.2 2.9 copy-start.2
  325.1 2.9 copy-start
  328.1 1.2 copy-start.6
  332.7 1.5 copy-start.1
Sparse Core Ops, SparseCore 0:
  58.8 40.2 reduce-scatter.4
  102.5 40.2 reduce-scatter.6
  146.2 40.1 reduce-scatter.8
  191.0 39.8 reduce-scatter.10

commit v15 on v11

--- a/solution.py
+++ b/solution.py
@@ -60,8 +60,13 @@
         arrival.wait_recv()
 
 
-def placed_gather_kernel(n, n_zhi, part, x_ref, out_ref, send_sem, recv_sem):
+def placed_gather_kernel(n, n_zhi, part, with_w, *refs):
+    if with_w:
+        x_ref, w_ref, out_ref, w_out, send_sem, recv_sem, w_sem = refs
+    else:
+        x_ref, out_ref, send_sem, recv_sem = refs
     me = lax.axis_index("shard")
+    partner = device_on("core", 1 - lax.axis_index("core"))
 
     def where(j):
         return out_ref.at[:, pl.ds(2 * lax.rem(j, n_zhi), 2), pl.ds(j // n_zhi, 1)]
@@ -70,8 +75,20 @@
     for off in range(1, n):
         peer = lax.rem(me + off, n)
         pl.semaphore_signal(barrier, inc=1, device_id=device_on("shard", peer), device_id_type=MESH)
-    pl.semaphore_wait(barrier, n - 1)
-
+    if with_w:
+        pl.semaphore_signal(barrier, inc=1, device_id=partner, device_id_type=MESH)
+    pl.semaphore_wait(barrier, n if with_w else n - 1)
+
+    if with_w:
+        w_copy = pltpu.make_async_remote_copy(
+            src_ref=w_ref,
+            dst_ref=w_out,
+            send_sem=w_sem.at[0],
+            recv_sem=w_sem.at[1],
+            device_id=partner,
+            device_id_type=MESH,
+        )
+        w_copy.start()
     copies = []
     for off in range(1, n):
         peer = lax.rem(me + off, n)
@@ -98,25 +115,35 @@
             device_id_type=MESH,
         )
         arrival.wait_recv()
-
-
-def gather_part(xt, part, collective_id, out_dims):
+    if with_w:
+        w_copy.wait()
+
+
+def gather_part(xt, part, collective_id, out_dims, w=None):
     n = lax.axis_size("shard")
     n_zhi = out_dims[1] // 2
-    received = pl.pallas_call(
-        functools.partial(placed_gather_kernel, n, n_zhi, part),
-        out_shape=jax.ShapeDtypeStruct(out_dims, xt.dtype),
-        in_specs=[pl.BlockSpec(memory_space=pl.ANY)],
-        out_specs=pl.BlockSpec(memory_space=pl.ANY),
-        scratch_shapes=[pltpu.SemaphoreType.DMA((n - 1,)), pltpu.SemaphoreType.DMA((n,))],
+    with_w = w is not None
+    operands = (xt, w) if with_w else (xt,)
+    out_shape = [jax.ShapeDtypeStruct(out_dims, xt.dtype)]
+    scratch = [pltpu.SemaphoreType.DMA((n - 1,)), pltpu.SemaphoreType.DMA((n,))]
+    if with_w:
+        out_shape.append(jax.ShapeDtypeStruct(w.shape, w.dtype))
+        scratch.append(pltpu.SemaphoreType.DMA((2,)))
+    results = pl.pallas_call(
+        functools.partial(placed_gather_kernel, n, n_zhi, part, with_w),
+        out_shape=tuple(out_shape),
+        in_specs=[pl.BlockSpec(memory_space=pl.ANY)] * len(operands),
+        out_specs=tuple(pl.BlockSpec(memory_space=pl.ANY) for _ in out_shape),
+        scratch_shapes=scratch,
         compiler_params=pltpu.CompilerParams(collective_id=collective_id, has_side_effects=True),
         cost_estimate=pl.CostEstimate(
             flops=0, bytes_accessed=2 * n * xt[part].nbytes, transcendentals=0
         ),
-    )(xt)
+    )(*operands)
     me = lax.axis_index("shard")
     at = (0, 2 * lax.rem(me, n_zhi), me // n_zhi, 0, 0)
-    return lax.dynamic_update_slice(received, xt[part], at)
+    whole = lax.dynamic_update_slice(results[0], xt[part], at)
+    return (whole, results[1]) if with_w else whole
 
 
 def swap_kernel(axis, halves, x_ref, out_ref, send_sem, recv_sem):
@@ -220,11 +247,14 @@
     me_yh = lax.axis_index("yh")
     xt = hidden.reshape(blocks // n_c, n_c, n_parts, 1, sub, ff_rows).transpose(2, 1, 0, 3, 4, 5)
     hp_parts, mlp_parts = [], []
-    pair_w = jnp.concatenate([w_down, swap_with_partner(w_down, 9, False)], axis=0)
     for part in range(n_parts):
         if part > 0:
             xt, _ = lax.optimization_barrier((xt, reduced))
-        got = gather_part(xt, part, 2 * part, (n_c, n_z, n_yh, sub, ff_rows))
+        if part == 0:
+            got, partner_w = gather_part(xt, part, 0, (n_c, n_z, n_yh, sub, ff_rows), w_down)
+            pair_w = jnp.concatenate([w_down, partner_w], axis=0)
+        else:
+            got = gather_part(xt, part, 2 * part, (n_c, n_z, n_yh, sub, ff_rows))
         hp = got.reshape(n_c, n_z * n_yh * sub, ff_rows)
         hp_parts.append(hp)
         from_partner = swap_with_partner(hp, 2 * part + 1, True)

time: 335 us -> 335 us (level)
  Pallas kernels: 228 us -> 221 us
    pallas_call x7 -> x6, Pallas kernels: 56.3 us -> 49.3 us  [swap_with_partner(): pl.pallas_call(functools.partial(swap_kernel, axis, halves), out_shape=ja...]
  transfers between devices with their start and end apart: 3 -> 3, of which waited for: 1 -> 1; matrix products, arithmetic and copies ran while one was open for 4% -> 4% of each run, Pallas kernels for 27% -> 26%
where the time goes in v15:
time: 335 us; the launch traced here: 334 us
  Pallas kernels  221 us (66%)
  waiting for transfers between devices  41.9 us (13%)
  matrix products  26 us (8%)
  local copies, waits for them, and re-layouts  19 us (6%)
  between operations  14.4 us (4%)
  other arithmetic  6.4 us (2%)
  starting transfers between devices  5.22 us (2%)
    pallas_call x2, Pallas kernels, gather_part(): pl.pallas_call(functools.partial(placed_gather_kernel, n, n_zhi, part, wi...  128 us
    pallas_call x6, Pallas kernels, swap_with_partner(): pl.pallas_call(functools.partial(swap_kernel, axis, halves), out_shape=ja...  49.3 us
    pallas_call x1, Pallas kernels, ring_gather(): pl.pallas_call(functools.partial(ring_gather_kernel, axis, n), out_shape=...  43.9 us
    reduce_scatter x2, waiting for transfers between devices, per_device(): reduced_z = lax.psum_scatter(reduced, 'z', scatter_dimension=0, tiled=True)  41.9 us
    dot_general x2, matrix products, per_device(): reduced = jnp.dot(pair_rows, pair_w, preferred_element_type=jnp.float32)  15.1 us
    dot_general x4, matrix products, per_device(): lax.dot_general(lax.dynamic_index_in_dim(hp_parts[part], rows, keepdims=F...  10.9 us
  transfers between devices with their start and end apart: 3, of which 1 were waited for; matrix products, arithmetic and copies ran while one was open for 4% of the time, Pallas kernels for 26%

profile of v15, /device:TPU:29, one launch (start us, length us, event | category | flops | bytes accessed | tf_op | source)
XLA Modules:
  0.0 333.6 jit_solution(10022222296827793629)
XLA Ops:
  7.2 0.0 reduce-scatter.3.cloned.1.call-start
  7.2 2.2 copy.22
  9.4 3.0 constant_dynamic-update-slice_fusion.1
  12.4 64.3 %shard_map.77 = (bf16[2,8,2,64,896]{4,3,2,1,0:T(8,128)(2,1)}, bf16[896,1024]{1,0:T(8,128)(2,1)}) custom-call(bf16[2,2,2,1,64,896]{5,4,3,2,1,0:T(8,128)(2,1)} %bitcast.71, bf16[896,1024]{1,0:T(8,128)(2,1)} %refs_1_.1), custom_call_target="tpu_custom_call" | custom-call | bytes 7340032 | tf_op jit(solution)/shard_map/pallas_call | solution.py:132
  76.7 0.8 fusion.19
  77.5 5.3 %shard_map.78 = bf16[1024,896]{1,0:T(8,128)(2,1)} custom-call(bf16[2,1024,896]{2,1,0:T(8,128)(2,1)} %bitcast.76), custom_call_target="tpu_custom_call" | custom-call | tf_op jit(solution)/shard_map/pallas_call | solution.py:170
  82.8 1.8 dynamic-slice_bitcast_fusion.1
  84.6 1.5 constant_dynamic-update-slice_fusion
  86.1 0.3 copy-done.8
  86.4 0.0 copy-done.10
  86.4 7.5 %fusion = f32[1024,1024]{1,0:T(8,128)} fusion(bf16[1792,1024]{1,0:T(8,128)(2,1)} %constant_dynamic-update-slice_fusion, bf16[1024,896]{1,0:T(8,128)(2,1)S(1)} %copy-done.10, bf16[1024,896]{1,0:T(8,128)(2,1)S(1)} %dynamic-slice_bitcast_fusion.1), kind=kOutput, calls=%fused_computation | convolution fusion | flops 3765436416 | bytes 11534336 | tf_op jit(solution)/shard_map/dot_general | solution.py:262
  94.0 0.0 reduce-scatter.3.cloned.1.call-update
  94.0 0.0 reduce-scatter.5.cloned.1.call-start
  94.0 63.3 %shard_map.80 = bf16[2,8,2,64,896]{4,3,2,1,0:T(8,128)(2,1)} custom-call(bf16[2,2,2,1,64,896]{5,4,3,2,1,0:T(8,128)(2,1)} %bitcast.72), custom_call_target="tpu_custom_call" | custom-call | bytes 7340032 | tf_op jit(solution)/shard_map/pallas_call | solution.py:132
  157.3 0.9 bitcast_dynamic-update-slice_fusion
  158.2 5.0 %shard_map.81 = bf16[1024,896]{1,0:T(8,128)(2,1)} custom-call(bf16[2,1024,896]{2,1,0:T(8,128)(2,1)} %bitcast.67), custom_call_target="tpu_custom_call" | custom-call | tf_op jit(solution)/shard_map/pallas_call | solution.py:170
  163.2 1.8 dynamic-slice_bitcast_fusion
  165.0 0.3 copy-done.11
  165.3 7.6 %fusion.4 = f32[1024,1024]{1,0:T(8,128)} fusion(bf16[1792,1024]{1,0:T(8,128)(2,1)} %constant_dynamic-update-slice_fusion, bf16[1024,896]{1,0:T(8,128)(2,1)S(1)} %copy-done.11, bf16[1024,896]{1,0:T(8,128)(2,1)S(1)} %dynamic-slice_bitcast_fusion), kind=kOutput, calls=%fused_computation.4 | convolution fusion | flops 3765436416 | bytes 11534336 | tf_op jit(solution)/shard_map/dot_general | solution.py:262
  172.8 0.0 reduce-scatter.5.cloned.1.call-update
  172.9 0.9 copy-done.12
  173.8 0.7 copy.23
  174.5 5.1 %all-to-all-start = ((bf16[16,8,1024]{2,0,1:T(8,128)(2,1)}), bf16[16,8,1024]{2,0,1:T(8,128)(2,1)S(1)}, u32[]{:S(2)}, u32[]{:S(2)}) async-start(bf16[16,8,1024]{2,0,1:T(8,128)(2,1)} %bitcast.64), calls=%async_computation.2 | async-start | bytes 524288 | tf_op jit(solution)/shard_map/all_to_all | solution.py:269
  179.7 0.1 select_reduce_fusion
  179.8 0.0 reduce-scatter.3.cloned.1.call-done
  179.8 8.9 %shard_map.79 = f32[64,1024]{1,0:T(8,128)} custom-call(f32[2,64,1024]{2,1,0:T(8,128)} %bitcast.84), custom_call_target="tpu_custom_call" | custom-call | tf_op jit(solution)/shard_map/pallas_call | solution.py:170
  188.7 41.9 %reduce-scatter.5.cloned.1.call-done = f32[128,1024]{1,0:T(8,128)} async-done(((f32[1024,1024]{1,0:T(8,128)}), f32[128,1024]{1,0:T(8,128)}) %reduce-scatter.5.cloned.1.call-update) | async-done | bytes 524304 | tf_op jit(solution)/shard_map/reduce_scatter | solution.py:263
  230.5 9.1 %shard_map.82 = f32[64,1024]{1,0:T(8,128)} custom-call(f32[2,64,1024]{2,1,0:T(8,128)} %bitcast.86), custom_call_target="tpu_custom_call" | custom-call | tf_op jit(solution)/shard_map/pallas_call | solution.py:170
  239.6 1.1 bitcast_add_fusion.1
  240.7 1.1 bitcast_add_fusion
  241.7 0.0 all-to-all-done
  241.8 1.0 fusion.18
  242.7 8.1 %shard_map.83 = bf16[128,1024]{1,0:T(8,128)(2,1)} custom-call(bf16[128,1024]{1,0:T(8,128)(2,1)} %get-tuple-element.12.x_ref), custom_call_target="tpu_custom_call" | custom-call | tf_op jit(solution)/shard_map/pallas_call | solution.py:170
  250.9 2.2 maximum_select_fusion.x_ref
  253.1 43.9 %shard_map.84 = bf16[8,256,1024]{2,1,0:T(8,128)(2,1)} custom-call(bf16[256,1024]{1,0:T(8,128)(2,1)} %maximum_select_fusion.x_ref), custom_call_target="tpu_custom_call" | custom-call | tf_op jit(solution)/shard_map/pallas_call | solution.py:226
  297.1 0.0 copy-done.5
  297.1 0.0 copy-done.6
  297.1 0.9 fusion.14
  298.0 12.9 %shard_map.85 = bf16[2048,1024]{1,0:T(8,128)(2,1)} custom-call(bf16[2048,1024]{1,0:T(8,128)(2,1)} %bitcast.65), custom_call_target="tpu_custom_call" | custom-call | tf_op jit(solution)/shard_map/pallas_call | solution.py:170
  311.0 2.9 fusion.26
  313.9 0.4 copy-done.4
  314.3 2.1 fusion.10
  316.4 2.1 fusion.8
  318.6 0.0 copy-done
  318.6 0.7 fusion.25
  319.3 0.8 copy-done.9
  320.1 2.1 fusion.27
  322.2 4.5 %add_add_fusion = f32[896,1024]{1,0:T(8,128)} fusion(f32[896,1024]{1,0:T(8,128)S(1)} %fusion.8, f32[896,1024]{1,0:T(8,128)S(1)} %fusion.27, f32[896,1024]{1,0:T(8,128)S(1)} %fusion.10, bf16[1024,896]{1,0:T(8,128)(2,1)S(1)} %dynamic-slice_bitcast_fusion, bf16[1024,1024]{1,0:T(8,128)(2,1)S(1)} %bitcast.75), kind=kOutput, calls=%fused_computation.8 | convolution fusion | flops 1881800704 | bytes 18612224 | tf_op jit(solution)/shard_map/dot_general | solution.py:295
  (27 shorter events, 0.1 us)
Async XLA Ops:
  7.2 172.6 %reduce-scatter.3.cloned.1.call-start = ((), (), s32[]{:S(2)}) async-start(), calls=%async_computation.3 | async-start | bytes 4718592 | tf_op jit(solution)/shard_map/reduce_scatter | solution.py:263
  9.4 67.3 %copy-start.2 = (bf16[2,2,2,1,64,896]{5,4,3,0,1,2:T(8,128)(2,1)S(1)}, bf16[2,2,2,1,64,896]{5,4,3,0,1,2:T(8,128)(2,1)}, u32[]{:S(2)}) copy-start(bf16[2,2,2,1,64,896]{5,4,3,0,1,2:T(8,128)(2,1)} %copy.22) | copy-start | bytes 2752516
  77.5 7.1 %copy-start.7 = (bf16[896,1024]{1,0:T(8,128)(2,1)S(1)}, bf16[896,1024]{1,0:T(8,128)(2,1)}, u32[]{:S(2)}) copy-start(bf16[896,1024]{1,0:T(8,128)(2,1)} %get-tuple-element.6) | copy-start | bytes 5505028
  82.8 3.6 %copy-start.10 = (bf16[1024,896]{1,0:T(8,128)(2,1)S(1)}, bf16[1024,896]{1,0:T(8,128)(2,1)}, u32[]{:S(2)}) copy-start(bf16[1024,896]{1,0:T(8,128)(2,1)} %shard_map.78) | copy-start | bytes 5505028
  84.6 1.8 copy-start.8
  94.0 63.3 %copy-start.3 = (bf16[2,2,2,1,64,896]{5,4,3,0,1,2:T(8,128)(2,1)S(1)}, bf16[2,2,2,1,64,896]{5,4,3,0,1,2:T(8,128)(2,1)}, u32[]{:S(2)}) copy-start(bf16[2,2,2,1,64,896]{5,4,3,0,1,2:T(8,128)(2,1)} %copy.22) | copy-start | bytes 2752516
  94.0 136.5 %reduce-scatter.5.cloned.1.call-start = ((), (), s32[]{:S(2)}) async-start(), calls=%async_computation.4 | async-start | bytes 4718592 | tf_op jit(solution)/shard_map/reduce_scatter | solution.py:263
  163.2 2.1 copy-start.11
  172.8 0.9 copy-start.12
  172.8 6.8 %copy-start.14 = (bf16[1024]{0:T(1024)(128)(2,1)S(1)}, bf16[1024]{0:T(1024)(128)(2,1)}, u32[]{:S(2)}) copy-start(bf16[1024]{0:T(1024)(128)(2,1)} %param.10) | copy-start | bytes 6148
  172.8 6.8 %copy-start.15 = (s32[16]{0:T(128)S(1)}, s32[16]{0:T(128)}, u32[]{:S(2)}) copy-start(s32[16]{0:T(128)} %param.11) | copy-start | bytes 196
  172.8 68.9 %copy-start.13 = (bf16[128,1024]{1,0:T(8,128)(2,1)S(1)}, bf16[128,1024]{1,0:T(8,128)(2,1)}, u32[]{:S(2)}) copy-start(bf16[128,1024]{1,0:T(8,128)(2,1)} %param.6) | copy-start | bytes 786436
  174.5 67.3 %all-to-all-start = ((bf16[16,8,1024]{2,0,1:T(8,128)(2,1)}), bf16[16,8,1024]{2,0,1:T(8,128)(2,1)S(1)}, u32[]{:S(2)}, u32[]{:S(2)}) async-start(bf16[16,8,1024]{2,0,1:T(8,128)(2,1)} %bitcast.64), calls=%async_computation.2 | async-start | bytes 524288 | tf_op jit(solution)/shard_map/all_to_all | solution.py:269
  242.7 54.3 %copy-start.5 = (bf16[128,1024]{1,0:T(8,128)(2,1)S(1)}, bf16[128,1024]{1,0:T(8,128)(2,1)}, u32[]{:S(2)}) copy-start(bf16[128,1024]{1,0:T(8,128)(2,1)} %get-tuple-element.12.x_ref) | copy-start | bytes 786436
  250.9 46.2 %copy-start.6 = (bf16[128,1024]{1,0:T(8,128)(2,1)S(1)}, bf16[128,1024]{1,0:T(8,128)(2,1)}, u32[]{:S(2)}) copy-start(bf16[128,1024]{1,0:T(8,128)(2,1)} %shard_map.83) | copy-start | bytes 786436
  311.0 3.3 copy-start.4
  314.3 2.1 copy-start.1
  316.4 2.2 copy-start
  318.6 1.5 copy-start.9
Sparse Core Ops, SparseCore 0:
  94.1 57.5 reduce-scatter.2
  173.0 57.5 reduce-scatter.4

commit v16 on v11

--- a/solution.py
+++ b/solution.py
@@ -150,14 +150,16 @@
     )(x)
 
 
-def ring_gather_kernel(axis, n, x_ref, out_ref, send_sem, recv_sem):
+def ring_gather_kernel(axis, n, x_ref, out_ref, pair_ref, send_sem, recv_sem, pair_send, pair_recv):
     me = lax.axis_index(axis)
     right, left = lax.rem(me + 1, n), lax.rem(me + n - 1, n)
+    partner = device_on("core", 1 - lax.axis_index("core"))
 
     barrier = pltpu.get_barrier_semaphore()
     for neighbour in (left, right):
         pl.semaphore_signal(barrier, inc=1, device_id=device_on(axis, neighbour), device_id_type=MESH)
-    pl.semaphore_wait(barrier, 2)
+    pl.semaphore_signal(barrier, inc=1, device_id=partner, device_id_type=MESH)
+    pl.semaphore_wait(barrier, 3)
 
     def arrival(slot):
         return pltpu.make_async_remote_copy(
@@ -169,7 +171,20 @@
             device_id_type=MESH,
         )
 
+    def to_partner(src, slot):
+        return pltpu.make_async_remote_copy(
+            src_ref=src,
+            dst_ref=pair_ref.at[slot],
+            send_sem=pair_send.at[slot],
+            recv_sem=pair_recv.at[slot],
+            device_id=partner,
+            device_id_type=MESH,
+        )
+
     copies = []
+    own = to_partner(x_ref, me)
+    own.start()
+    copies.append(own)
     steps = (n // 2, (n - 1) // 2)
     for k in range(max(steps)):
         for ring, (sign, target) in enumerate(((-1, right), (1, left))):
@@ -178,6 +193,9 @@
             slot = lax.rem(me + sign * k + n, n)
             if k > 0:
                 arrival(slot).wait_recv()
+                forward = to_partner(out_ref.at[slot], slot)
+                forward.start()
+                copies.append(forward)
             copy = pltpu.make_async_remote_copy(
                 src_ref=x_ref if k == 0 else out_ref.at[slot],
                 dst_ref=out_ref.at[slot],
@@ -188,24 +206,38 @@
             )
             copy.start()
             copies.append(copy)
-    arrival(lax.rem(me - steps[0] + n, n)).wait_recv()
-    arrival(lax.rem(me + steps[1], n)).wait_recv()
+    for slot in (lax.rem(me - steps[0] + n, n), lax.rem(me + steps[1], n)):
+        arrival(slot).wait_recv()
+        forward = to_partner(out_ref.at[slot], slot)
+        forward.start()
+        copies.append(forward)
     for copy in copies:
         copy.wait_send()
+    for slot in range(n):
+        to_partner(x_ref, slot).wait_recv()
 
 
 def ring_gather(x, axis, collective_id):
     n = lax.axis_size(axis)
-    received = pl.pallas_call(
+    received, from_partner = pl.pallas_call(
         functools.partial(ring_gather_kernel, axis, n),
-        out_shape=jax.ShapeDtypeStruct((n,) + x.shape, x.dtype),
+        out_shape=(
+            jax.ShapeDtypeStruct((n,) + x.shape, x.dtype),
+            jax.ShapeDtypeStruct((n,) + x.shape, x.dtype),
+        ),
         in_specs=[pl.BlockSpec(memory_space=pl.ANY)],
-        out_specs=pl.BlockSpec(memory_space=pl.ANY),
-        scratch_shapes=[pltpu.SemaphoreType.DMA((2, n // 2)), pltpu.SemaphoreType.DMA((n,))],
+        out_specs=(pl.BlockSpec(memory_space=pl.ANY), pl.BlockSpec(memory_space=pl.ANY)),
+        scratch_shapes=[
+            pltpu.SemaphoreType.DMA((2, n // 2)),
+            pltpu.SemaphoreType.DMA((n,)),
+            pltpu.SemaphoreType.DMA((n,)),
+            pltpu.SemaphoreType.DMA((n,)),
+        ],
         compiler_params=pltpu.CompilerParams(collective_id=collective_id, has_side_effects=True),
     )(x)
     whole = lax.dynamic_update_index_in_dim(received, x, lax.axis_index(axis), 0)
-    return whole.reshape((n * x.shape[0],) + x.shape[1:])
+    rows = (n * x.shape[0],) + x.shape[1:]
+    return whole.reshape(rows), from_partner.reshape(rows)
 
 
 def per_device(resid_in, hidden, w_down, frozen, steer, forget_flags):
@@ -255,8 +287,7 @@
         jnp.concatenate([slopes, other_yh], axis=0),
         jnp.concatenate([other_yh, slopes], axis=0),
     )
-    gathered = ring_gather(gathered, "z", 10)
-    partner_slopes = swap_with_partner(gathered, 2 * n_parts + 1, False)
+    gathered, partner_slopes = ring_gather(gathered, "z", 10)
     contract = (((0,), (0,)), ((), ()))
     grad_down = None
     for part in range(n_parts):

time: 335 us -> 333 us (level)
    pallas_call x7 -> x6, Pallas kernels: 56.3 us -> 43.4 us  [swap_with_partner(): pl.pallas_call(functools.partial(swap_kernel, axis, halves), out_shape=ja...]
    pallas_call x1, Pallas kernels: 43.9 us -> 56 us  [ring_gather(): pl.pallas_call(functools.partial(ring_gather_kernel, axis, n), out_shape=...]
where the time goes in v16:
time: 333 us; the launch traced here: 332 us
  Pallas kernels  228 us (68%)
  waiting for transfers between devices  39.1 us (12%)
  matrix products  24.3 us (7%)
  local copies, waits for them, and re-layouts  16 us (5%)
  between operations  14.4 us (4%)
  other arithmetic  5.55 us (2%)
  starting transfers between devices  5.22 us (2%)
    pallas_call x2, Pallas kernels, gather_part(): pl.pallas_call(functools.partial(placed_gather_kernel, n, n_zhi, part), o...  128 us
    pallas_call x1, Pallas kernels, ring_gather(): pl.pallas_call(functools.partial(ring_gather_kernel, axis, n), out_shape=...  56 us
    pallas_call x6, Pallas kernels, swap_with_partner(): pl.pallas_call(functools.partial(swap_kernel, axis, halves), out_shape=ja...  43.4 us
    reduce_scatter x2, waiting for transfers between devices, per_device(): reduced_z = lax.psum_scatter(reduced, 'z', scatter_dimension=0, tiled=True)  39.1 us
    dot_general x2, matrix products, per_device(): reduced = jnp.dot(pair_rows, pair_w, preferred_element_type=jnp.float32)  13.4 us
    dot_general x4, matrix products, per_device(): lax.dot_general(lax.dynamic_index_in_dim(hp_parts[part], rows, keepdims=F...  10.9 us
  transfers between devices with their start and end apart: 3, of which 1 were waited for; matrix products, arithmetic and copies ran while one was open for 4% of the time, Pallas kernels for 27%

profile of v16, /device:TPU:29, one launch (start us, length us, event | category | flops | bytes accessed | tf_op | source)
XLA Modules:
  0.0 332.0 jit_solution(12559127901199669077)
XLA Ops:
  7.2 0.0 reduce-scatter.3.cloned.1.call-start
  7.2 2.2 copy.22
  9.4 4.4 %shard_map.79 = bf16[896,1024]{1,0:T(8,128)(2,1)} custom-call(bf16[896,1024]{1,0:T(8,128)(2,1)} %x_ref.1), custom_call_target="tpu_custom_call" | custom-call | tf_op jit(solution)/shard_map/pallas_call | solution.py:143
  13.9 64.9 %shard_map.77 = bf16[2,8,2,64,896]{4,3,2,1,0:T(8,128)(2,1)} custom-call(bf16[2,2,2,1,64,896]{5,4,3,2,1,0:T(8,128)(2,1)} %bitcast.68), custom_call_target="tpu_custom_call" | custom-call | bytes 7340032 | tf_op jit(solution)/shard_map/pallas_call | solution.py:106
  78.8 0.8 fusion.19
  79.6 5.0 %shard_map.78 = bf16[1024,896]{1,0:T(8,128)(2,1)} custom-call(bf16[2,1024,896]{2,1,0:T(8,128)(2,1)} %bitcast.62), custom_call_target="tpu_custom_call" | custom-call | tf_op jit(solution)/shard_map/pallas_call | solution.py:143
  84.7 1.8 dynamic-slice_bitcast_fusion.1
  86.5 0.0 copy-start.11
  86.5 1.2 copy-done.11
  87.7 5.9 %fusion = f32[1024,1024]{1,0:T(8,128)} fusion(bf16[1024,896]{1,0:T(8,128)(2,1)S(1)} %copy-done.13, bf16[1024,896]{1,0:T(8,128)(2,1)S(1)} %dynamic-slice_bitcast_fusion.1, bf16[896,1024]{1,0:T(8,128)(2,1)S(1)} %copy-done.9, bf16[896,1024]{1,0:T(8,128)(2,1)S(1)} %copy-done.7), kind=kOutput, calls=%fused_computation | convolution fusion | flops 3772776448 | bytes 11534336 | tf_op jit(solution)/shard_map/dot_general | solution.py:264
  93.6 0.0 reduce-scatter.3.cloned.1.call-update
  93.7 0.0 reduce-scatter.5.cloned.1.call-start
  93.7 63.3 %shard_map.81 = bf16[2,8,2,64,896]{4,3,2,1,0:T(8,128)(2,1)} custom-call(bf16[2,2,2,1,64,896]{5,4,3,2,1,0:T(8,128)(2,1)} %bitcast.69), custom_call_target="tpu_custom_call" | custom-call | bytes 7340032 | tf_op jit(solution)/shard_map/pallas_call | solution.py:106
  157.0 0.8 bitcast_dynamic-update-slice_fusion
  157.8 5.0 %shard_map.82 = bf16[1024,896]{1,0:T(8,128)(2,1)} custom-call(bf16[2,1024,896]{2,1,0:T(8,128)(2,1)} %bitcast.65), custom_call_target="tpu_custom_call" | custom-call | tf_op jit(solution)/shard_map/pallas_call | solution.py:143
  162.9 0.0 copy-start.8
  162.9 1.8 dynamic-slice_bitcast_fusion
  164.7 0.2 copy-done.8
  164.9 0.6 copy-done.10
  165.5 7.5 %fusion.4 = f32[1024,1024]{1,0:T(8,128)} fusion(bf16[1024,896]{1,0:T(8,128)(2,1)} %shard_map.82, bf16[1024,896]{1,0:T(8,128)(2,1)S(1)} %dynamic-slice_bitcast_fusion, bf16[896,1024]{1,0:T(8,128)(2,1)S(1)} %copy-done.10, bf16[896,1024]{1,0:T(8,128)(2,1)S(1)} %copy-done.8), kind=kOutput, calls=%fused_computation.5 | convolution fusion | flops 3772776448 | bytes 11534336 | tf_op jit(solution)/shard_map/dot_general | solution.py:264
  172.9 0.0 reduce-scatter.5.cloned.1.call-update
  173.0 0.9 copy-done.14
  173.9 0.7 copy.23
  174.6 5.1 %all-to-all-start = ((bf16[16,8,1024]{2,0,1:T(8,128)(2,1)}), bf16[16,8,1024]{2,0,1:T(8,128)(2,1)S(1)}, u32[]{:S(2)}, u32[]{:S(2)}) async-start(bf16[16,8,1024]{2,0,1:T(8,128)(2,1)} %bitcast.61), calls=%async_computation.2 | async-start | bytes 524288 | tf_op jit(solution)/shard_map/all_to_all | solution.py:271
  179.8 0.1 select_reduce_fusion
  179.9 0.0 reduce-scatter.3.cloned.1.call-done
  179.9 11.7 %shard_map.80 = f32[64,1024]{1,0:T(8,128)} custom-call(f32[2,64,1024]{2,1,0:T(8,128)} %bitcast.80), custom_call_target="tpu_custom_call" | custom-call | tf_op jit(solution)/shard_map/pallas_call | solution.py:143
  191.6 39.0 %reduce-scatter.5.cloned.1.call-done = f32[128,1024]{1,0:T(8,128)} async-done(((f32[1024,1024]{1,0:T(8,128)}), f32[128,1024]{1,0:T(8,128)}) %reduce-scatter.5.cloned.1.call-update) | async-done | bytes 524304 | tf_op jit(solution)/shard_map/reduce_scatter | solution.py:265
  230.6 9.1 %shard_map.83 = f32[64,1024]{1,0:T(8,128)} custom-call(f32[2,64,1024]{2,1,0:T(8,128)} %bitcast.82), custom_call_target="tpu_custom_call" | custom-call | tf_op jit(solution)/shard_map/pallas_call | solution.py:143
  239.7 1.1 bitcast_add_fusion.1
  240.8 1.1 bitcast_add_fusion
  241.9 1.0 fusion.18
  242.9 8.1 %shard_map.84 = bf16[128,1024]{1,0:T(8,128)(2,1)} custom-call(bf16[128,1024]{1,0:T(8,128)(2,1)} %get-tuple-element.12.x_ref), custom_call_target="tpu_custom_call" | custom-call | tf_op jit(solution)/shard_map/pallas_call | solution.py:143
  251.0 2.2 maximum_select_fusion.x_ref
  253.2 56.0 %shard_map.85 = (bf16[8,256,1024]{2,1,0:T(8,128)(2,1)}, bf16[8,256,1024]{2,1,0:T(8,128)(2,1)}) custom-call(bf16[256,1024]{1,0:T(8,128)(2,1)} %maximum_select_fusion.x_ref), custom_call_target="tpu_custom_call" | custom-call | tf_op jit(solution)/shard_map/pallas_call | solution.py:222
  309.2 2.9 fusion.26
  312.1 0.4 copy-done
  312.5 2.1 fusion.10
  314.6 2.1 fusion.8
  316.8 0.0 copy-done.4
  316.8 0.0 copy-done.5
  316.8 0.1 copy-done.6
  316.9 0.1 fusion.14
  317.1 0.0 copy-start.12
  317.1 0.7 fusion.25
  317.8 0.8 copy-done.12
  318.6 2.1 fusion.27
  320.7 4.5 %add_add_fusion = f32[896,1024]{1,0:T(8,128)} fusion(f32[896,1024]{1,0:T(8,128)S(1)} %fusion.8, f32[896,1024]{1,0:T(8,128)S(1)} %fusion.27, f32[896,1024]{1,0:T(8,128)S(1)} %fusion.10, bf16[1024,896]{1,0:T(8,128)(2,1)S(1)} %dynamic-slice_bitcast_fusion, bf16[1024,1024]{1,0:T(8,128)(2,1)S(1)} %bitcast.72), kind=kOutput, calls=%fused_computation.9 | convolution fusion | flops 1881800704 | bytes 18612224 | tf_op jit(solution)/shard_map/dot_general | solution.py:296
  (29 shorter events, 0.1 us)
Async XLA Ops:
  7.2 172.7 %reduce-scatter.3.cloned.1.call-start = ((), (), s32[]{:S(2)}) async-start(), calls=%async_computation.3 | async-start | bytes 4718592 | tf_op jit(solution)/shard_map/reduce_scatter | solution.py:265
  9.4 69.4 %copy-start.2 = (bf16[2,2,2,1,64,896]{5,4,3,0,1,2:T(8,128)(2,1)S(1)}, bf16[2,2,2,1,64,896]{5,4,3,0,1,2:T(8,128)(2,1)}, u32[]{:S(2)}) copy-start(bf16[2,2,2,1,64,896]{5,4,3,0,1,2:T(8,128)(2,1)} %copy.22) | copy-start | bytes 2752516
  79.6 8.1 %copy-start.7 = (bf16[896,1024]{1,0:T(8,128)(2,1)S(1)}, bf16[896,1024]{1,0:T(8,128)(2,1)}, u32[]{:S(2)}) copy-start(bf16[896,1024]{1,0:T(8,128)(2,1)} %x_ref.1) | copy-start | bytes 5505028
  84.7 3.1 copy-start.9
  84.7 3.1 copy-start.13
  86.5 1.2 copy-start.11
  93.6 63.3 %copy-start.3 = (bf16[2,2,2,1,64,896]{5,4,3,0,1,2:T(8,128)(2,1)S(1)}, bf16[2,2,2,1,64,896]{5,4,3,0,1,2:T(8,128)(2,1)}, u32[]{:S(2)}) copy-start(bf16[2,2,2,1,64,896]{5,4,3,0,1,2:T(8,128)(2,1)} %copy.22) | copy-start | bytes 2752516
  93.7 137.0 %reduce-scatter.5.cloned.1.call-start = ((), (), s32[]{:S(2)}) async-start(), calls=%async_computation.4 | async-start | bytes 4718592 | tf_op jit(solution)/shard_map/reduce_scatter | solution.py:265
  162.9 2.1 copy-start.8
  162.9 2.6 copy-start.10
  172.9 0.9 copy-start.14
  172.9 6.8 %copy-start.16 = (bf16[1024]{0:T(1024)(128)(2,1)S(1)}, bf16[1024]{0:T(1024)(128)(2,1)}, u32[]{:S(2)}) copy-start(bf16[1024]{0:T(1024)(128)(2,1)} %param.10) | copy-start | bytes 6148
  172.9 6.8 %copy-start.17 = (s32[16]{0:T(128)S(1)}, s32[16]{0:T(128)}, u32[]{:S(2)}) copy-start(s32[16]{0:T(128)} %param.11) | copy-start | bytes 196
  172.9 68.9 %copy-start.15 = (bf16[128,1024]{1,0:T(8,128)(2,1)S(1)}, bf16[128,1024]{1,0:T(8,128)(2,1)}, u32[]{:S(2)}) copy-start(bf16[128,1024]{1,0:T(8,128)(2,1)} %param.6) | copy-start | bytes 786436
  174.6 67.2 %all-to-all-start = ((bf16[16,8,1024]{2,0,1:T(8,128)(2,1)}), bf16[16,8,1024]{2,0,1:T(8,128)(2,1)S(1)}, u32[]{:S(2)}, u32[]{:S(2)}) async-start(bf16[16,8,1024]{2,0,1:T(8,128)(2,1)} %bitcast.61), calls=%async_computation.2 | async-start | bytes 524288 | tf_op jit(solution)/shard_map/all_to_all | solution.py:271
  309.2 3.3 copy-start
  312.5 2.1 copy-start.1
  314.6 2.2 copy-start.4
  314.6 2.2 copy-start.5
  314.6 2.3 copy-start.6
  317.1 1.5 copy-start.12
Sparse Core Ops, SparseCore 0:
  93.8 57.5 reduce-scatter.2
  173.1 57.5 reduce-scatter.4

commit v17 on v16

--- a/solution.py
+++ b/solution.py
@@ -58,6 +58,20 @@
             device_id_type=MESH,
         )
         arrival.wait_recv()
+
+
+def gather_along(x, axis, collective_id):
+    n = lax.axis_size(axis)
+    received = pl.pallas_call(
+        functools.partial(gather_kernel, axis, n, 0),
+        out_shape=jax.ShapeDtypeStruct((n,) + x.shape, x.dtype),
+        in_specs=[pl.BlockSpec(memory_space=pl.ANY)],
+        out_specs=pl.BlockSpec(memory_space=pl.ANY),
+        scratch_shapes=[pltpu.SemaphoreType.DMA((n - 1,)), pltpu.SemaphoreType.DMA((n,))],
+        compiler_params=pltpu.CompilerParams(collective_id=collective_id, has_side_effects=True),
+    )(x[None])
+    whole = lax.dynamic_update_index_in_dim(received, x, lax.axis_index(axis), 0)
+    return whole.reshape((n * x.shape[0],) + x.shape[1:])
 
 
 def placed_gather_kernel(n, n_zhi, part, x_ref, out_ref, send_sem, recv_sem):
@@ -281,12 +295,7 @@
     slopes = (loss_weight[:, None] * (residual - target) * (1.0 / math.sqrt(total_tokens))).astype(
         jnp.bfloat16
     )
-    other_yh = swap_with_partner(slopes, 6 + n_parts, False, "yh")
-    gathered = jnp.where(
-        me_yh == 0,
-        jnp.concatenate([slopes, other_yh], axis=0),
-        jnp.concatenate([other_yh, slopes], axis=0),
-    )
+    gathered = gather_along(slopes, "yh", 6 + n_parts)
     gathered, partner_slopes = ring_gather(gathered, "z", 10)
     contract = (((0,), (0,)), ((), ()))
     grad_down = None

time: 333 us -> 333 us (level)
    pallas_call x0 -> x1, Pallas kernels: none -> 8.15 us  [gather_along(): pl.pallas_call(functools.partial(gather_kernel, axis, n, 0), out_shape=ja...]
    pallas_call x6 -> x5, Pallas kernels: 43.4 us -> 35.2 us  [swap_with_partner(): pl.pallas_call(functools.partial(swap_kernel, axis, halves), out_shape=ja...]
where the time goes in v17:
time: 333 us; the launch traced here: 332 us
  Pallas kernels  228 us (68%)
  waiting for transfers between devices  39.1 us (12%)
  matrix products  24.2 us (7%)
  local copies, waits for them, and re-layouts  17.8 us (5%)
  between operations  14.4 us (4%)
  starting transfers between devices  5.22 us (2%)
    pallas_call x2, Pallas kernels, gather_part(): pl.pallas_call(functools.partial(placed_gather_kernel, n, n_zhi, part), o...  128 us
    pallas_call x1, Pallas kernels, ring_gather(): pl.pallas_call(functools.partial(ring_gather_kernel, axis, n), out_shape=...  56 us
    reduce_scatter x2, waiting for transfers between devices, per_device(): reduced_z = lax.psum_scatter(reduced, 'z', scatter_dimension=0, tiled=True)  39.1 us
    pallas_call x5, Pallas kernels, swap_with_partner(): pl.pallas_call(functools.partial(swap_kernel, axis, halves), out_shape=ja...  35.2 us
    dot_general x2, matrix products, per_device(): reduced = jnp.dot(pair_rows, pair_w, preferred_element_type=jnp.float32)  13.4 us
    dot_general x4, matrix products, per_device(): lax.dot_general(lax.dynamic_index_in_dim(hp_parts[part], rows, keepdims=F...  10.9 us
    pallas_call x1, Pallas kernels, gather_along(): pl.pallas_call(functools.partial(gather_kernel, axis, n, 0), out_shape=ja...  8.15 us
  transfers between devices with their start and end apart: 3, of which 1 were waited for; matrix products, arithmetic and copies ran while one was open for 4% of the time, Pallas kernels for 27%

profile of v17, /device:TPU:29, one launch (start us, length us, event | category | flops | bytes accessed | tf_op | source)
XLA Modules:
  0.0 331.5 jit_solution(13350209312910565600)
XLA Ops:
  7.2 0.0 reduce-scatter.3.cloned.1.call-start
  7.2 2.2 copy.22
  9.4 4.4 %shard_map.79 = bf16[896,1024]{1,0:T(8,128)(2,1)} custom-call(bf16[896,1024]{1,0:T(8,128)(2,1)} %x_ref.1), custom_call_target="tpu_custom_call" | custom-call | tf_op jit(solution)/shard_map/pallas_call | solution.py:157
  13.9 64.9 %shard_map.77 = bf16[2,8,2,64,896]{4,3,2,1,0:T(8,128)(2,1)} custom-call(bf16[2,2,2,1,64,896]{5,4,3,2,1,0:T(8,128)(2,1)} %bitcast.72), custom_call_target="tpu_custom_call" | custom-call | bytes 7340032 | tf_op jit(solution)/shard_map/pallas_call | solution.py:120
  78.8 0.8 fusion.18
  79.6 5.0 %shard_map.78 = bf16[1024,896]{1,0:T(8,128)(2,1)} custom-call(bf16[2,1024,896]{2,1,0:T(8,128)(2,1)} %bitcast.66), custom_call_target="tpu_custom_call" | custom-call | tf_op jit(solution)/shard_map/pallas_call | solution.py:157
  84.7 1.8 dynamic-slice_bitcast_fusion.1
  86.5 0.0 copy-start.10
  86.5 1.2 copy-done.10
  87.7 0.0 copy-done.6
  87.7 0.0 copy-done.12
  87.7 5.9 %fusion = f32[1024,1024]{1,0:T(8,128)} fusion(bf16[1024,896]{1,0:T(8,128)(2,1)S(1)} %copy-done.12, bf16[1024,896]{1,0:T(8,128)(2,1)S(1)} %dynamic-slice_bitcast_fusion.1, bf16[896,1024]{1,0:T(8,128)(2,1)S(1)} %copy-done.8, bf16[896,1024]{1,0:T(8,128)(2,1)S(1)} %copy-done.6), kind=kOutput, calls=%fused_computation | convolution fusion | flops 3772776448 | bytes 11534336 | tf_op jit(solution)/shard_map/dot_general | solution.py:278
  93.7 0.0 reduce-scatter.3.cloned.1.call-update
  93.7 0.0 reduce-scatter.5.cloned.1.call-start
  93.7 63.3 %shard_map.81 = bf16[2,8,2,64,896]{4,3,2,1,0:T(8,128)(2,1)} custom-call(bf16[2,2,2,1,64,896]{5,4,3,2,1,0:T(8,128)(2,1)} %bitcast.73), custom_call_target="tpu_custom_call" | custom-call | bytes 7340032 | tf_op jit(solution)/shard_map/pallas_call | solution.py:120
  157.0 0.9 bitcast_dynamic-update-slice_fusion.1
  157.9 5.0 %shard_map.82 = bf16[1024,896]{1,0:T(8,128)(2,1)} custom-call(bf16[2,1024,896]{2,1,0:T(8,128)(2,1)} %bitcast.69), custom_call_target="tpu_custom_call" | custom-call | tf_op jit(solution)/shard_map/pallas_call | solution.py:157
  162.9 0.0 copy-start.7
  162.9 1.8 dynamic-slice_bitcast_fusion
  164.7 0.2 copy-done.7
  165.0 0.6 copy-done.9
  165.5 7.5 %fusion.4 = f32[1024,1024]{1,0:T(8,128)} fusion(bf16[1024,896]{1,0:T(8,128)(2,1)} %shard_map.82, bf16[1024,896]{1,0:T(8,128)(2,1)S(1)} %dynamic-slice_bitcast_fusion, bf16[896,1024]{1,0:T(8,128)(2,1)S(1)} %copy-done.9, bf16[896,1024]{1,0:T(8,128)(2,1)S(1)} %copy-done.7), kind=kOutput, calls=%fused_computation.5 | convolution fusion | flops 3772776448 | bytes 11534336 | tf_op jit(solution)/shard_map/dot_general | solution.py:278
  173.0 0.0 reduce-scatter.5.cloned.1.call-update
  173.0 0.9 copy-done.13
  173.9 0.7 copy.23
  174.6 5.1 %all-to-all-start = ((bf16[16,8,1024]{2,0,1:T(8,128)(2,1)}), bf16[16,8,1024]{2,0,1:T(8,128)(2,1)S(1)}, u32[]{:S(2)}, u32[]{:S(2)}) async-start(bf16[16,8,1024]{2,0,1:T(8,128)(2,1)} %bitcast.64), calls=%async_computation.2 | async-start | bytes 524288 | tf_op jit(solution)/shard_map/all_to_all | solution.py:285
  179.8 0.1 select_reduce_fusion
  179.9 0.0 reduce-scatter.3.cloned.1.call-done
  179.9 11.7 %shard_map.80 = f32[64,1024]{1,0:T(8,128)} custom-call(f32[2,64,1024]{2,1,0:T(8,128)} %bitcast.85), custom_call_target="tpu_custom_call" | custom-call | tf_op jit(solution)/shard_map/pallas_call | solution.py:157
  191.6 39.0 %reduce-scatter.5.cloned.1.call-done = f32[128,1024]{1,0:T(8,128)} async-done(((f32[1024,1024]{1,0:T(8,128)}), f32[128,1024]{1,0:T(8,128)}) %reduce-scatter.5.cloned.1.call-update) | async-done | bytes 524304 | tf_op jit(solution)/shard_map/reduce_scatter | solution.py:279
  230.7 9.1 %shard_map.83 = f32[64,1024]{1,0:T(8,128)} custom-call(f32[2,64,1024]{2,1,0:T(8,128)} %bitcast.87), custom_call_target="tpu_custom_call" | custom-call | tf_op jit(solution)/shard_map/pallas_call | solution.py:157
  239.7 1.1 bitcast_add_fusion.1
  240.8 1.1 bitcast_add_fusion
  241.9 0.0 all-to-all-done
  241.9 1.0 fusion.17
  242.9 8.2 %shard_map.84 = bf16[2,128,1024]{2,1,0:T(8,128)(2,1)} custom-call(bf16[1,128,1024]{2,1,0:T(8,128)(2,1)} %bitcast.81), custom_call_target="tpu_custom_call" | custom-call | tf_op jit(solution)/shard_map/pallas_call | solution.py:65
  251.0 1.7 constant_dynamic-update-slice_fusion
  252.7 56.0 %shard_map.85 = (bf16[8,256,1024]{2,1,0:T(8,128)(2,1)}, bf16[8,256,1024]{2,1,0:T(8,128)(2,1)}) custom-call(bf16[256,1024]{1,0:T(8,128)(2,1)} %bitcast.77), custom_call_target="tpu_custom_call" | custom-call | tf_op jit(solution)/shard_map/pallas_call | solution.py:236
  308.7 2.9 fusion.25
  311.6 0.4 copy-done
  312.0 2.1 fusion.10
  314.2 2.1 fusion.8
  316.3 0.2 copy-done.5
  316.5 0.0 copy-start.11
  316.5 0.7 fusion.24
  317.3 0.8 copy-done.11
  318.0 2.1 fusion.26
  320.2 4.5 %add_add_fusion = f32[896,1024]{1,0:T(8,128)} fusion(f32[896,1024]{1,0:T(8,128)S(1)} %fusion.8, f32[896,1024]{1,0:T(8,128)S(1)} %fusion.26, f32[896,1024]{1,0:T(8,128)S(1)} %fusion.10, bf16[1024,896]{1,0:T(8,128)(2,1)S(1)} %dynamic-slice_bitcast_fusion, bf16[1024,1024]{1,0:T(8,128)(2,1)S(1)} %bitcast.76), kind=kOutput, calls=%fused_computation.9 | convolution fusion | flops 1881800704 | bytes 18612224 | tf_op jit(solution)/shard_map/dot_general | solution.py:305
  (27 shorter events, 0.1 us)
Async XLA Ops:
  7.2 172.8 %reduce-scatter.3.cloned.1.call-start = ((), (), s32[]{:S(2)}) async-start(), calls=%async_computation.3 | async-start | bytes 4718592 | tf_op jit(solution)/shard_map/reduce_scatter | solution.py:279
  9.4 69.4 %copy-start.2 = (bf16[2,2,2,1,64,896]{5,4,3,0,1,2:T(8,128)(2,1)S(1)}, bf16[2,2,2,1,64,896]{5,4,3,0,1,2:T(8,128)(2,1)}, u32[]{:S(2)}) copy-start(bf16[2,2,2,1,64,896]{5,4,3,0,1,2:T(8,128)(2,1)} %copy.22) | copy-start | bytes 2752516
  79.6 8.1 %copy-start.6 = (bf16[896,1024]{1,0:T(8,128)(2,1)S(1)}, bf16[896,1024]{1,0:T(8,128)(2,1)}, u32[]{:S(2)}) copy-start(bf16[896,1024]{1,0:T(8,128)(2,1)} %x_ref.1) | copy-start | bytes 5505028
  84.7 3.1 copy-start.8
  84.7 3.1 copy-start.12
  86.5 1.2 copy-start.10
  93.7 63.3 %copy-start.3 = (bf16[2,2,2,1,64,896]{5,4,3,0,1,2:T(8,128)(2,1)S(1)}, bf16[2,2,2,1,64,896]{5,4,3,0,1,2:T(8,128)(2,1)}, u32[]{:S(2)}) copy-start(bf16[2,2,2,1,64,896]{5,4,3,0,1,2:T(8,128)(2,1)} %copy.22) | copy-start | bytes 2752516
  93.7 137.0 %reduce-scatter.5.cloned.1.call-start = ((), (), s32[]{:S(2)}) async-start(), calls=%async_computation.4 | async-start | bytes 4718592 | tf_op jit(solution)/shard_map/reduce_scatter | solution.py:279
  162.9 2.1 copy-start.7
  162.9 2.6 copy-start.9
  173.0 0.9 copy-start.13
  173.0 6.8 %copy-start.15 = (bf16[1024]{0:T(1024)(128)(2,1)S(1)}, bf16[1024]{0:T(1024)(128)(2,1)}, u32[]{:S(2)}) copy-start(bf16[1024]{0:T(1024)(128)(2,1)} %param.10) | copy-start | bytes 6148
  173.0 6.8 %copy-start.16 = (s32[16]{0:T(128)S(1)}, s32[16]{0:T(128)}, u32[]{:S(2)}) copy-start(s32[16]{0:T(128)} %param.11) | copy-start | bytes 196
  173.0 68.9 %copy-start.14 = (bf16[128,1024]{1,0:T(8,128)(2,1)S(1)}, bf16[128,1024]{1,0:T(8,128)(2,1)}, u32[]{:S(2)}) copy-start(bf16[128,1024]{1,0:T(8,128)(2,1)} %param.6) | copy-start | bytes 786436
  174.6 67.2 %all-to-all-start = ((bf16[16,8,1024]{2,0,1:T(8,128)(2,1)}), bf16[16,8,1024]{2,0,1:T(8,128)(2,1)S(1)}, u32[]{:S(2)}, u32[]{:S(2)}) async-start(bf16[16,8,1024]{2,0,1:T(8,128)(2,1)} %bitcast.64), calls=%async_computation.2 | async-start | bytes 524288 | tf_op jit(solution)/shard_map/all_to_all | solution.py:285
  308.7 3.3 copy-start
  312.0 2.1 copy-start.1
  314.1 2.2 copy-start.4
  314.1 2.3 copy-start.5
  316.5 1.5 copy-start.11
Sparse Core Ops, SparseCore 0:
  93.8 57.5 reduce-scatter.2
  173.1 57.5 reduce-scatter.4

commit v18 on v17

--- a/solution.py
+++ b/solution.py
@@ -164,8 +164,9 @@
     )(x)
 
 
-def ring_gather_kernel(axis, n, x_ref, out_ref, pair_ref, send_sem, recv_sem, pair_send, pair_recv):
+def ring_gather_kernel(axis, n, x_ref, both_ref, send_sem, recv_sem, pair_send, pair_recv):
     me = lax.axis_index(axis)
+    out_ref = both_ref.at[lax.axis_index("core")]
     right, left = lax.rem(me + 1, n), lax.rem(me + n - 1, n)
     partner = device_on("core", 1 - lax.axis_index("core"))
 
@@ -188,7 +189,7 @@
     def to_partner(src, slot):
         return pltpu.make_async_remote_copy(
             src_ref=src,
-            dst_ref=pair_ref.at[slot],
+            dst_ref=out_ref.at[slot],
             send_sem=pair_send.at[slot],
             recv_sem=pair_recv.at[slot],
             device_id=partner,
@@ -227,20 +228,25 @@
         copies.append(forward)
     for copy in copies:
         copy.wait_send()
+    theirs = both_ref.at[1 - lax.axis_index("core")]
     for slot in range(n):
-        to_partner(x_ref, slot).wait_recv()
+        pltpu.make_async_remote_copy(
+            src_ref=x_ref,
+            dst_ref=theirs.at[slot],
+            send_sem=pair_send.at[slot],
+            recv_sem=pair_recv.at[slot],
+            device_id=partner,
+            device_id_type=MESH,
+        ).wait_recv()
 
 
 def ring_gather(x, axis, collective_id):
     n = lax.axis_size(axis)
-    received, from_partner = pl.pallas_call(
+    received = pl.pallas_call(
         functools.partial(ring_gather_kernel, axis, n),
-        out_shape=(
-            jax.ShapeDtypeStruct((n,) + x.shape, x.dtype),
-            jax.ShapeDtypeStruct((n,) + x.shape, x.dtype),
-        ),
+        out_shape=jax.ShapeDtypeStruct((2, n) + x.shape, x.dtype),
         in_specs=[pl.BlockSpec(memory_space=pl.ANY)],
-        out_specs=(pl.BlockSpec(memory_space=pl.ANY), pl.BlockSpec(memory_space=pl.ANY)),
+        out_specs=pl.BlockSpec(memory_space=pl.ANY),
         scratch_shapes=[
             pltpu.SemaphoreType.DMA((2, n // 2)),
             pltpu.SemaphoreType.DMA((n,)),
@@ -249,9 +255,9 @@
         ],
         compiler_params=pltpu.CompilerParams(collective_id=collective_id, has_side_effects=True),
     )(x)
-    whole = lax.dynamic_update_index_in_dim(received, x, lax.axis_index(axis), 0)
-    rows = (n * x.shape[0],) + x.shape[1:]
-    return whole.reshape(rows), from_partner.reshape(rows)
+    at = (lax.axis_index("core"), lax.axis_index(axis), 0, 0)
+    whole = lax.dynamic_update_slice(received, x[None, None], at)
+    return whole.reshape((2, n * x.shape[0]) + x.shape[1:])
 
 
 def per_device(resid_in, hidden, w_down, frozen, steer, forget_flags):
@@ -296,19 +302,17 @@
         jnp.bfloat16
     )
     gathered = gather_along(slopes, "yh", 6 + n_parts)
-    gathered, partner_slopes = ring_gather(gathered, "z", 10)
-    contract = (((0,), (0,)), ((), ()))
+    both = ring_gather(gathered, "z", 10).reshape(n_c, n_z * n_yh, n_parts, sub, d_cols)
+    contract = (((0, 1), (0, 1)), ((), ()))
     grad_down = None
     for part in range(n_parts):
-        for rows, got in ((me_c, gathered), (1 - me_c, partner_slopes)):
-            s_part = got.reshape(n_z * n_yh, n_parts, sub, d_cols)[:, part].reshape(-1, d_cols)
-            term = lax.dot_general(
-                lax.dynamic_index_in_dim(hp_parts[part], rows, keepdims=False),
-                s_part,
-                contract,
-                preferred_element_type=jnp.float32,
-            )
-            grad_down = term if grad_down is None else grad_down + term
+        term = lax.dot_general(
+            hp_parts[part],
+            both[:, :, part].reshape(n_c, -1, d_cols),
+            contract,
+            preferred_element_type=jnp.float32,
+        )
+        grad_down = term if grad_down is None else grad_down + term
     return (updated, grad_down)
 
 

time: 333 us -> 330 us (level)
    dot_general x4 -> x2, matrix products: 10.9 us -> 10.1 us  [per_device(): lax.dot_general(hp_parts[part], both[:, :, part].reshape(n_c, -1, d_cols)...]
where the time goes in v18:
time: 330 us; the launch traced here: 329 us
  Pallas kernels  228 us (69%)
  waiting for transfers between devices  39.1 us (12%)
  matrix products  22 us (7%)
  local copies, waits for them, and re-layouts  17.7 us (5%)
  between operations  14.3 us (4%)
  starting transfers between devices  5.22 us (2%)
    pallas_call x2, Pallas kernels, gather_part(): pl.pallas_call(functools.partial(placed_gather_kernel, n, n_zhi, part), o...  128 us
    pallas_call x1, Pallas kernels, ring_gather(): pl.pallas_call(functools.partial(ring_gather_kernel, axis, n), out_shape=...  56 us
    reduce_scatter x2, waiting for transfers between devices, per_device(): reduced_z = lax.psum_scatter(reduced, 'z', scatter_dimension=0, tiled=True)  39.1 us
    pallas_call x5, Pallas kernels, swap_with_partner(): pl.pallas_call(functools.partial(swap_kernel, axis, halves), out_shape=ja...  35.2 us
    dot_general x2, matrix products, per_device(): reduced = jnp.dot(pair_rows, pair_w, preferred_element_type=jnp.float32)  11.8 us
    dot_general x2, matrix products, per_device(): lax.dot_general(hp_parts[part], both[:, :, part].reshape(n_c, -1, d_cols)...  10.1 us
    pallas_call x1, Pallas kernels, gather_along(): pl.pallas_call(functools.partial(gather_kernel, axis, n, 0), out_shape=ja...  8.15 us
  transfers between devices with their start and end apart: 3, of which 1 were waited for; matrix products, arithmetic and copies ran while one was open for 4% of the time, Pallas kernels for 27%

profile of v18, /device:TPU:29, one launch (start us, length us, event | category | flops | bytes accessed | tf_op | source)
XLA Modules:
  0.0 329.0 jit_solution(11312698888367085885)
XLA Ops:
  7.2 0.0 reduce-scatter.3.cloned.1.call-start
  7.2 2.2 copy.30
  9.4 4.4 %shard_map.79 = bf16[896,1024]{1,0:T(8,128)(2,1)} custom-call(bf16[896,1024]{1,0:T(8,128)(2,1)} %x_ref.1), custom_call_target="tpu_custom_call" | custom-call | tf_op jit(solution)/shard_map/pallas_call | solution.py:157
  13.9 64.9 %shard_map.77 = bf16[2,8,2,64,896]{4,3,2,1,0:T(8,128)(2,1)} custom-call(bf16[2,2,2,1,64,896]{5,4,3,2,1,0:T(8,128)(2,1)} %bitcast.64), custom_call_target="tpu_custom_call" | custom-call | bytes 7340032 | tf_op jit(solution)/shard_map/pallas_call | solution.py:120
  78.8 0.0 copy-done.2
  78.8 0.8 fusion.12
  79.6 5.0 %shard_map.78 = bf16[1024,896]{1,0:T(8,128)(2,1)} custom-call(bf16[2,1024,896]{2,1,0:T(8,128)(2,1)} %bitcast.58), custom_call_target="tpu_custom_call" | custom-call | tf_op jit(solution)/shard_map/pallas_call | solution.py:157
  84.6 0.0 copy-start.6
  84.7 0.0 copy-start.8
  84.7 1.8 dynamic-slice_bitcast_fusion.1
  86.5 0.0 copy-done.5
  86.5 0.2 copy-done.6
  86.7 0.6 copy-done.8
  87.2 5.9 %fusion = f32[1024,1024]{1,0:T(8,128)} fusion(bf16[1024,896]{1,0:T(8,128)(2,1)S(1)} %copy-done.8, bf16[1024,896]{1,0:T(8,128)(2,1)S(1)} %dynamic-slice_bitcast_fusion.1, bf16[896,1024]{1,0:T(8,128)(2,1)S(1)} %copy-done.6, bf16[896,1024]{1,0:T(8,128)(2,1)S(1)} %copy-done.5), kind=kOutput, calls=%fused_computation | convolution fusion | flops 3772776448 | bytes 11534336 | tf_op jit(solution)/shard_map/dot_general | solution.py:284
  93.2 0.0 reduce-scatter.3.cloned.1.call-update
  93.2 0.0 reduce-scatter.5.cloned.1.call-start
  93.2 63.3 %shard_map.81 = bf16[2,8,2,64,896]{4,3,2,1,0:T(8,128)(2,1)} custom-call(bf16[2,2,2,1,64,896]{5,4,3,2,1,0:T(8,128)(2,1)} %bitcast.65), custom_call_target="tpu_custom_call" | custom-call | bytes 7340032 | tf_op jit(solution)/shard_map/pallas_call | solution.py:120
  156.5 0.0 copy-done.3
  156.5 0.9 bitcast_dynamic-update-slice_fusion
  157.4 5.0 %shard_map.82 = bf16[1024,896]{1,0:T(8,128)(2,1)} custom-call(bf16[2,1024,896]{2,1,0:T(8,128)(2,1)} %bitcast.61), custom_call_target="tpu_custom_call" | custom-call | tf_op jit(solution)/shard_map/pallas_call | solution.py:157
  162.4 0.0 copy-start.7
  162.4 0.0 copy-start.9
  162.4 1.8 dynamic-slice_bitcast_fusion
  164.2 0.2 copy-done.7
  164.5 0.6 copy-done.9
  165.0 5.9 %fusion.4 = f32[1024,1024]{1,0:T(8,128)} fusion(bf16[1024,896]{1,0:T(8,128)(2,1)S(1)} %copy-done.9, bf16[1024,896]{1,0:T(8,128)(2,1)S(1)} %dynamic-slice_bitcast_fusion, bf16[896,1024]{1,0:T(8,128)(2,1)S(1)} %copy-done.7, bf16[896,1024]{1,0:T(8,128)(2,1)S(1)} %copy-done.5), kind=kOutput, calls=%fused_computation.5 | convolution fusion | flops 3772776448 | bytes 11534336 | tf_op jit(solution)/shard_map/dot_general | solution.py:284
  171.0 0.0 reduce-scatter.5.cloned.1.call-update
  171.0 0.9 copy-done.10
  171.9 0.7 copy.31
  172.6 5.1 %all-to-all-start = ((bf16[16,8,1024]{2,0,1:T(8,128)(2,1)}), bf16[16,8,1024]{2,0,1:T(8,128)(2,1)S(1)}, u32[]{:S(2)}, u32[]{:S(2)}) async-start(bf16[16,8,1024]{2,0,1:T(8,128)(2,1)} %bitcast.56), calls=%async_computation.2 | async-start | bytes 524288 | tf_op jit(solution)/shard_map/all_to_all | solution.py:291
  177.8 0.0 copy-done.13
  177.8 0.1 select_reduce_fusion
  177.9 0.0 reduce-scatter.3.cloned.1.call-done
  177.9 11.7 %shard_map.80 = f32[64,1024]{1,0:T(8,128)} custom-call(f32[2,64,1024]{2,1,0:T(8,128)} %bitcast.73), custom_call_target="tpu_custom_call" | custom-call | tf_op jit(solution)/shard_map/pallas_call | solution.py:157
  189.6 39.0 %reduce-scatter.5.cloned.1.call-done = f32[128,1024]{1,0:T(8,128)} async-done(((f32[1024,1024]{1,0:T(8,128)}), f32[128,1024]{1,0:T(8,128)}) %reduce-scatter.5.cloned.1.call-update) | async-done | bytes 524304 | tf_op jit(solution)/shard_map/reduce_scatter | solution.py:285
  228.7 9.1 %shard_map.83 = f32[64,1024]{1,0:T(8,128)} custom-call(f32[2,64,1024]{2,1,0:T(8,128)} %bitcast.75), custom_call_target="tpu_custom_call" | custom-call | tf_op jit(solution)/shard_map/pallas_call | solution.py:157
  237.7 1.1 bitcast_add_fusion.2
  238.8 1.1 bitcast_add_fusion.1
  239.9 0.0 all-to-all-done
  239.9 1.0 fusion.11
  240.9 8.2 %shard_map.84 = bf16[2,128,1024]{2,1,0:T(8,128)(2,1)} custom-call(bf16[1,128,1024]{2,1,0:T(8,128)(2,1)} %bitcast.72), custom_call_target="tpu_custom_call" | custom-call | tf_op jit(solution)/shard_map/pallas_call | solution.py:65
  249.0 1.7 constant_dynamic-update-slice_fusion
  250.7 56.0 %shard_map.85 = bf16[2,8,256,1024]{3,2,1,0:T(8,128)(2,1)} custom-call(bf16[256,1024]{1,0:T(8,128)(2,1)} %bitcast.68), custom_call_target="tpu_custom_call" | custom-call | tf_op jit(solution)/shard_map/pallas_call | solution.py:245
  306.7 0.8 constant_dynamic-update-slice_fusion.1
  307.5 4.2 %fusion.16 = (bf16[2,16,1,64,1024]{4,3,2,1,0:T(8,128)(2,1)S(1)}, bf16[2,16,1,64,1024]{4,3,2,1,0:T(8,128)(2,1)S(1)}) fusion(bf16[2,16,2,64,1024]{4,3,2,1,0:T(8,128)(2,1)} %bitcast.57), kind=kLoop, calls=%fused_computation.38 | loop fusion | bytes 16777216 | tf_op jit(solution)/shard_map/slice | solution.py:311
  311.7 0.3 copy-done
  312.1 4.0 %fusion.17 = f32[896,1024,1]{1,0,2:T(8,128)S(1)} fusion(bf16[2,1024,896]{2,1,0:T(8,128)(2,1)S(1)} %bitcast.60, bf16[2,1024,1024]{2,1,0:T(8,128)(2,1)S(1)} %bitcast.71), kind=kOutput, calls=%fused_computation.39 | convolution fusion | flops 3758096384 | bytes 11534336 | tf_op jit(solution)/shard_map/dot_general | solution.py:309
  316.1 6.1 %bitcast_add_fusion = f32[896,1024]{1,0:T(8,128)} fusion(f32[896,1024,1]{1,0,2:T(8,128)S(1)} %fusion.17, bf16[2,1024,896]{2,1,0:T(8,128)(2,1)S(1)} %bitcast.63, bf16[2,1024,1024]{2,1,0:T(8,128)(2,1)S(1)} %bitcast.70), kind=kOutput, calls=%fused_computation.9 | convolution fusion | flops 3759013888 | bytes 15204352 | tf_op jit(solution)/shard_map/dot_general | solution.py:309
  (18 shorter events, 0.0 us)
Async XLA Ops:
  7.2 170.8 %reduce-scatter.3.cloned.1.call-start = ((), (), s32[]{:S(2)}) async-start(), calls=%async_computation.3 | async-start | bytes 4718592 | tf_op jit(solution)/shard_map/reduce_scatter | solution.py:285
  9.4 69.4 %copy-start.2 = (bf16[2,2,2,1,64,896]{5,4,3,0,1,2:T(8,128)(2,1)S(1)}, bf16[2,2,2,1,64,896]{5,4,3,0,1,2:T(8,128)(2,1)}, u32[]{:S(2)}) copy-start(bf16[2,2,2,1,64,896]{5,4,3,0,1,2:T(8,128)(2,1)} %copy.30) | copy-start | bytes 2752516
  79.6 6.9 %copy-start.5 = (bf16[896,1024]{1,0:T(8,128)(2,1)S(1)}, bf16[896,1024]{1,0:T(8,128)(2,1)}, u32[]{:S(2)}) copy-start(bf16[896,1024]{1,0:T(8,128)(2,1)} %x_ref.1) | copy-start | bytes 5505028
  84.6 2.1 copy-start.6
  84.7 2.6 copy-start.8
  93.2 63.3 %copy-start.3 = (bf16[2,2,2,1,64,896]{5,4,3,0,1,2:T(8,128)(2,1)S(1)}, bf16[2,2,2,1,64,896]{5,4,3,0,1,2:T(8,128)(2,1)}, u32[]{:S(2)}) copy-start(bf16[2,2,2,1,64,896]{5,4,3,0,1,2:T(8,128)(2,1)} %copy.30) | copy-start | bytes 2752516
  93.2 135.5 %reduce-scatter.5.cloned.1.call-start = ((), (), s32[]{:S(2)}) async-start(), calls=%async_computation.4 | async-start | bytes 4718592 | tf_op jit(solution)/shard_map/reduce_scatter | solution.py:285
  162.4 2.1 copy-start.7
  162.4 2.6 copy-start.9
  170.9 0.9 copy-start.10
  171.0 6.8 %copy-start.12 = (bf16[1024]{0:T(1024)(128)(2,1)S(1)}, bf16[1024]{0:T(1024)(128)(2,1)}, u32[]{:S(2)}) copy-start(bf16[1024]{0:T(1024)(128)(2,1)} %param.10) | copy-start | bytes 6148
  171.0 6.8 %copy-start.13 = (s32[16]{0:T(128)S(1)}, s32[16]{0:T(128)}, u32[]{:S(2)}) copy-start(s32[16]{0:T(128)} %param.11) | copy-start | bytes 196
  171.0 68.9 %copy-start.11 = (bf16[128,1024]{1,0:T(8,128)(2,1)S(1)}, bf16[128,1024]{1,0:T(8,128)(2,1)}, u32[]{:S(2)}) copy-start(bf16[128,1024]{1,0:T(8,128)(2,1)} %param.6) | copy-start | bytes 786436
  172.6 67.2 %all-to-all-start = ((bf16[16,8,1024]{2,0,1:T(8,128)(2,1)}), bf16[16,8,1024]{2,0,1:T(8,128)(2,1)S(1)}, u32[]{:S(2)}, u32[]{:S(2)}) async-start(bf16[16,8,1024]{2,0,1:T(8,128)(2,1)} %bitcast.56), calls=%async_computation.2 | async-start | bytes 524288 | tf_op jit(solution)/shard_map/all_to_all | solution.py:291
  250.7 56.0 %copy-start.4 = (bf16[2,128,1024]{2,1,0:T(8,128)(2,1)S(1)}, bf16[2,128,1024]{2,1,0:T(8,128)(2,1)}, u32[]{:S(2)}) copy-start(bf16[2,128,1024]{2,1,0:T(8,128)(2,1)} %constant_dynamic-update-slice_fusion) | copy-start | bytes 1572868
  307.5 4.5 %copy-start = (bf16[2,8,2,64,896]{4,3,2,1,0:T(8,128)(2,1)S(1)}, bf16[2,8,2,64,896]{4,3,2,1,0:T(8,128)(2,1)}, u32[]{:S(2)}) copy-start(bf16[2,8,2,64,896]{4,3,2,1,0:T(8,128)(2,1)} %fusion.12) | copy-start | bytes 11010052
  312.1 4.1 %copy-start.1 = (bf16[2,8,2,64,896]{4,3,2,1,0:T(8,128)(2,1)S(1)}, bf16[2,8,2,64,896]{4,3,2,1,0:T(8,128)(2,1)}, u32[]{:S(2)}) copy-start(bf16[2,8,2,64,896]{4,3,2,1,0:T(8,128)(2,1)} %bitcast_dynamic-update-slice_fusion) | copy-start | bytes 11010052
Sparse Core Ops, SparseCore 0:
  93.3 57.5 reduce-scatter.2
  171.1 57.5 reduce-scatter.4

commit v19 on v18

--- a/solution.py
+++ b/solution.py
@@ -76,9 +76,10 @@
 
 def placed_gather_kernel(n, n_zhi, part, x_ref, out_ref, send_sem, recv_sem):
     me = lax.axis_index("shard")
-
-    def where(j):
-        return out_ref.at[:, pl.ds(2 * lax.rem(j, n_zhi), 2), pl.ds(j // n_zhi, 1)]
+    n_c = out_ref.shape[0]
+
+    def where(j, c):
+        return out_ref.at[c, pl.ds(2 * lax.rem(j, n_zhi), 2), pl.ds(j // n_zhi, 1)]
 
     barrier = pltpu.get_barrier_semaphore()
     for off in range(1, n):
@@ -86,51 +87,47 @@
         pl.semaphore_signal(barrier, inc=1, device_id=device_on("shard", peer), device_id_type=MESH)
     pl.semaphore_wait(barrier, n - 1)
 
+    def transfer(off, c, dest, slot):
+        return pltpu.make_async_remote_copy(
+            src_ref=x_ref.at[:, c, part],
+            dst_ref=where(slot, c),
+            send_sem=send_sem.at[off - 1, c],
+            recv_sem=recv_sem.at[slot, c],
+            device_id=device_on("shard", dest),
+            device_id_type=MESH,
+        )
+
     copies = []
     for off in range(1, n):
-        peer = lax.rem(me + off, n)
-        copy = pltpu.make_async_remote_copy(
-            src_ref=x_ref.at[part],
-            dst_ref=where(me),
-            send_sem=send_sem.at[off - 1],
-            recv_sem=recv_sem.at[me],
-            device_id=device_on("shard", peer),
-            device_id_type=MESH,
-        )
-        copy.start()
-        copies.append(copy)
+        for c in range(n_c):
+            copy = transfer(off, c, lax.rem(me + off, n), me)
+            copy.start()
+            copies.append(copy)
     for copy in copies:
         copy.wait_send()
     for off in range(1, n):
         src = lax.rem(me + n - off, n)
-        arrival = pltpu.make_async_remote_copy(
-            src_ref=x_ref.at[part],
-            dst_ref=where(src),
-            send_sem=send_sem.at[off - 1],
-            recv_sem=recv_sem.at[src],
-            device_id=device_on("shard", src),
-            device_id_type=MESH,
-        )
-        arrival.wait_recv()
-
-
-def gather_part(xt, part, collective_id, out_dims):
+        for c in range(n_c):
+            transfer(off, c, src, src).wait_recv()
+
+
+def gather_part(x6, part, collective_id, out_dims):
     n = lax.axis_size("shard")
-    n_zhi = out_dims[1] // 2
+    n_c, n_zhi = out_dims[0], out_dims[1] // 2
     received = pl.pallas_call(
         functools.partial(placed_gather_kernel, n, n_zhi, part),
-        out_shape=jax.ShapeDtypeStruct(out_dims, xt.dtype),
+        out_shape=jax.ShapeDtypeStruct(out_dims, x6.dtype),
         in_specs=[pl.BlockSpec(memory_space=pl.ANY)],
         out_specs=pl.BlockSpec(memory_space=pl.ANY),
-        scratch_shapes=[pltpu.SemaphoreType.DMA((n - 1,)), pltpu.SemaphoreType.DMA((n,))],
+        scratch_shapes=[pltpu.SemaphoreType.DMA((n - 1, n_c)), pltpu.SemaphoreType.DMA((n, n_c))],
         compiler_params=pltpu.CompilerParams(collective_id=collective_id, has_side_effects=True),
         cost_estimate=pl.CostEstimate(
-            flops=0, bytes_accessed=2 * n * xt[part].nbytes, transcendentals=0
+            flops=0, bytes_accessed=2 * n * x6[:, :, part].nbytes, transcendentals=0
         ),
-    )(xt)
+    )(x6)
     me = lax.axis_index("shard")
     at = (0, 2 * lax.rem(me, n_zhi), me // n_zhi, 0, 0)
-    return lax.dynamic_update_slice(received, xt[part], at)
+    return lax.dynamic_update_slice(received, x6[:, :, part].swapaxes(0, 1), at)
 
 
 def swap_kernel(axis, halves, x_ref, out_ref, send_sem, recv_sem):
@@ -270,7 +267,7 @@
     total_tokens = own_tokens * lax.axis_size("shard")
     me_c = lax.axis_index("core")
     me_yh = lax.axis_index("yh")
-    xt = hidden.reshape(blocks // n_c, n_c, n_parts, 1, sub, ff_rows).transpose(2, 1, 0, 3, 4, 5)
+    xt = hidden.reshape(blocks // n_c, n_c, n_parts, 1, sub, ff_rows)
     hp_parts, mlp_parts = [], []
     pair_w = jnp.concatenate([w_down, swap_with_partner(w_down, 9, False)], axis=0)
     for part in range(n_parts):

time: 330 us -> 329 us (level)
  no operation moved by 1% of the time
where the time goes in v19:
time: 329 us; the launch traced here: 327 us
  Pallas kernels  228 us (69%)
  waiting for transfers between devices  39.1 us (12%)
  matrix products  22 us (7%)
  local copies, waits for them, and re-layouts  15.5 us (5%)
  between operations  14.3 us (4%)
  starting transfers between devices  5.22 us (2%)
    pallas_call x2, Pallas kernels, gather_part(): pl.pallas_call(functools.partial(placed_gather_kernel, n, n_zhi, part), o...  128 us
    pallas_call x1, Pallas kernels, ring_gather(): pl.pallas_call(functools.partial(ring_gather_kernel, axis, n), out_shape=...  56 us
    reduce_scatter x2, waiting for transfers between devices, per_device(): reduced_z = lax.psum_scatter(reduced, 'z', scatter_dimension=0, tiled=True)  39.1 us
    pallas_call x5, Pallas kernels, swap_with_partner(): pl.pallas_call(functools.partial(swap_kernel, axis, halves), out_shape=ja...  35.4 us
    dot_general x2, matrix products, per_device(): reduced = jnp.dot(pair_rows, pair_w, preferred_element_type=jnp.float32)  11.8 us
    dot_general x2, matrix products, per_device(): lax.dot_general(hp_parts[part], both[:, :, part].reshape(n_c, -1, d_cols)...  10.1 us
    pallas_call x1, Pallas kernels, gather_along(): pl.pallas_call(functools.partial(gather_kernel, axis, n, 0), out_shape=ja...  8.15 us
  transfers between devices with their start and end apart: 3, of which 1 were waited for; matrix products, arithmetic and copies ran while one was open for 4% of the time, Pallas kernels for 27%

profile of v19, /device:TPU:29, one launch (start us, length us, event | category | flops | bytes accessed | tf_op | source)
XLA Modules:
  0.0 327.3 jit_solution(15898405469006404154)
XLA Ops:
  7.2 0.0 reduce-scatter.3.cloned.1.call-start
  7.2 0.0 copy-start.2
  7.2 4.6 %shard_map.79 = bf16[896,1024]{1,0:T(8,128)(2,1)} custom-call(bf16[896,1024]{1,0:T(8,128)(2,1)} %x_ref.1), custom_call_target="tpu_custom_call" | custom-call | tf_op jit(solution)/shard_map/pallas_call | solution.py:154
  11.9 65.0 %shard_map.77 = bf16[2,8,2,64,896]{4,3,2,1,0:T(8,128)(2,1)} custom-call(bf16[2,2,2,1,64,896]{5,4,3,2,1,0:T(8,128)(2,1)} %bitcast.61), custom_call_target="tpu_custom_call" | custom-call | bytes 7340032 | tf_op jit(solution)/shard_map/pallas_call | solution.py:117
  76.9 0.0 copy-done.2
  76.9 0.8 copy_dynamic-update-slice_fusion.1
  77.7 5.0 %shard_map.78 = bf16[1024,896]{1,0:T(8,128)(2,1)} custom-call(bf16[2,1024,896]{2,1,0:T(8,128)(2,1)} %bitcast.55), custom_call_target="tpu_custom_call" | custom-call | tf_op jit(solution)/shard_map/pallas_call | solution.py:154
  82.8 0.0 copy-start.6
  82.8 0.0 copy-start.8
  82.8 1.8 dynamic-slice_bitcast_fusion.1
  84.6 0.0 copy-done.5
  84.6 0.2 copy-done.6
  84.8 0.6 copy-done.8
  85.4 5.9 %fusion = f32[1024,1024]{1,0:T(8,128)} fusion(bf16[1024,896]{1,0:T(8,128)(2,1)S(1)} %copy-done.8, bf16[1024,896]{1,0:T(8,128)(2,1)S(1)} %dynamic-slice_bitcast_fusion.1, bf16[896,1024]{1,0:T(8,128)(2,1)S(1)} %copy-done.6, bf16[896,1024]{1,0:T(8,128)(2,1)S(1)} %copy-done.5), kind=kOutput, calls=%fused_computation | convolution fusion | flops 3772776448 | bytes 11534336 | tf_op jit(solution)/shard_map/dot_general | solution.py:281
  91.3 0.0 reduce-scatter.3.cloned.1.call-update
  91.3 0.0 reduce-scatter.5.cloned.1.call-start
  91.4 63.4 %shard_map.81 = bf16[2,8,2,64,896]{4,3,2,1,0:T(8,128)(2,1)} custom-call(bf16[2,2,2,1,64,896]{5,4,3,2,1,0:T(8,128)(2,1)} %bitcast.62), custom_call_target="tpu_custom_call" | custom-call | bytes 7340032 | tf_op jit(solution)/shard_map/pallas_call | solution.py:117
  154.8 0.0 copy-done.3
  154.8 0.9 copy_dynamic-update-slice_fusion
  155.6 5.0 %shard_map.82 = bf16[1024,896]{1,0:T(8,128)(2,1)} custom-call(bf16[2,1024,896]{2,1,0:T(8,128)(2,1)} %bitcast.58), custom_call_target="tpu_custom_call" | custom-call | tf_op jit(solution)/shard_map/pallas_call | solution.py:154
  160.7 0.0 copy-start.7
  160.7 1.8 dynamic-slice_bitcast_fusion
  162.5 0.2 copy-done.7
  162.7 0.6 copy-done.9
  163.3 5.9 %fusion.4 = f32[1024,1024]{1,0:T(8,128)} fusion(bf16[1024,896]{1,0:T(8,128)(2,1)S(1)} %copy-done.9, bf16[1024,896]{1,0:T(8,128)(2,1)S(1)} %dynamic-slice_bitcast_fusion, bf16[896,1024]{1,0:T(8,128)(2,1)S(1)} %copy-done.7, bf16[896,1024]{1,0:T(8,128)(2,1)S(1)} %copy-done.5), kind=kOutput, calls=%fused_computation.5 | convolution fusion | flops 3772776448 | bytes 11534336 | tf_op jit(solution)/shard_map/dot_general | solution.py:281
  169.2 0.0 reduce-scatter.5.cloned.1.call-update
  169.2 0.9 copy-done.10
  170.2 0.7 copy.24
  170.9 5.1 %all-to-all-start = ((bf16[16,8,1024]{2,0,1:T(8,128)(2,1)}), bf16[16,8,1024]{2,0,1:T(8,128)(2,1)S(1)}, u32[]{:S(2)}, u32[]{:S(2)}) async-start(bf16[16,8,1024]{2,0,1:T(8,128)(2,1)} %bitcast.53), calls=%async_computation.2 | async-start | bytes 524288 | tf_op jit(solution)/shard_map/all_to_all | solution.py:288
  176.1 0.0 copy-done.13
  176.1 0.1 select_reduce_fusion
  176.2 0.0 reduce-scatter.3.cloned.1.call-done
  176.2 11.7 %shard_map.80 = f32[64,1024]{1,0:T(8,128)} custom-call(f32[2,64,1024]{2,1,0:T(8,128)} %bitcast.70), custom_call_target="tpu_custom_call" | custom-call | tf_op jit(solution)/shard_map/pallas_call | solution.py:154
  187.9 39.0 %reduce-scatter.5.cloned.1.call-done = f32[128,1024]{1,0:T(8,128)} async-done(((f32[1024,1024]{1,0:T(8,128)}), f32[128,1024]{1,0:T(8,128)}) %reduce-scatter.5.cloned.1.call-update) | async-done | bytes 524304 | tf_op jit(solution)/shard_map/reduce_scatter | solution.py:282
  226.9 9.1 %shard_map.83 = f32[64,1024]{1,0:T(8,128)} custom-call(f32[2,64,1024]{2,1,0:T(8,128)} %bitcast.72), custom_call_target="tpu_custom_call" | custom-call | tf_op jit(solution)/shard_map/pallas_call | solution.py:154
  236.0 1.1 bitcast_add_fusion.2
  237.1 1.1 bitcast_add_fusion.1
  238.1 0.0 all-to-all-done
  238.1 1.0 fusion.11
  239.1 8.2 %shard_map.84 = bf16[2,128,1024]{2,1,0:T(8,128)(2,1)} custom-call(bf16[1,128,1024]{2,1,0:T(8,128)(2,1)} %bitcast.69), custom_call_target="tpu_custom_call" | custom-call | tf_op jit(solution)/shard_map/pallas_call | solution.py:65
  247.3 1.7 constant_dynamic-update-slice_fusion
  249.0 56.0 %shard_map.85 = bf16[2,8,256,1024]{3,2,1,0:T(8,128)(2,1)} custom-call(bf16[256,1024]{1,0:T(8,128)(2,1)} %bitcast.65), custom_call_target="tpu_custom_call" | custom-call | tf_op jit(solution)/shard_map/pallas_call | solution.py:242
  305.0 0.8 constant_dynamic-update-slice_fusion.1
  305.8 4.2 %fusion.15 = (bf16[2,16,1,64,1024]{4,3,2,1,0:T(8,128)(2,1)S(1)}, bf16[2,16,1,64,1024]{4,3,2,1,0:T(8,128)(2,1)S(1)}) fusion(bf16[2,16,2,64,1024]{4,3,2,1,0:T(8,128)(2,1)} %bitcast.54), kind=kLoop, calls=%fused_computation.38 | loop fusion | bytes 16777216 | tf_op jit(solution)/shard_map/slice | solution.py:308
  310.0 0.3 copy-done
  310.3 4.0 %fusion.16 = f32[896,1024,1]{1,0,2:T(8,128)S(1)} fusion(bf16[2,1024,896]{2,1,0:T(8,128)(2,1)S(1)} %bitcast.57, bf16[2,1024,1024]{2,1,0:T(8,128)(2,1)S(1)} %bitcast.68), kind=kOutput, calls=%fused_computation.39 | convolution fusion | flops 3758096384 | bytes 11534336 | tf_op jit(solution)/shard_map/dot_general | solution.py:306
  314.4 0.0 copy-done.1
  314.4 6.1 %bitcast_add_fusion = f32[896,1024]{1,0:T(8,128)} fusion(f32[896,1024,1]{1,0,2:T(8,128)S(1)} %fusion.16, bf16[2,1024,896]{2,1,0:T(8,128)(2,1)S(1)} %bitcast.60, bf16[2,1024,1024]{2,1,0:T(8,128)(2,1)S(1)} %bitcast.67), kind=kOutput, calls=%fused_computation.9 | convolution fusion | flops 3759013888 | bytes 15204352 | tf_op jit(solution)/shard_map/dot_general | solution.py:306
  (17 shorter events, 0.0 us)
Async XLA Ops:
  7.2 169.0 %reduce-scatter.3.cloned.1.call-start = ((), (), s32[]{:S(2)}) async-start(), calls=%async_computation.3 | async-start | bytes 4718592 | tf_op jit(solution)/shard_map/reduce_scatter | solution.py:282
  7.2 69.7 %copy-start.2 = (bf16[512,896]{1,0:T(8,128)(2,1)S(1)}, bf16[512,896]{1,0:T(8,128)(2,1)}, u32[]{:S(2)}) copy-start(bf16[512,896]{1,0:T(8,128)(2,1)} %param.7) | copy-start | bytes 2752516
  77.7 6.9 %copy-start.5 = (bf16[896,1024]{1,0:T(8,128)(2,1)S(1)}, bf16[896,1024]{1,0:T(8,128)(2,1)}, u32[]{:S(2)}) copy-start(bf16[896,1024]{1,0:T(8,128)(2,1)} %x_ref.1) | copy-start | bytes 5505028
  82.8 2.1 copy-start.6
  82.8 2.6 copy-start.8
  91.3 63.5 %copy-start.3 = (bf16[512,896]{1,0:T(8,128)(2,1)S(1)}, bf16[512,896]{1,0:T(8,128)(2,1)}, u32[]{:S(2)}) copy-start(bf16[512,896]{1,0:T(8,128)(2,1)} %param.7) | copy-start | bytes 2752516
  91.3 135.6 %reduce-scatter.5.cloned.1.call-start = ((), (), s32[]{:S(2)}) async-start(), calls=%async_computation.4 | async-start | bytes 4718592 | tf_op jit(solution)/shard_map/reduce_scatter | solution.py:282
  160.7 2.1 copy-start.7
  160.7 2.6 copy-start.9
  169.2 0.9 copy-start.10
  169.2 6.8 %copy-start.12 = (bf16[1024]{0:T(1024)(128)(2,1)S(1)}, bf16[1024]{0:T(1024)(128)(2,1)}, u32[]{:S(2)}) copy-start(bf16[1024]{0:T(1024)(128)(2,1)} %param.10) | copy-start | bytes 6148
  169.2 6.8 %copy-start.13 = (s32[16]{0:T(128)S(1)}, s32[16]{0:T(128)}, u32[]{:S(2)}) copy-start(s32[16]{0:T(128)} %param.11) | copy-start | bytes 196
  169.2 68.9 %copy-start.11 = (bf16[128,1024]{1,0:T(8,128)(2,1)S(1)}, bf16[128,1024]{1,0:T(8,128)(2,1)}, u32[]{:S(2)}) copy-start(bf16[128,1024]{1,0:T(8,128)(2,1)} %param.6) | copy-start | bytes 786436
  170.9 67.2 %all-to-all-start = ((bf16[16,8,1024]{2,0,1:T(8,128)(2,1)}), bf16[16,8,1024]{2,0,1:T(8,128)(2,1)S(1)}, u32[]{:S(2)}, u32[]{:S(2)}) async-start(bf16[16,8,1024]{2,0,1:T(8,128)(2,1)} %bitcast.53), calls=%async_computation.2 | async-start | bytes 524288 | tf_op jit(solution)/shard_map/all_to_all | solution.py:288
  249.0 56.0 %copy-start.4 = (bf16[2,128,1024]{2,1,0:T(8,128)(2,1)S(1)}, bf16[2,128,1024]{2,1,0:T(8,128)(2,1)}, u32[]{:S(2)}) copy-start(bf16[2,128,1024]{2,1,0:T(8,128)(2,1)} %constant_dynamic-update-slice_fusion) | copy-start | bytes 1572868
  305.8 4.5 %copy-start = (bf16[2,8,2,64,896]{4,3,2,1,0:T(8,128)(2,1)S(1)}, bf16[2,8,2,64,896]{4,3,2,1,0:T(8,128)(2,1)}, u32[]{:S(2)}) copy-start(bf16[2,8,2,64,896]{4,3,2,1,0:T(8,128)(2,1)} %copy_dynamic-update-slice_fusion.1) | copy-start | bytes 11010052
  310.3 4.1 %copy-start.1 = (bf16[2,8,2,64,896]{4,3,2,1,0:T(8,128)(2,1)S(1)}, bf16[2,8,2,64,896]{4,3,2,1,0:T(8,128)(2,1)}, u32[]{:S(2)}) copy-start(bf16[2,8,2,64,896]{4,3,2,1,0:T(8,128)(2,1)} %copy_dynamic-update-slice_fusion) | copy-start | bytes 11010052
Sparse Core Ops, SparseCore 0:
  91.4 57.5 reduce-scatter.2
  169.4 57.5 reduce-scatter.4
